TPU v7x, 256 devices: a whole 4x4x8 slice. The times are simulated.
256 devices in a mesh: dp: 16 (over y, z_lo, core), own: 16 (over x, z_hi).
Axes of the slice: x: 4, y: 4, z: 8 (z_hi: 4, z_lo: 2; z = z_hi * 2 + z_lo), core: 2. Of those that a mesh axis runs over, the one named last changes fastest.
Arguments:
- grads: bfloat16 [16, 32, 768, 768], P('dp', 'own'), may hold values from -0.059814453 to 0.059814453
- owner: int32 [32], replicated, may hold values from 0 to 15, as said below
- weights: float32 [64, 768, 768], P('own', 'dp'), may hold values from -6 to 6
- stat_left: float32 [64, 768, 768], P('own', 'dp'), may hold values from -3 to 3
- stat_right: float32 [64, 768, 768], P('own', 'dp'), may hold values from -3 to 3
- adam_second: float32 [64, 768, 768], P('own', 'dp'), may hold values from 0.0002 to 1
- root_left: bfloat16 [64, 768, 768], P('own', 'dp'), may hold values from -0.21875 to 0.21875
- root_right: bfloat16 [64, 768, 768], P('own', 'dp'), may hold values from -0.21875 to 0.21875
Outputs:
- new_weights: bfloat16 [64, 768, 768], P('own')
- new_left: float32 [64, 768, 768], P('own', 'dp')
- new_right: float32 [64, 768, 768], P('own', 'dp')
- new_second: float32 [64, 768, 768], P('own', 'dp')
Inputs may be any that keep to these rules, and one draw needn't show every extreme that they name: The 2 blocks 2 * j to 2 * j + 1 have different owners, for every j; one owner holds exactly 4 blocks and none holds more.
All inputs are finite; a program needn't handle non-finite values.
Results may differ from a plain program's by a relative error of at most 0.0095.
Values may be sent and summed in bfloat16 or wider, within the bound.
No kernel may reach another device: no remote copies, remote signals or barrier semaphores. Data moves between devices by JAX's collectives and lax.ppermute only.
A program may use at most 64 MiB of HBM per device.

v0:
```python
import jax
import jax.numpy as jnp
from jax import lax
from jax.sharding import PartitionSpec as P


def slot_index(owner, capacity):
    count = owner.shape[0]
    same = owner[:, None] == owner[None, :]
    earlier = (
        jnp.arange(count, dtype=jnp.int32)[None, :] < jnp.arange(count, dtype=jnp.int32)[:, None]
    )
    rank = jnp.sum((same & earlier).astype(jnp.int32), axis=1)
    return owner * capacity + rank


def on_device(grads, owner, weights, stat_left, stat_right, adam_second, root_left, root_right):
    per_index = grads.shape[1]
    width = grads.shape[3]
    capacity = 2 * per_index
    replicas = lax.axis_size("dp")
    me = lax.axis_index("own")
    rep = lax.axis_index("dp")
    col_count = width // replicas
    summed = lax.psum_scatter(
        grads[0].astype(jnp.float32).astype(jnp.bfloat16), "dp", scatter_dimension=1, tiled=True
    )
    row_count = summed.shape[1]
    slot = slot_index(owner, capacity)
    targets = me * capacity + jnp.arange(capacity, dtype=jnp.int32)
    every = lax.all_gather(summed, "own", axis=0, tiled=True)
    pick = (slot[None, :] == targets[:, None]).astype(jnp.bfloat16)
    mine = jnp.dot(
        pick, every.reshape(every.shape[0], row_count * width), preferred_element_type=jnp.float32
    )
    mine = mine.astype(jnp.bfloat16).reshape(capacity, row_count, width)
    full = lax.all_gather(mine, "dp", axis=1, tiled=True)
    new_left = 0.5 * stat_left + 0.5 * jnp.einsum(
        "srd,sbd->srb", mine, full, preferred_element_type=jnp.float32
    )
    columns = lax.dynamic_slice_in_dim(full, rep * col_count, col_count, 2)
    new_right = 0.5 * stat_right + 0.5 * jnp.einsum(
        "sbc,sbd->scd", columns, full, preferred_element_type=jnp.float32
    )
    grad32 = mine.astype(jnp.float32)
    new_second = 0.9 * adam_second + 0.1 * grad32 * grad32
    adam_dir = grad32 / (jnp.sqrt(new_second) + 1e-08)
    half = jnp.einsum("srb,sbd->srd", root_left, full, preferred_element_type=jnp.float32).astype(
        jnp.bfloat16
    )
    precond = jnp.einsum(
        "src,scd->srd",
        half,
        lax.all_gather(root_right, "dp", axis=1, tiled=True),
        preferred_element_type=jnp.float32,
    )
    adam_sq = jnp.sum(adam_dir * adam_dir, axis=(1, 2))
    prec_sq = jnp.sum(precond * precond, axis=(1, 2))
    adam_total, prec_total = lax.psum((adam_sq, prec_sq), "dp")
    graft = jnp.sqrt(adam_total) / (jnp.sqrt(prec_total) + 1e-06)
    fresh_rows = (weights - graft[:, None, None] * precond).astype(jnp.bfloat16)
    new_weights = lax.all_gather(fresh_rows, "dp", axis=1, tiled=True)
    return (new_weights, new_left, new_right, new_second)


def solution(mesh):
    placed = (
        P("dp", "own", None, None),
        P(),
        P("own", "dp", None),
        P("own", "dp", None),
        P("own", "dp", None),
        P("own", "dp", None),
        P("own", "dp", None),
        P("own", "dp", None),
    )
    return jax.shard_map(
        on_device,
        mesh=mesh,
        in_specs=placed,
        out_specs=(
            P("own", None, None),
            P("own", "dp", None),
            P("own", "dp", None),
            P("own", "dp", None),
        ),
        check_vma=False,
    )
```

profile of v0, /device:TPU:1, one launch (start us, length us, event | category | flops | bytes accessed | tf_op | source)
XLA Modules:
  0.0 314.4 jit_solution(17411451454313605039)
XLA Ops:
  7.2 0.0 copy-start
  7.2 0.0 reduce-scatter.2.cloned.1.call-start
  7.2 0.7 reduce-scatter.2.cloned.1.call-update
  7.9 0.0 copy-start.3
  7.9 0.0 all-gather.5.cloned.1.call-start
  8.0 71.1 %reduce-scatter.2.cloned.1.call-done = bf16[2,48,768]{2,1,0:T(8,128)(2,1)} async-done(((bf16[2,768,768]{2,1,0:T(8,128)(2,1)}), bf16[2,48,768]{2,1,0:T(8,128)(2,1)}) %reduce-scatter.2.cloned.1.call-update) | async-done | bytes 147472 | tf_op jit(solution)/shard_map/reduce_scatter | solution.py:25
  79.1 0.0 all-gather.5.cloned.1.call-update
  79.1 0.0 all-gather.9.cloned.1.call-start
  79.1 0.7 all-gather.9.cloned.1.call-update
  79.8 0.0 all-gather.7.cloned.1.call-start
  79.9 0.9 convert_reduce_fusion
  80.8 0.7 multiply_add_fusion
  81.5 62.1 %all-gather.5.cloned.1.call-done = bf16[32,48,768]{2,1,0:T(8,128)(2,1)} async-done(((bf16[2,48,768]{2,1,0:T(8,128)(2,1)}), bf16[32,48,768]{2,1,0:T(8,128)(2,1)}) %all-gather.5.cloned.1.call-update) | async-done | bytes 2359312 | tf_op jit(solution)/shard_map/all_gather | solution.py:31
  143.5 2.4 copy.16
  146.0 0.5 convolution_convert_fusion
  146.5 0.7 copy.25
  147.2 0.0 all-gather.7.cloned.1.call-update
  147.2 0.0 all-gather.11.cloned.1.call-start
  147.3 0.0 copy-done.3
  147.3 1.1 fusion.6
  148.4 0.0 copy-start.4
  148.4 0.0 copy-start.1
  148.4 36.5 %all-gather.9.cloned.1.call-done = bf16[4,768,768]{2,1,0:T(8,128)(2,1)} async-done(((bf16[4,48,768]{2,1,0:T(8,128)(2,1)}), bf16[4,768,768]{2,1,0:T(8,128)(2,1)}) %all-gather.9.cloned.1.call-update) | async-done | bytes 4718608 | tf_op jit(solution)/shard_map/all_gather | solution.py:54
  185.0 43.2 %all-gather.7.cloned.1.call-done = bf16[4,768,768]{2,1,0:T(8,128)(2,1)} async-done(((bf16[4,48,768]{2,1,0:T(8,128)(2,1)}), bf16[4,768,768]{2,1,0:T(8,128)(2,1)}) %all-gather.7.cloned.1.call-update) | async-done | bytes 4718608 | tf_op jit(solution)/shard_map/all_gather | solution.py:37
  228.2 0.0 copy-done
  228.2 5.6 %multiply_reduce_fusion = (f32[4]{0:T(128)S(1)}, f32[4,48,768]{2,1,0:T(8,128)S(1)}) fusion(bf16[4,768,768]{2,1,0:T(8,128)(2,1)} %all-gather.9.cloned.1.call-done, bf16[4,48,768]{2,1,0:T(8,128)(2,1)S(1)} %copy-done, bf16[4,768,768]{2,1,0:T(8,128)(2,1)} %all-gather.7.cloned.1.call-done), kind=kOutput, calls=%fused_computation.13 | convolution fusion | flops 453427200 | bytes 10321936 | tf_op jit(solution)/shard_map/src,scd->srd/dot_general | solution.py:51
  233.8 26.8 %all-reduce = (f32[4]{0:T(128)S(1)}, f32[4]{0:T(128)S(1)}) all-reduce(f32[4]{0:T(128)S(1)} %get-tuple-element.8, f32[4]{0:T(128)S(1)} %get-tuple-element.6), channel_id=1, replica_groups=mesh['dp'=16,'own'=16] {'dp'}, use_global_device_ids=true, to_apply=%region_5.0 | all-reduce | flops 8 | bytes 64 | tf_op jit(solution)/shard_map/psum | solution.py:59
  260.5 0.0 copy-done.4
  260.5 0.8 subtract_convert_fusion
  261.4 0.0 slice-start
  261.4 0.0 copy-start.2
  261.4 0.0 all-gather.11.cloned.1.call-update
  261.4 0.0 copy-done.1
  261.4 0.0 slice-start.1
  261.4 5.0 %fusion.1 = f32[4,48,768]{2,1,0:T(8,128)} fusion(f32[4,48,768]{2,1,0:T(8,128)S(1)} %copy-done.1, bf16[4,768,768]{2,1,0:T(8,128)(2,1)} %all-gather.7.cloned.1.call-done, s32[]{:T(128)S(6)} %select_n.3), kind=kOutput, calls=%fused_computation.4 | convolution fusion | flops 226787328 | bytes 6684676 | tf_op jit(solution)/shard_map/sbc,sbd->scd/dot_general | solution.py:42
  266.4 0.0 slice-done
  266.4 0.0 copy-done.2
  266.4 0.0 slice-done.1
  266.4 2.3 fusion
  268.7 34.3 %all-gather.11.cloned.1.call-done = bf16[4,768,768]{2,1,0:T(8,128)(2,1)} async-done(((bf16[4,48,768]{2,1,0:T(8,128)(2,1)}), bf16[4,768,768]{2,1,0:T(8,128)(2,1)}) %all-gather.11.cloned.1.call-update) | async-done | bytes 4718608 | tf_op jit(solution)/shard_map/all_gather | solution.py:62
  303.1 4.8 %copy.27 = bf16[4,768,768]{2,1,0:T(8,128)(2,1)} copy(bf16[4,768,768]{2,1,0:T(8,128)(2,1)} %all-gather.11.cloned.1.call-done) | data formatting | bytes 9437184
  (3 shorter events, 0.0 us)
Async XLA Ops:
  7.2 221.0 %copy-start = (bf16[4,48,768]{2,1,0:T(8,128)(2,1)S(1)}, bf16[4,48,768]{2,1,0:T(8,128)(2,1)}, u32[]{:S(2)}) copy-start(bf16[4,48,768]{2,1,0:T(8,128)(2,1)} %param.14) | copy-start | bytes 884740
  7.2 71.9 %reduce-scatter.2.cloned.1.call-start = ((), (), s32[]{:S(2)}) async-start(), calls=%async_computation.1 | async-start | bytes 2506752 | tf_op jit(solution)/shard_map/reduce_scatter | solution.py:25
  7.9 139.4 %copy-start.3 = (f32[4,48,768]{2,1,0:T(8,128)S(1)}, f32[4,48,768]{2,1,0:T(8,128)}, u32[]{:S(2)}) copy-start(f32[4,48,768]{2,1,0:T(8,128)} %param.13) | copy-start | bytes 1769476
  7.9 135.6 %all-gather.5.cloned.1.call-start = ((), (), s32[]{:S(2)}) async-start(), calls=%async_computation.2 | async-start | bytes 2506752 | tf_op jit(solution)/shard_map/all_gather | solution.py:31
  79.1 105.9 %all-gather.9.cloned.1.call-start = ((), (), s32[]{:S(2)}) async-start(), calls=%async_computation.4 | async-start | bytes 5013504 | tf_op jit(solution)/shard_map/all_gather | solution.py:54
  79.8 148.3 %all-gather.7.cloned.1.call-start = ((), (), s32[]{:S(2)}) async-start(), calls=%async_computation.3 | async-start | bytes 5013504 | tf_op jit(solution)/shard_map/all_gather | solution.py:37
  147.2 155.8 %all-gather.11.cloned.1.call-start = ((), (), s32[]{:S(2)}) async-start(), calls=%async_computation.5 | async-start | bytes 5013504 | tf_op jit(solution)/shard_map/all_gather | solution.py:62
  148.4 112.1 %copy-start.4 = (f32[4,48,768]{2,1,0:T(8,128)S(1)}, f32[4,48,768]{2,1,0:T(8,128)}, u32[]{:S(2)}) copy-start(f32[4,48,768]{2,1,0:T(8,128)} %param.10) | copy-start | bytes 1769476
  148.4 113.0 %copy-start.1 = (f32[4,48,768]{2,1,0:T(8,128)S(1)}, f32[4,48,768]{2,1,0:T(8,128)}, u32[]{:S(2)}) copy-start(f32[4,48,768]{2,1,0:T(8,128)} %param.12) | copy-start | bytes 1769476
  261.4 5.0 %slice-start = ((s8[4718592]{0:T(1024)(128)(4,1)}), s8[524288]{0:T(1024)(128)(4,1)S(1)}, s32[]{:S(2)}) async-start(s8[4718592]{0:T(1024)(128)(4,1)} %bitcast.19), calls=%async_computation.6 | async-start | bytes 1048576
  261.4 5.0 %copy-start.2 = (f32[4,48,768]{2,1,0:T(8,128)S(1)}, f32[4,48,768]{2,1,0:T(8,128)}, u32[]{:S(2)}) copy-start(f32[4,48,768]{2,1,0:T(8,128)} %param.11) | copy-start | bytes 1769476
  261.4 5.0 %slice-start.1 = ((s8[4718592]{0:T(1024)(128)(4,1)}), s8[4194304]{0:T(1024)(128)(4,1)S(1)}, s32[]{:S(2)}) async-start(s8[4718592]{0:T(1024)(128)(4,1)} %bitcast.19), calls=%async_computation.7 | async-start | bytes 8388608
Sparse Core Ops, SparseCore 0:
  10.6 68.4 reduce-scatter.1
  81.5 61.9 all-gather.4
  145.3 39.5 all-gather.8
  187.2 40.9 all-gather.6
  261.5 41.4 all-gather.10
where the time goes:
time: 315 us; the launch traced here: 314 us
  waiting for transfers between devices  249 us (79%)
  blocking collectives  26.8 us (9%)
  between operations  13.9 us (4%)
  matrix products  13.4 us (4%)
  local copies, waits for them, and re-layouts  8.03 us (3%)
  other arithmetic  3.58 us (1%)
    reduce_scatter x1, waiting for transfers between devices, on_device(): lax.psum_scatter(grads[0].astype(jnp.float32).astype(jnp.bfloat16), 'dp',...  71.1 us
    all_gather x1, waiting for transfers between devices, on_device(): every = lax.all_gather(summed, 'own', axis=0, tiled=True)  62.1 us
    all_gather x1, waiting for transfers between devices, on_device(): full = lax.all_gather(mine, 'dp', axis=1, tiled=True)  43.2 us
    all_gather x1, waiting for transfers between devices, on_device(): lax.all_gather(root_right, 'dp', axis=1, tiled=True)  36.5 us
    all_gather x1, waiting for transfers between devices, on_device(): new_weights = lax.all_gather(fresh_rows, 'dp', axis=1, tiled=True)  34.3 us
    psum x1, blocking collectives, on_device(): adam_total, prec_total = lax.psum((adam_sq, prec_sq), 'dp')  26.8 us
    unnamed x17, local copies, waits for them, and re-layouts  8.03 us
  transfers between devices with their start and end apart: 5, of which 5 were waited for; matrix products, arithmetic and copies ran while one was open for 4% of the time, Pallas kernels for 0%

commit v1 on v0

v1 whole, which is shorter than its diff:
```python
import jax
import jax.numpy as jnp
from jax import lax
from jax.experimental import pallas as pl
from jax.experimental.pallas import tpu as pltpu
from jax.sharding import Mesh
from jax.sharding import PartitionSpec as P

Y, ZL, CORE, X, ZH = 4, 2, 2, 4, 4
CHIPS = Y * ZL
CAP = 4
BPD = 2
HALF = CAP // CORE
BF = jnp.bfloat16
F32 = jnp.float32


def slot_index(owner, capacity):
    count = owner.shape[0]
    same = owner[:, None] == owner[None, :]
    earlier = (
        jnp.arange(count, dtype=jnp.int32)[None, :] < jnp.arange(count, dtype=jnp.int32)[:, None]
    )
    rank = jnp.sum((same & earlier).astype(jnp.int32), axis=1)
    return owner * capacity + rank


def shift(axis, size, by):
    pairs = [(i, (i + by) % size) for i in range(size)]
    return lambda value: lax.ppermute(value, axis, pairs)


y_up, y_down = shift("y", Y, 1), shift("y", Y, Y - 1)
y_two = shift("y", Y, 2)
z_swap = shift("zl", ZL, 1)
core_swap = shift("core", CORE, 1)


def gather_chips(mine):
    back, ahead, other, far = y_up(mine), y_down(mine), z_swap(mine), y_two(mine)
    return (mine, back, ahead, other, far, y_up(other), y_down(other), z_swap(far))


def piece_rows(place_ref, rows):
    chip = place_ref[0] // CORE
    y, zl = chip // ZL, chip % ZL
    return [
        (((y + dy) % Y) * ZL + (zl + dz) % ZL) * rows
        for dy, dz in ((0, 0), (3, 0), (1, 0), (0, 1), (2, 0), (3, 1), (1, 1), (2, 1))
    ]


def place(refs, offs, dest, rows, slot0=0):
    for p in range(CHIPS):
        at = pl.ds(pl.multiple_of(offs[p], 16), rows)
        for s in range(HALF):
            dest[slot0 + s, at] = refs[p][s]


ANY = pl.BlockSpec(memory_space=pl.ANY)
HB = pl.BlockSpec(memory_space=pltpu.HBM)
VM = pl.BlockSpec(memory_space=pltpu.VMEM)
SM = pl.BlockSpec(memory_space=pltpu.SMEM)


def give_body(at_dp, grads, out, sems):
    copies = []
    for b in range(BPD):
        copies.append(pltpu.make_async_copy(grads.at[b, :, 1 - at_dp[0] % CORE], out.at[:, b], sems.at[b]))
    for c in copies:
        c.start()
    for c in copies:
        c.wait()


def give_call(at_dp, parts):
    blocks, chips, _, rows, width = parts.shape
    return pl.pallas_call(
        give_body,
        in_specs=[SM, ANY],
        out_specs=VM,
        out_shape=jax.ShapeDtypeStruct((chips, blocks, rows, width), BF),
        scratch_shapes=[pltpu.SemaphoreType.DMA((BPD,))],
        compiler_params=pltpu.CompilerParams(vmem_limit_bytes=4 << 20),
        name="give",
    )(at_dp, parts)


def pair_body(at_dp, grads, came, out, keep, sems):
    copies = []
    for b in range(BPD):
        copies.append(pltpu.make_async_copy(grads.at[b, :, at_dp[0] % CORE], keep.at[:, b], sems.at[b]))
    for c in copies:
        c.start()
    for c in copies:
        c.wait()
    for k in range(CHIPS):
        out[k] = (keep[k].astype(F32) + came[k].astype(F32)).astype(BF)


def pair_call(at_dp, parts, came):
    return pl.pallas_call(
        pair_body,
        in_specs=[SM, ANY, VM],
        out_specs=VM,
        out_shape=jax.ShapeDtypeStruct(came.shape, BF),
        scratch_shapes=[pltpu.VMEM(came.shape, BF), pltpu.SemaphoreType.DMA((BPD,))],
        compiler_params=pltpu.CompilerParams(vmem_limit_bytes=6 << 20),
        name="pair",
    )(at_dp, parts, came)


def precond_body(at_dp, adam_sq, left, *refs):
    rows = left.shape[1]
    g_refs, r_refs = refs[:CHIPS], refs[CHIPS : CHIPS + Y]
    prec, sums, g, r = refs[CHIPS + Y :]
    offs = piece_rows(at_dp, rows)
    place(g_refs, offs, g, rows)
    for p, n in enumerate((0, 1, 2, 4)):
        at = pl.ds(pl.multiple_of(offs[n] // (ZL * rows) * (ZL * rows), 16), ZL * rows)
        for s in range(HALF):
            r[s, at] = r_refs[p][s]
    lane = lax.broadcasted_iota(jnp.int32, (1, 128), 1)
    packed = jnp.zeros((1, 128), F32)
    for s in range(HALF):
        half = jnp.dot(left[s], g[s], preferred_element_type=F32).astype(BF)
        out = jnp.dot(half, r[s], preferred_element_type=F32)
        prec[s] = out
        packed = jnp.where(lane == s, jnp.sum(out * out), packed)
        packed = jnp.where(lane == HALF + s, adam_sq[s], packed)
    for k in range(CHIPS):
        sums[k] = packed


def precond_call(at_dp, adam_sq, left, g, r):
    slots, rows, width = left.shape
    return pl.pallas_call(
        precond_body,
        in_specs=[SM, SM] + [VM] * (1 + CHIPS + Y),
        out_specs=[VM] * 3,
        out_shape=[
            jax.ShapeDtypeStruct((slots, rows, width), F32),
            jax.ShapeDtypeStruct((CHIPS, 1, 128), F32),
            jax.ShapeDtypeStruct((slots, width, width), BF),
        ],
        scratch_shapes=[pltpu.VMEM((slots, width, width), BF)],
        compiler_params=pltpu.CompilerParams(vmem_limit_bytes=14 << 20),
        name="precond",
    )(at_dp, adam_sq, left, *g, *r)


def stats_body(at_dp, g, lout, rout):
    rows, width = lout.shape[1], lout.shape[2]
    first = piece_rows(at_dp, rows)[0]
    row_id = lax.broadcasted_iota(jnp.int32, (rows, width), 0) + first
    col_id = lax.broadcasted_iota(jnp.int32, (rows, width), 1)
    pick = (row_id == col_id).astype(BF)
    nt = (((1,), (1,)), ((), ()))
    for s in range(HALF):
        full = g[s]
        own = g[s, pl.ds(pl.multiple_of(first, 16), rows)]
        both = lax.dot_general(
            jnp.concatenate([own, pick], axis=0), full, nt, preferred_element_type=F32
        )
        lout[s] = both[:rows]
        rout[s] = jnp.dot(both[rows:].astype(BF), full, preferred_element_type=F32)


def stats_call(at_dp, g, rows):
    slots, _, width = g.shape
    return pl.pallas_call(
        stats_body,
        in_specs=[SM, VM],
        out_specs=[VM, VM],
        out_shape=[jax.ShapeDtypeStruct((slots, rows, width), F32)] * 2,
        compiler_params=pltpu.CompilerParams(vmem_limit_bytes=8 << 20),
        name="stats",
    )(at_dp, g)


def fresh_body(sums, weights, prec, out):
    total = sums[0]
    for k in range(1, CHIPS):
        total = total + sums[k]
    for s in range(HALF):
        prec_norm = jnp.sqrt(total[:, s : s + 1])
        adam_norm = jnp.sqrt(total[:, HALF + s : HALF + s + 1])
        graft = adam_norm / (prec_norm + 1e-06)
        out[s] = (weights[s] - graft * prec[s]).astype(BF)


def fresh_call(sums, weights, prec):
    return pl.pallas_call(
        fresh_body,
        in_specs=[VM] * 3,
        out_specs=VM,
        out_shape=jax.ShapeDtypeStruct(prec.shape, BF),
        compiler_params=pltpu.CompilerParams(vmem_limit_bytes=4 << 20),
        name="fresh",
    )(sums, weights, prec)


def sort_body(table, parts, out):
    for b in range(BPD):
        total = parts[0, b].astype(F32)
        for k in range(1, CHIPS):
            total = total + parts[k, b].astype(F32)
        total = total.astype(BF)
        for n in range(out.shape[0]):

            @pl.when(table[n] == b)
            def _(n=n, total=total):
                out[n] = total

    for n in range(out.shape[0]):

        @pl.when(table[n] < 0)
        def _(n=n):
            out[n] = jnp.zeros(out.shape[1:], BF)


def sort_call(table, parts):
    rows, width = parts.shape[2:]
    return pl.pallas_call(
        sort_body,
        in_specs=[SM, VM],
        out_specs=VM,
        out_shape=jax.ShapeDtypeStruct((table.shape[0], rows, width), BF),
        compiler_params=pltpu.CompilerParams(vmem_limit_bytes=5 << 20),
        name="sort",
    )(table, parts)


def pick_body(table, blocks, out):
    for n in range(out.shape[0]):
        at = table[n]
        block = blocks[jnp.maximum(at, 0)]
        out[n] = jnp.where(at >= 0, block, jnp.zeros_like(block))


def pick_call(table, blocks):
    _, rows, width = blocks.shape
    return pl.pallas_call(
        pick_body,
        in_specs=[SM, VM],
        out_specs=VM,
        out_shape=jax.ShapeDtypeStruct((table.shape[0], rows, width), BF),
        compiler_params=pltpu.CompilerParams(vmem_limit_bytes=4 << 20),
        name="pick",
    )(table, blocks)


def assemble_body(at_dp, *refs):
    mine, theirs, out = refs[:CHIPS], refs[CHIPS : 2 * CHIPS], refs[2 * CHIPS]
    rows = mine[0].shape[1]
    offs = piece_rows(at_dp, rows)
    at = HALF * (at_dp[0] % CORE)
    place(mine, offs, out, rows, at)
    place(theirs, offs, out, rows, HALF - at)


def assemble_call(at_dp, mine, theirs):
    slots, rows, width = mine[0].shape
    return pl.pallas_call(
        assemble_body,
        in_specs=[SM] + [VM] * (2 * CHIPS),
        out_specs=VM,
        out_shape=jax.ShapeDtypeStruct((CORE * slots, CHIPS * rows, width), BF),
        compiler_params=pltpu.CompilerParams(vmem_limit_bytes=12 << 20),
        name="assemble",
    )(at_dp, *mine, *theirs)


def on_device(grads, owner, weights, stat_left, stat_right, adam_second, root_left, root_right):
    y, zl, core, x, zh = (lax.axis_index(a) for a in ("y", "zl", "core", "x", "zh"))
    blocks, height, width = grads.shape[1:]
    rows = height // (CHIPS * CORE)

    def halves(value):
        return (
            lax.dynamic_slice_in_dim(value, HALF * core, HALF, 0),
            lax.dynamic_slice_in_dim(value, HALF * (1 - core), HALF, 0),
        )

    def join_rows(keep, came):
        return jnp.where(
            core == 0,
            jnp.concatenate([keep, came], axis=1),
            jnp.concatenate([came, keep], axis=1),
        )

    def to_chip_rows(value):
        keep, give = halves(value)
        return join_rows(keep, core_swap(give))

    def to_core_rows(value):
        keep = lax.dynamic_slice_in_dim(value, rows * core, rows, 1)
        give = lax.dynamic_slice_in_dim(value, rows * (1 - core), rows, 1)
        came = core_swap(give)
        return jnp.where(
            core == 0,
            jnp.concatenate([keep, came], axis=0),
            jnp.concatenate([came, keep], axis=0),
        )

    parts = grads[0].reshape(blocks, CHIPS, CORE, rows, width)
    at_dp = lax.axis_index(("y", "zl", "core")).astype(jnp.int32)[None]
    r_near = z_swap(root_right)
    chip = pair_call(at_dp, parts, core_swap(give_call(at_dp, parts)))
    chip, r_near = lax.optimization_barrier((chip, r_near))
    r_keep, r_give = halves(
        jnp.where(
            zl == 0, jnp.stack([root_right, r_near], axis=1), jnp.stack([r_near, root_right], axis=1)
        )
    )
    r_came = core_swap(r_give)
    pair = jnp.where(
        core == 0, jnp.stack([r_keep, r_came], axis=2), jnp.stack([r_came, r_keep], axis=2)
    ).reshape(HALF, ZL * CORE * rows, width)
    parts = lax.all_to_all(chip, ("y", "zl"), 0, 0, tiled=True)

    slot = slot_index(owner, CAP)
    owners = X * ZH
    me = x * ZH + zh
    mine_of = lax.dynamic_slice_in_dim(owner, me * BPD, BPD, 0)
    to = jnp.sum(
        jnp.where(
            mine_of[None, :] == jnp.arange(owners, dtype=jnp.int32)[:, None],
            jnp.arange(1, BPD + 1, dtype=jnp.int32)[None, :],
            0,
        ),
        axis=1,
    )
    to = to - 1
    target = me * CAP + jnp.arange(CAP, dtype=jnp.int32)
    source = jnp.arange(owners * BPD, dtype=jnp.int32) // BPD + 1
    held = jnp.sum(jnp.where(slot[None, :] == target[:, None], source[None, :], 0), axis=1) - 1

    left2 = to_chip_rows(root_left)
    weights2 = to_chip_rows(weights)
    left2, weights2, to, held, parts = lax.optimization_barrier(
        (left2, weights2, to, held, parts)
    )
    sends, pair = lax.optimization_barrier((sort_call(to, parts), pair))
    came = lax.all_to_all(sends, ("x", "zh"), 0, 0, tiled=True)
    r_all = (pair, y_up(pair), y_down(pair), y_two(pair))
    mine = pick_call(held, came)
    mine, r_all = lax.optimization_barrier((mine, r_all))

    g_own = to_chip_rows(mine)
    g_all = gather_chips(g_own)

    grad32 = mine.astype(F32)
    new_second = 0.9 * adam_second + 0.1 * grad32 * grad32
    adam_dir = grad32 / (jnp.sqrt(new_second) + 1e-08)
    adam_keep, adam_give = halves(jnp.sum(adam_dir * adam_dir, axis=(1, 2)))
    adam_sq = adam_keep + core_swap(adam_give)

    precond, sums, g_full = precond_call(at_dp, adam_sq, left2, g_all, r_all)
    sums = lax.all_to_all(sums, ("y", "zl"), 0, 0, tiled=True)
    lprod, rprod = stats_call(at_dp, g_full, CORE * rows)
    sums, lprod, rprod = lax.optimization_barrier((sums, lprod, rprod))
    fresh = fresh_call(sums, weights2, precond)
    new_left = 0.5 * stat_left + 0.5 * to_core_rows(lprod)
    new_right = 0.5 * stat_right + 0.5 * to_core_rows(rprod)

    n_all = gather_chips(fresh)
    n_other = tuple(core_swap(p) for p in n_all)
    new_weights = assemble_call(at_dp, n_all, n_other)
    return (new_weights, new_left, new_right, new_second)


def solution(mesh):
    fine = Mesh(mesh.devices.reshape(Y, ZL, CORE, X, ZH), ("y", "zl", "core", "x", "zh"))
    dp, own = ("y", "zl", "core"), ("x", "zh")
    rows = P(own, dp, None)
    return jax.shard_map(
        on_device,
        mesh=fine,
        in_specs=(P(dp, own, None, None), P()) + (rows,) * 6,
        out_specs=(P(own, None, None), rows, rows, rows),
        check_vma=False,
    )
```

time: 315 us -> 156 us (0.50)
  waiting for transfers between devices: 249 us -> 72.7 us
  starting transfers between devices: 0.19 us -> 55.2 us
  blocking collectives: 26.8 us -> 0 us
  matrix products: 13.4 us -> 0 us
  between operations: 13.9 us -> 0.94 us
  Pallas kernels: 0 us -> 12.7 us
  other arithmetic: 3.58 us -> 6.83 us
    all_gather x4 -> x0, waiting for transfers between devices: 176 us -> none  [the longest x1 62.1 us: on_device(): every = lax.all_gather(summed, 'own', axis=0, tiled=True)]
    reduce_scatter x1 -> x0, waiting for transfers between devices: 71.1 us -> none  [on_device(): lax.psum_scatter(grads[0].astype(jnp.float32).astype(jnp.bfloat16), 'dp',...]
    ppermute x0 -> x34, starting transfers between devices: none -> 36.9 us  [shift(): return lambda value: lax.ppermute(value, axis, pairs)]
    ppermute x0 -> x34, waiting for transfers between devices: none -> 36.6 us  [shift(): return lambda value: lax.ppermute(value, axis, pairs)]
    all_to_all x0 -> x3, waiting for transfers between devices: none -> 36.1 us  [the longest x1 25 us: on_device(): came = lax.all_to_all(sends, ('x', 'zh'), 0, 0, tiled=True)]
    psum x1 -> x0, blocking collectives: 26.8 us -> none  [on_device(): adam_total, prec_total = lax.psum((adam_sq, prec_sq), 'dp')]
    all_to_all x0 -> x3, starting transfers between devices: none -> 18.3 us  [the longest x1 9.85 us: on_device(): came = lax.all_to_all(sends, ('x', 'zh'), 0, 0, tiled=True)]
    dot_general x4 -> x0, matrix products: 13.4 us -> none  [the longest x1 5.61 us: on_device(): jnp.einsum('src,scd->srd', half, lax.all_gather(root_right, 'dp', axis=1,...]
  transfers between devices with their start and end apart: 5 -> 37, of which waited for: 5 -> 15; matrix products, arithmetic and copies ran while one was open for 4% -> 5% of each run, Pallas kernels for 0% -> 2%
where the time goes in v1:
time: 156 us; the launch traced here: 155 us
  waiting for transfers between devices  72.7 us (47%)
  starting transfers between devices  55.2 us (35%)
  Pallas kernels  12.7 us (8%)
  local copies, waits for them, and re-layouts  6.99 us (4%)
  other arithmetic  6.83 us (4%)
    ppermute x34, starting transfers between devices, shift(): return lambda value: lax.ppermute(value, axis, pairs)  36.9 us
    ppermute x34, waiting for transfers between devices, shift(): return lambda value: lax.ppermute(value, axis, pairs)  36.6 us
    all_to_all x1, waiting for transfers between devices, on_device(): came = lax.all_to_all(sends, ('x', 'zh'), 0, 0, tiled=True)  25 us
    all_to_all x1, starting transfers between devices, on_device(): came = lax.all_to_all(sends, ('x', 'zh'), 0, 0, tiled=True)  9.85 us
    all_to_all x1, waiting for transfers between devices, on_device(): parts = lax.all_to_all(chip, ('y', 'zl'), 0, 0, tiled=True)  8.5 us
    unnamed x32, local copies, waits for them, and re-layouts  5.46 us
    all_to_all x1, starting transfers between devices, on_device(): sums = lax.all_to_all(sums, ('y', 'zl'), 0, 0, tiled=True)  4.67 us
    all_to_all x1, starting transfers between devices, on_device(): parts = lax.all_to_all(chip, ('y', 'zl'), 0, 0, tiled=True)  3.81 us
  transfers between devices with their start and end apart: 37, of which 15 were waited for; matrix products, arithmetic and copies ran while one was open for 5% of the time, Pallas kernels for 2%

profile of v1, /device:TPU:1, one launch (start us, length us, event | category | flops | bytes accessed | tf_op | source)
XLA Modules:
  0.0 155.4 jit_solution(10068893058237032379)
XLA Ops:
  0.7 1.7 %copy-done = bf16[1,2,768,768]{3,2,1,0:T(8,128)(2,1)S(1)} copy-done((bf16[1,2,768,768]{3,2,1,0:T(8,128)(2,1)S(1)}, bf16[1,2,768,768]{3,2,1,0:T(8,128)(2,1)}, u32[]{:S(2)}) %copy-start) | copy-done | bytes 2359320
  2.3 1.1 give.1
  3.4 3.3 %collective-permute-start.2 = (bf16[8,2,48,768]{3,2,1,0:T(8,128)(2,1)}, bf16[8,2,48,768]{3,2,1,0:T(8,128)(2,1)S(1)}, u32[]{:S(2)}, u32[]{:S(2)}) collective-permute-start(bf16[8,2,48,768]{3,2,1,0:T(8,128)(2,1)} %give.1), channel_id=1, source_target_pairs={{0,16},{16,0},{1,17},{17,1},{2,18},{18,2},{3,19},{19,3},{4,20},{20... | collective-permute-start | bytes 3538952 | tf_op jit(solution)/shard_map/ppermute | solution.py:30
  6.8 2.7 %collective-permute-done.2.came = bf16[8,2,48,768]{3,2,1,0:T(8,128)(2,1)S(1)} collective-permute-done((bf16[8,2,48,768]{3,2,1,0:T(8,128)(2,1)}, bf16[8,2,48,768]{3,2,1,0:T(8,128)(2,1)S(1)}, u32[]{:S(2)}, u32[]{:S(2)}) %collective-permute-start.2) | collective-permute-done | bytes 1179680 | tf_op jit(solution)/shard_map/ppermute | solution.py:30
  9.5 1.4 pair.1
  10.9 4.8 %collective-permute-done.3 = bf16[4,48,768]{2,1,0:T(8,128)(2,1)} collective-permute-done((bf16[4,48,768]{2,1,0:T(8,128)(2,1)}, bf16[4,48,768]{2,1,0:T(8,128)(2,1)}, u32[]{:S(2)}, u32[]{:S(2)}) %collective-permute-start.3) | collective-permute-done | bytes 294944 | tf_op jit(solution)/shard_map/ppermute | solution.py:30
  15.7 3.8 %all-to-all-start = ((bf16[8,2,48,768]{3,2,1,0:T(8,128)(2,1)}), bf16[8,2,48,768]{3,2,1,0:T(8,128)(2,1)S(1)}, u32[]{:S(2)}, u32[]{:S(2)}) async-start(bf16[8,2,48,768]{3,2,1,0:T(8,128)(2,1)} %pair.1), calls=%async_computation | async-start | bytes 2359296 | tf_op jit(solution)/shard_map/all_to_all | solution.py:320
  19.6 1.2 collective-permute-start.1
  20.8 0.9 collective-permute-start
  22.2 1.4 maximum_select_fusion.1
  23.8 0.8 maximum_select_fusion.5.left
  24.6 0.8 collective-permute-done.4
  25.5 1.1 maximum_select_fusion.2
  26.7 8.5 %all-to-all-done.parts = bf16[8,2,48,768]{3,2,1,0:T(8,128)(2,1)S(1)} async-done(((bf16[8,2,48,768]{3,2,1,0:T(8,128)(2,1)}), bf16[8,2,48,768]{3,2,1,0:T(8,128)(2,1)S(1)}, u32[]{:S(2)}, u32[]{:S(2)}) %all-to-all-start) | async-done | bytes 1179680 | tf_op jit(solution)/shard_map/all_to_all | solution.py:320
  35.2 2.1 %sort.1 = bf16[16,48,768]{2,1,0:T(8,128)(2,1)} custom-call(s32[16]{0:T(128)S(1)} %broadcast_add_fusion.1.table, bf16[8,2,48,768]{3,2,1,0:T(8,128)(2,1)S(1)} %all-to-all-done.parts), custom_call_target="tpu_custom_call" | custom-call | tf_op jit(solution)/shard_map/sort/pallas_call | solution.py:224
  37.3 9.8 %all-to-all-start.1 = ((bf16[16,48,768]{2,1,0:T(8,128)(2,1)}), bf16[16,48,768]{2,1,0:T(8,128)(2,1)S(1)}, u32[]{:S(2)}, u32[]{:S(2)}) async-start(bf16[16,48,768]{2,1,0:T(8,128)(2,1)} %sort.1), calls=%async_computation.1 | async-start | bytes 2359296 | tf_op jit(solution)/shard_map/all_to_all | solution.py:345
  47.2 2.7 %collective-permute-start.6 = (bf16[2,192,768]{2,1,0:T(8,128)(2,1)S(1)}, bf16[2,192,768]{2,1,0:T(8,128)(2,1)S(1)}, u32[]{:S(2)}, u32[]{:S(2)}) collective-permute-start(bf16[2,192,768]{2,1,0:T(8,128)(2,1)S(1)} %bitcast.11), channel_id=1, source_target_pairs={{0,192},{64,0},{128,64},{192,128},{1,193},{65,1},{129,65},{193,129... | collective-permute-start | bytes 1769480 | tf_op jit(solution)/shard_map/ppermute | solution.py:30
  49.9 25.0 %all-to-all-done.1.blocks = bf16[16,48,768]{2,1,0:T(8,128)(2,1)S(1)} async-done(((bf16[16,48,768]{2,1,0:T(8,128)(2,1)}), bf16[16,48,768]{2,1,0:T(8,128)(2,1)S(1)}, u32[]{:S(2)}, u32[]{:S(2)}) %all-to-all-start.1) | async-done | bytes 1179680 | tf_op jit(solution)/shard_map/all_to_all | solution.py:345
  74.9 0.6 pick.1
  75.6 3.5 %collective-permute-start.9 = (bf16[2,48,768]{2,1,0:T(8,128)(2,1)S(1)}, bf16[2,48,768]{2,1,0:T(8,128)(2,1)S(1)}, u32[]{:S(2)}, u32[]{:S(2)}) collective-permute-start(bf16[2,48,768]{2,1,0:T(8,128)(2,1)S(1)} %get-tuple-element.59), channel_id=1, source_target_pairs={{0,16},{16,0},{1,17},{17,1},{2,18},{18,2},{3,19},{19,3},{4,20},{20... | collective-permute-start | bytes 442376 | tf_op jit(solution)/shard_map/ppermute | solution.py:30
  79.1 1.0 collective-permute-done.9
  80.2 1.3 collective-permute-start.12
  81.5 2.0 %collective-permute-start.13 = (bf16[2,96,768]{2,1,0:T(8,128)(2,1)S(1)}, bf16[2,96,768]{2,1,0:T(8,128)(2,1)S(1)}, u32[]{:S(2)}, u32[]{:S(2)}) collective-permute-start(bf16[2,96,768]{2,1,0:T(8,128)(2,1)S(1)} %maximum_select_fusion.6.refs_0_), channel_id=1, source_target_pairs={{0,128},{64,192},{128,0},{192,64},{1,129},{65,193},{129,1},{193,65... | collective-permute-start | bytes 884744 | tf_op jit(solution)/shard_map/ppermute | solution.py:30
  83.5 1.1 fusion.6
  84.7 0.7 collective-permute-start.8
  85.4 2.3 %collective-permute-start.10 = (bf16[2,96,768]{2,1,0:T(8,128)(2,1)S(1)}, bf16[2,96,768]{2,1,0:T(8,128)(2,1)S(1)}, u32[]{:S(2)}, u32[]{:S(2)}) collective-permute-start(bf16[2,96,768]{2,1,0:T(8,128)(2,1)S(1)} %maximum_select_fusion.6.refs_0_), channel_id=1, source_target_pairs={{0,64},{64,128},{128,192},{192,0},{1,65},{65,129},{129,193},{193,1... | collective-permute-start | bytes 884744 | tf_op jit(solution)/shard_map/ppermute | solution.py:30
  87.7 0.4 collective-permute-start.11
  88.1 0.4 collective-permute-done.12.refs_3_
  88.5 2.1 %collective-permute-start.14 = (bf16[2,96,768]{2,1,0:T(8,128)(2,1)S(1)}, bf16[2,96,768]{2,1,0:T(8,128)(2,1)S(1)}, u32[]{:S(2)}, u32[]{:S(2)}) collective-permute-start(bf16[2,96,768]{2,1,0:T(8,128)(2,1)S(1)} %collective-permute-done.12.refs_3_), channel_id=1, source_target_pairs={{0,64},{64,128},{128,192},{192,0},{1,65},{65,129},{129,193},{193,1... | collective-permute-start | bytes 884744 | tf_op jit(solution)/shard_map/ppermute | solution.py:30
  90.5 1.5 collective-permute-start.15
  92.0 1.1 collective-permute-start.16
  93.2 5.1 %collective-permute-done.10.refs_1_ = bf16[2,96,768]{2,1,0:T(8,128)(2,1)S(1)} collective-permute-done((bf16[2,96,768]{2,1,0:T(8,128)(2,1)S(1)}, bf16[2,96,768]{2,1,0:T(8,128)(2,1)S(1)}, u32[]{:S(2)}, u32[]{:S(2)}) %collective-permute-start.10) | collective-permute-done | bytes 294944 | tf_op jit(solution)/shard_map/ppermute | solution.py:30
  98.3 6.3 %collective-permute-done.14.refs_5_ = bf16[2,96,768]{2,1,0:T(8,128)(2,1)S(1)} collective-permute-done((bf16[2,96,768]{2,1,0:T(8,128)(2,1)S(1)}, bf16[2,96,768]{2,1,0:T(8,128)(2,1)S(1)}, u32[]{:S(2)}, u32[]{:S(2)}) %collective-permute-start.14) | collective-permute-done | bytes 294944 | tf_op jit(solution)/shard_map/ppermute | solution.py:30
  104.6 1.1 copy-done.5
  105.7 1.1 copy-done.7
  106.8 3.1 %precond.1 = (f32[2,96,768]{2,1,0:T(8,128)S(1)}, f32[8,1,128]{2,1,0:T(1,128)}, bf16[2,768,768]{2,1,0:T(8,128)(2,1)S(1)}) custom-call(s32[1]{0:T(128)} %bitcast.at_dp, f32[2]{0:T(128)S(1)} %dynamic-slice_add_fusion.adam_sq, bf16[2,96,768]{2,1,0:T(8,128)(2,1)S(1)} %copy-done.2, bf16[2,96,768]{2,1,0:T(8,128)(2,1)S(1)} %maximum_select_fusion.6.refs_0_, ...), custom_call_target="tpu_custom_call" | custom-call | tf_op jit(solution)/shard_map/precond/pallas_call | solution.py:137
  109.9 0.8 copy-done.8
  110.7 4.7 %all-to-all-start.2 = ((f32[8,1,128]{2,1,0:T(1,128)}), f32[8,1,128]{2,1,0:T(1,128)S(1)}, u32[]{:S(2)}, u32[]{:S(2)}) async-start(f32[8,1,128]{2,1,0:T(1,128)} %get-tuple-element.39), calls=%async_computation.2 | async-start | bytes 8192 | tf_op jit(solution)/shard_map/all_to_all | solution.py:360
  115.4 1.6 %stats.1 = (f32[2,96,768]{2,1,0:T(8,128)S(1)}, f32[2,96,768]{2,1,0:T(8,128)S(1)}) custom-call(s32[1]{0:T(128)} %bitcast.at_dp, bf16[2,768,768]{2,1,0:T(8,128)(2,1)S(1)} %get-tuple-element.40.g), custom_call_target="tpu_custom_call" | custom-call | tf_op jit(solution)/shard_map/stats/pallas_call | solution.py:171
  117.0 0.8 copy-done.3
  117.8 2.5 %all-to-all-done.2.sums = f32[8,1,128]{2,1,0:T(1,128)S(1)} async-done(((f32[8,1,128]{2,1,0:T(1,128)}), f32[8,1,128]{2,1,0:T(1,128)S(1)}, u32[]{:S(2)}, u32[]{:S(2)}) %all-to-all-start.2) | async-done | bytes 4128 | tf_op jit(solution)/shard_map/all_to_all | solution.py:360
  120.3 1.2 constant_dynamic-slice_fusion.1
  121.5 2.0 %collective-permute-start.33 = (f32[2,48,768]{2,1,0:T(8,128)S(1)}, f32[2,48,768]{2,1,0:T(8,128)S(1)}, u32[]{:S(2)}, u32[]{:S(2)}) collective-permute-start(f32[2,48,768]{2,1,0:T(8,128)S(1)} %get-tuple-element.51), channel_id=1, source_target_pairs={{0,16},{16,0},{1,17},{17,1},{2,18},{18,2},{3,19},{19,3},{4,20},{20... | collective-permute-start | bytes 884744 | tf_op jit(solution)/shard_map/ppermute | solution.py:30
  123.7 0.3 fresh.1.refs_0_
  123.9 0.4 collective-permute-start.19
  124.3 0.9 collective-permute-start.20
  125.2 0.6 collective-permute-start.17
  125.8 2.1 %collective-permute-start.18 = (bf16[2,96,768]{2,1,0:T(8,128)(2,1)S(1)}, bf16[2,96,768]{2,1,0:T(8,128)(2,1)S(1)}, u32[]{:S(2)}, u32[]{:S(2)}) collective-permute-start(bf16[2,96,768]{2,1,0:T(8,128)(2,1)S(1)} %fresh.1.refs_0_), channel_id=1, source_target_pairs={{0,192},{64,0},{128,64},{192,128},{1,193},{65,1},{129,65},{193,129... | collective-permute-start | bytes 884744 | tf_op jit(solution)/shard_map/ppermute | solution.py:30
  127.9 1.6 %collective-permute-start.24 = (bf16[2,96,768]{2,1,0:T(8,128)(2,1)S(1)}, bf16[2,96,768]{2,1,0:T(8,128)(2,1)S(1)}, u32[]{:S(2)}, u32[]{:S(2)}) collective-permute-start(bf16[2,96,768]{2,1,0:T(8,128)(2,1)S(1)} %fresh.1.refs_0_), channel_id=1, source_target_pairs={{0,16},{16,0},{1,17},{17,1},{2,18},{18,2},{3,19},{19,3},{4,20},{20... | collective-permute-start | bytes 884744 | tf_op jit(solution)/shard_map/ppermute | solution.py:30
  129.5 2.6 %collective-permute-done.19.refs_3_ = bf16[2,96,768]{2,1,0:T(8,128)(2,1)S(1)} collective-permute-done((bf16[2,96,768]{2,1,0:T(8,128)(2,1)S(1)}, bf16[2,96,768]{2,1,0:T(8,128)(2,1)S(1)}, u32[]{:S(2)}, u32[]{:S(2)}) %collective-permute-start.19) | collective-permute-done | bytes 294944 | tf_op jit(solution)/shard_map/ppermute | solution.py:30
  132.1 0.3 collective-permute-start.21
  132.4 1.2 collective-permute-done.20.refs_4_
  133.6 1.2 collective-permute-start.22
  134.8 6.3 %collective-permute-done.17.refs_1_ = bf16[2,96,768]{2,1,0:T(8,128)(2,1)S(1)} collective-permute-done((bf16[2,96,768]{2,1,0:T(8,128)(2,1)S(1)}, bf16[2,96,768]{2,1,0:T(8,128)(2,1)S(1)}, u32[]{:S(2)}, u32[]{:S(2)}) %collective-permute-start.17) | collective-permute-done | bytes 294944 | tf_op jit(solution)/shard_map/ppermute | solution.py:30
  141.1 1.2 collective-permute-start.23
  142.2 0.9 collective-permute-start.25
  143.2 4.2 %collective-permute-done.21.refs_5_ = bf16[2,96,768]{2,1,0:T(8,128)(2,1)S(1)} collective-permute-done((bf16[2,96,768]{2,1,0:T(8,128)(2,1)S(1)}, bf16[2,96,768]{2,1,0:T(8,128)(2,1)S(1)}, u32[]{:S(2)}, u32[]{:S(2)}) %collective-permute-start.21) | collective-permute-done | bytes 294944 | tf_op jit(solution)/shard_map/ppermute | solution.py:30
  147.4 0.5 collective-permute-start.27
  147.9 1.1 collective-permute-done.23.refs_7_
  149.0 1.4 collective-permute-start.29
  150.5 0.5 collective-permute-start.31
  151.0 0.9 fusion.5
  151.9 0.9 fusion.3
  152.8 2.6 %assemble.1 = bf16[4,768,768]{2,1,0:T(8,128)(2,1)} custom-call(s32[1]{0:T(128)} %bitcast.at_dp, bf16[2,96,768]{2,1,0:T(8,128)(2,1)S(1)} %fresh.1.refs_0_, bf16[2,96,768]{2,1,0:T(8,128)(2,1)S(1)} %collective-permute-done.17.refs_1_, bf16[2,96,768]{2,1,0:T(8,128)(2,1)S(1)} %collective-permute-done.18.refs_2_, ...), custom_call_target="tpu_custom_call" | custom-call | tf_op jit(solution)/shard_map/assemble/pallas_call | solution.py:264
  (76 shorter events, 1.6 us)
Async XLA Ops:
  0.6 1.7 %copy-start = (bf16[1,2,768,768]{3,2,1,0:T(8,128)(2,1)S(1)}, bf16[1,2,768,768]{3,2,1,0:T(8,128)(2,1)}, u32[]{:S(2)}) copy-start(bf16[1,2,768,768]{3,2,1,0:T(8,128)(2,1)} %param.8) | copy-start | bytes 7077892
  2.3 7.1 %copy-start.1 = (bf16[1,2,768,768]{3,2,1,0:T(8,128)(2,1)S(1)}, bf16[1,2,768,768]{3,2,1,0:T(8,128)(2,1)}, u32[]{:S(2)}) copy-start(bf16[1,2,768,768]{3,2,1,0:T(8,128)(2,1)} %param.8) | copy-start | bytes 7077892
  3.4 6.0 %collective-permute-start.2 = (bf16[8,2,48,768]{3,2,1,0:T(8,128)(2,1)}, bf16[8,2,48,768]{3,2,1,0:T(8,128)(2,1)S(1)}, u32[]{:S(2)}, u32[]{:S(2)}) collective-permute-start(bf16[8,2,48,768]{3,2,1,0:T(8,128)(2,1)} %give.1), channel_id=1, source_target_pairs={{0,16},{16,0},{1,17},{17,1},{2,18},{18,2},{3,19},{19,3},{4,20},{20... | collective-permute-start | bytes 3538952 | tf_op jit(solution)/shard_map/ppermute | solution.py:30
  6.8 8.9 %collective-permute-start.3 = (bf16[4,48,768]{2,1,0:T(8,128)(2,1)}, bf16[4,48,768]{2,1,0:T(8,128)(2,1)}, u32[]{:S(2)}, u32[]{:S(2)}) collective-permute-start(bf16[4,48,768]{2,1,0:T(8,128)(2,1)} %param.15), channel_id=1, source_target_pairs={{0,32},{32,0},{1,33},{33,1},{2,34},{34,2},{3,35},{35,3},{4,36},{36... | collective-permute-start | bytes 884744 | tf_op jit(solution)/shard_map/ppermute | solution.py:30
  10.9 8.6 %copy-start.11 = (f32[4,48,768]{2,1,0:T(8,128)S(1)}, f32[4,48,768]{2,1,0:T(8,128)}, u32[]{:S(2)}) copy-start(f32[4,48,768]{2,1,0:T(8,128)} %param.10) | copy-start | bytes 1769476
  15.7 19.5 %all-to-all-start = ((bf16[8,2,48,768]{3,2,1,0:T(8,128)(2,1)}), bf16[8,2,48,768]{3,2,1,0:T(8,128)(2,1)S(1)}, u32[]{:S(2)}, u32[]{:S(2)}) async-start(bf16[8,2,48,768]{3,2,1,0:T(8,128)(2,1)} %pair.1), calls=%async_computation | async-start | bytes 2359296 | tf_op jit(solution)/shard_map/all_to_all | solution.py:320
  19.5 1.3 copy-start.14
  19.5 2.2 %copy-start.15 = (s32[32]{0:T(128)S(1)}, s32[32]{0:T(128)}, u32[]{:S(2)}) copy-start(s32[32]{0:T(128)} %param.9) | copy-start | bytes 388
  19.6 5.0 %collective-permute-start.1 = (f32[2,48,768]{2,1,0:T(8,128)S(1)}, f32[2,48,768]{2,1,0:T(8,128)S(1)}, u32[]{:S(2)}, u32[]{:S(2)}) collective-permute-start(f32[2,48,768]{2,1,0:T(8,128)S(1)} %get-tuple-element.57), channel_id=1, source_target_pairs={{0,16},{16,0},{1,17},{17,1},{2,18},{18,2},{3,19},{19,3},{4,20},{20... | collective-permute-start | bytes 884744 | tf_op jit(solution)/shard_map/ppermute | solution.py:30
  20.8 3.0 %collective-permute-start = (bf16[2,48,768]{2,1,0:T(8,128)(2,1)S(1)}, bf16[2,48,768]{2,1,0:T(8,128)(2,1)S(1)}, u32[]{:S(2)}, u32[]{:S(2)}) collective-permute-start(bf16[2,48,768]{2,1,0:T(8,128)(2,1)S(1)} %get-tuple-element.61), channel_id=1, source_target_pairs={{0,16},{16,0},{1,17},{17,1},{2,18},{18,2},{3,19},{19,3},{4,20},{20... | collective-permute-start | bytes 442376 | tf_op jit(solution)/shard_map/ppermute | solution.py:30
  23.7 1.8 %collective-permute-start.4 = (bf16[2,2,48,768]{3,2,0,1:T(8,128)(2,1)S(1)}, bf16[2,2,48,768]{3,2,0,1:T(8,128)(2,1)}, u32[]{:S(2)}, u32[]{:S(2)}) collective-permute-start(bf16[2,2,48,768]{3,2,0,1:T(8,128)(2,1)S(1)} %get-tuple-element.55), channel_id=1, source_target_pairs={{0,16},{16,0},{1,17},{17,1},{2,18},{18,2},{3,19},{19,3},{4,20},{20... | collective-permute-start | bytes 884744 | tf_op jit(solution)/shard_map/ppermute | solution.py:30
  37.3 37.6 %all-to-all-start.1 = ((bf16[16,48,768]{2,1,0:T(8,128)(2,1)}), bf16[16,48,768]{2,1,0:T(8,128)(2,1)S(1)}, u32[]{:S(2)}, u32[]{:S(2)}) async-start(bf16[16,48,768]{2,1,0:T(8,128)(2,1)} %sort.1), calls=%async_computation.1 | async-start | bytes 2359296 | tf_op jit(solution)/shard_map/all_to_all | solution.py:345
  47.1 28.4 %collective-permute-start.5 = (bf16[2,192,768]{2,1,0:T(8,128)(2,1)S(1)}, bf16[2,192,768]{2,1,0:T(8,128)(2,1)S(1)}, u32[]{:S(2)}, u32[]{:S(2)}) collective-permute-start(bf16[2,192,768]{2,1,0:T(8,128)(2,1)S(1)} %bitcast.10), channel_id=1, source_target_pairs={{0,64},{64,128},{128,192},{192,0},{1,65},{65,129},{129,193},{193,1... | collective-permute-start | bytes 1769480 | tf_op jit(solution)/shard_map/ppermute | solution.py:30
  47.2 28.3 %collective-permute-start.6 = (bf16[2,192,768]{2,1,0:T(8,128)(2,1)S(1)}, bf16[2,192,768]{2,1,0:T(8,128)(2,1)S(1)}, u32[]{:S(2)}, u32[]{:S(2)}) collective-permute-start(bf16[2,192,768]{2,1,0:T(8,128)(2,1)S(1)} %bitcast.11), channel_id=1, source_target_pairs={{0,192},{64,0},{128,64},{192,128},{1,193},{65,1},{129,65},{193,129... | collective-permute-start | bytes 1769480 | tf_op jit(solution)/shard_map/ppermute | solution.py:30
  49.9 25.7 %collective-permute-start.7 = (bf16[2,192,768]{2,1,0:T(8,128)(2,1)S(1)}, bf16[2,192,768]{2,1,0:T(8,128)(2,1)}, u32[]{:S(2)}, u32[]{:S(2)}) collective-permute-start(bf16[2,192,768]{2,1,0:T(8,128)(2,1)S(1)} %bitcast.12), channel_id=1, source_target_pairs={{0,128},{64,192},{128,0},{192,64},{1,129},{65,193},{129,1},{193,65... | collective-permute-start | bytes 1769480 | tf_op jit(solution)/shard_map/ppermute | solution.py:30
  74.9 8.6 %copy-start.10 = (f32[4,48,768]{2,1,0:T(8,128)S(1)}, f32[4,48,768]{2,1,0:T(8,128)}, u32[]{:S(2)}) copy-start(f32[4,48,768]{2,1,0:T(8,128)} %param.13) | copy-start | bytes 1769476
  75.5 9.1 %copy-start.4 = (bf16[2,192,768]{2,1,0:T(8,128)(2,1)}, bf16[2,192,768]{2,1,0:T(8,128)(2,1)S(1)}, u32[]{:S(2)}) copy-start(bf16[2,192,768]{2,1,0:T(8,128)(2,1)S(1)} %collective-permute-done.5.refs_9_) | copy-start | bytes 1769476
  75.5 9.1 %copy-start.6 = (bf16[2,192,768]{2,1,0:T(8,128)(2,1)}, bf16[2,192,768]{2,1,0:T(8,128)(2,1)S(1)}, u32[]{:S(2)}) copy-start(bf16[2,192,768]{2,1,0:T(8,128)(2,1)S(1)} %collective-permute-done.6.refs_10_) | copy-start | bytes 1769476
  75.6 29.1 %copy-start.2 = (bf16[2,96,768]{2,1,0:T(8,128)(2,1)S(1)}, bf16[2,96,768]{2,1,0:T(8,128)(2,1)}, u32[]{:S(2)}) copy-start(bf16[2,96,768]{2,1,0:T(8,128)(2,1)} %maximum_select_fusion.5.left) | copy-start | bytes 884740
  75.6 4.5 %collective-permute-start.9 = (bf16[2,48,768]{2,1,0:T(8,128)(2,1)S(1)}, bf16[2,48,768]{2,1,0:T(8,128)(2,1)S(1)}, u32[]{:S(2)}, u32[]{:S(2)}) collective-permute-start(bf16[2,48,768]{2,1,0:T(8,128)(2,1)S(1)} %get-tuple-element.59), channel_id=1, source_target_pairs={{0,16},{16,0},{1,17},{17,1},{2,18},{18,2},{3,19},{19,3},{4,20},{20... | collective-permute-start | bytes 442376 | tf_op jit(solution)/shard_map/ppermute | solution.py:30
  80.2 8.3 %collective-permute-start.12 = (bf16[2,96,768]{2,1,0:T(8,128)(2,1)S(1)}, bf16[2,96,768]{2,1,0:T(8,128)(2,1)S(1)}, u32[]{:S(2)}, u32[]{:S(2)}) collective-permute-start(bf16[2,96,768]{2,1,0:T(8,128)(2,1)S(1)} %maximum_select_fusion.6.refs_0_), channel_id=1, source_target_pairs={{0,32},{32,0},{1,33},{33,1},{2,34},{34,2},{3,35},{35,3},{4,36},{36... | collective-permute-start | bytes 884744 | tf_op jit(solution)/shard_map/ppermute | solution.py:30
  81.5 10.5 %collective-permute-start.13 = (bf16[2,96,768]{2,1,0:T(8,128)(2,1)S(1)}, bf16[2,96,768]{2,1,0:T(8,128)(2,1)S(1)}, u32[]{:S(2)}, u32[]{:S(2)}) collective-permute-start(bf16[2,96,768]{2,1,0:T(8,128)(2,1)S(1)} %maximum_select_fusion.6.refs_0_), channel_id=1, source_target_pairs={{0,128},{64,192},{128,0},{192,64},{1,129},{65,193},{129,1},{193,65... | collective-permute-start | bytes 884744 | tf_op jit(solution)/shard_map/ppermute | solution.py:30
  84.7 5.8 %collective-permute-start.8 = (f32[2]{0:T(128)S(1)}, f32[2]{0:T(128)S(1)}, u32[]{:S(2)}, u32[]{:S(2)}) collective-permute-start(f32[2]{0:T(128)S(1)} %dynamic_slice.53), channel_id=1, source_target_pairs={{0,16},{16,0},{1,17},{17,1},{2,18},{18,2},{3,19},{19,3},{4,20},{20... | collective-permute-start | bytes 32 | tf_op jit(solution)/shard_map/ppermute | solution.py:30
  85.4 12.9 %collective-permute-start.10 = (bf16[2,96,768]{2,1,0:T(8,128)(2,1)S(1)}, bf16[2,96,768]{2,1,0:T(8,128)(2,1)S(1)}, u32[]{:S(2)}, u32[]{:S(2)}) collective-permute-start(bf16[2,96,768]{2,1,0:T(8,128)(2,1)S(1)} %maximum_select_fusion.6.refs_0_), channel_id=1, source_target_pairs={{0,64},{64,128},{128,192},{192,0},{1,65},{65,129},{129,193},{193,1... | collective-permute-start | bytes 884744 | tf_op jit(solution)/shard_map/ppermute | solution.py:30
  87.7 10.6 %collective-permute-start.11 = (bf16[2,96,768]{2,1,0:T(8,128)(2,1)S(1)}, bf16[2,96,768]{2,1,0:T(8,128)(2,1)S(1)}, u32[]{:S(2)}, u32[]{:S(2)}) collective-permute-start(bf16[2,96,768]{2,1,0:T(8,128)(2,1)S(1)} %maximum_select_fusion.6.refs_0_), channel_id=1, source_target_pairs={{0,192},{64,0},{128,64},{192,128},{1,193},{65,1},{129,65},{193,129... | collective-permute-start | bytes 884744 | tf_op jit(solution)/shard_map/ppermute | solution.py:30
  88.5 16.2 %collective-permute-start.14 = (bf16[2,96,768]{2,1,0:T(8,128)(2,1)S(1)}, bf16[2,96,768]{2,1,0:T(8,128)(2,1)S(1)}, u32[]{:S(2)}, u32[]{:S(2)}) collective-permute-start(bf16[2,96,768]{2,1,0:T(8,128)(2,1)S(1)} %collective-permute-done.12.refs_3_), channel_id=1, source_target_pairs={{0,64},{64,128},{128,192},{192,0},{1,65},{65,129},{129,193},{193,1... | collective-permute-start | bytes 884744 | tf_op jit(solution)/shard_map/ppermute | solution.py:30
  90.5 14.1 %collective-permute-start.15 = (bf16[2,96,768]{2,1,0:T(8,128)(2,1)S(1)}, bf16[2,96,768]{2,1,0:T(8,128)(2,1)S(1)}, u32[]{:S(2)}, u32[]{:S(2)}) collective-permute-start(bf16[2,96,768]{2,1,0:T(8,128)(2,1)S(1)} %collective-permute-done.12.refs_3_), channel_id=1, source_target_pairs={{0,192},{64,0},{128,64},{192,128},{1,193},{65,1},{129,65},{193,129... | collective-permute-start | bytes 884744 | tf_op jit(solution)/shard_map/ppermute | solution.py:30
  92.0 12.6 %collective-permute-start.16 = (bf16[2,96,768]{2,1,0:T(8,128)(2,1)S(1)}, bf16[2,96,768]{2,1,0:T(8,128)(2,1)S(1)}, u32[]{:S(2)}, u32[]{:S(2)}) collective-permute-start(bf16[2,96,768]{2,1,0:T(8,128)(2,1)S(1)} %collective-permute-done.13.refs_4_), channel_id=1, source_target_pairs={{0,32},{32,0},{1,33},{33,1},{2,34},{34,2},{3,35},{35,3},{4,36},{36... | collective-permute-start | bytes 884744 | tf_op jit(solution)/shard_map/ppermute | solution.py:30
  104.6 1.1 copy-start.5
  105.7 1.1 copy-start.7
  109.9 0.8 copy-start.8
  110.7 9.6 %all-to-all-start.2 = ((f32[8,1,128]{2,1,0:T(1,128)}), f32[8,1,128]{2,1,0:T(1,128)S(1)}, u32[]{:S(2)}, u32[]{:S(2)}) async-start(f32[8,1,128]{2,1,0:T(1,128)} %get-tuple-element.39), calls=%async_computation.2 | async-start | bytes 8192 | tf_op jit(solution)/shard_map/all_to_all | solution.py:360
  117.0 0.8 copy-start.3
  120.3 3.3 %copy-start.9 = (f32[2,96,768]{2,1,0:T(8,128)S(1)}, f32[2,96,768]{2,1,0:T(8,128)}, u32[]{:S(2)}) copy-start(f32[2,96,768]{2,1,0:T(8,128)} %copy-done.8) | copy-start | bytes 1769476
  121.5 29.5 %copy-start.12 = (f32[4,48,768]{2,1,0:T(8,128)S(1)}, f32[4,48,768]{2,1,0:T(8,128)}, u32[]{:S(2)}) copy-start(f32[4,48,768]{2,1,0:T(8,128)} %param.12) | copy-start | bytes 1769476
  121.5 4.3 %collective-permute-start.33 = (f32[2,48,768]{2,1,0:T(8,128)S(1)}, f32[2,48,768]{2,1,0:T(8,128)S(1)}, u32[]{:S(2)}, u32[]{:S(2)}) collective-permute-start(f32[2,48,768]{2,1,0:T(8,128)S(1)} %get-tuple-element.51), channel_id=1, source_target_pairs={{0,16},{16,0},{1,17},{17,1},{2,18},{18,2},{3,19},{19,3},{4,20},{20... | collective-permute-start | bytes 884744 | tf_op jit(solution)/shard_map/ppermute | solution.py:30
  123.5 4.3 %collective-permute-start.32 = (f32[2,48,768]{2,1,0:T(8,128)S(1)}, f32[2,48,768]{2,1,0:T(8,128)S(1)}, u32[]{:S(2)}, u32[]{:S(2)}) collective-permute-start(f32[2,48,768]{2,1,0:T(8,128)S(1)} %get-tuple-element.53), channel_id=1, source_target_pairs={{0,16},{16,0},{1,17},{17,1},{2,18},{18,2},{3,19},{19,3},{4,20},{20... | collective-permute-start | bytes 884744 | tf_op jit(solution)/shard_map/ppermute | solution.py:30
  123.9 28.0 %copy-start.13 = (f32[4,48,768]{2,1,0:T(8,128)S(1)}, f32[4,48,768]{2,1,0:T(8,128)}, u32[]{:S(2)}) copy-start(f32[4,48,768]{2,1,0:T(8,128)} %param.11) | copy-start | bytes 1769476
  123.9 8.2 %collective-permute-start.19 = (bf16[2,96,768]{2,1,0:T(8,128)(2,1)S(1)}, bf16[2,96,768]{2,1,0:T(8,128)(2,1)S(1)}, u32[]{:S(2)}, u32[]{:S(2)}) collective-permute-start(bf16[2,96,768]{2,1,0:T(8,128)(2,1)S(1)} %fresh.1.refs_0_), channel_id=1, source_target_pairs={{0,32},{32,0},{1,33},{33,1},{2,34},{34,2},{3,35},{35,3},{4,36},{36... | collective-permute-start | bytes 884744 | tf_op jit(solution)/shard_map/ppermute | solution.py:30
  124.3 9.3 %collective-permute-start.20 = (bf16[2,96,768]{2,1,0:T(8,128)(2,1)S(1)}, bf16[2,96,768]{2,1,0:T(8,128)(2,1)S(1)}, u32[]{:S(2)}, u32[]{:S(2)}) collective-permute-start(bf16[2,96,768]{2,1,0:T(8,128)(2,1)S(1)} %fresh.1.refs_0_), channel_id=1, source_target_pairs={{0,128},{64,192},{128,0},{192,64},{1,129},{65,193},{129,1},{193,65... | collective-permute-start | bytes 884744 | tf_op jit(solution)/shard_map/ppermute | solution.py:30
  125.2 15.9 %collective-permute-start.17 = (bf16[2,96,768]{2,1,0:T(8,128)(2,1)S(1)}, bf16[2,96,768]{2,1,0:T(8,128)(2,1)S(1)}, u32[]{:S(2)}, u32[]{:S(2)}) collective-permute-start(bf16[2,96,768]{2,1,0:T(8,128)(2,1)S(1)} %fresh.1.refs_0_), channel_id=1, source_target_pairs={{0,64},{64,128},{128,192},{192,0},{1,65},{65,129},{129,193},{193,1... | collective-permute-start | bytes 884744 | tf_op jit(solution)/shard_map/ppermute | solution.py:30
  125.8 16.5 %collective-permute-start.18 = (bf16[2,96,768]{2,1,0:T(8,128)(2,1)S(1)}, bf16[2,96,768]{2,1,0:T(8,128)(2,1)S(1)}, u32[]{:S(2)}, u32[]{:S(2)}) collective-permute-start(bf16[2,96,768]{2,1,0:T(8,128)(2,1)S(1)} %fresh.1.refs_0_), channel_id=1, source_target_pairs={{0,192},{64,0},{128,64},{192,128},{1,193},{65,1},{129,65},{193,129... | collective-permute-start | bytes 884744 | tf_op jit(solution)/shard_map/ppermute | solution.py:30
  127.9 15.2 %collective-permute-start.24 = (bf16[2,96,768]{2,1,0:T(8,128)(2,1)S(1)}, bf16[2,96,768]{2,1,0:T(8,128)(2,1)S(1)}, u32[]{:S(2)}, u32[]{:S(2)}) collective-permute-start(bf16[2,96,768]{2,1,0:T(8,128)(2,1)S(1)} %fresh.1.refs_0_), channel_id=1, source_target_pairs={{0,16},{16,0},{1,17},{17,1},{2,18},{18,2},{3,19},{19,3},{4,20},{20... | collective-permute-start | bytes 884744 | tf_op jit(solution)/shard_map/ppermute | solution.py:30
  132.1 15.3 %collective-permute-start.21 = (bf16[2,96,768]{2,1,0:T(8,128)(2,1)S(1)}, bf16[2,96,768]{2,1,0:T(8,128)(2,1)S(1)}, u32[]{:S(2)}, u32[]{:S(2)}) collective-permute-start(bf16[2,96,768]{2,1,0:T(8,128)(2,1)S(1)} %collective-permute-done.19.refs_3_), channel_id=1, source_target_pairs={{0,64},{64,128},{128,192},{192,0},{1,65},{65,129},{129,193},{193,1... | collective-permute-start | bytes 884744 | tf_op jit(solution)/shard_map/ppermute | solution.py:30
  133.6 14.2 %collective-permute-start.22 = (bf16[2,96,768]{2,1,0:T(8,128)(2,1)S(1)}, bf16[2,96,768]{2,1,0:T(8,128)(2,1)S(1)}, u32[]{:S(2)}, u32[]{:S(2)}) collective-permute-start(bf16[2,96,768]{2,1,0:T(8,128)(2,1)S(1)} %collective-permute-done.19.refs_3_), channel_id=1, source_target_pairs={{0,192},{64,0},{128,64},{192,128},{1,193},{65,1},{129,65},{193,129... | collective-permute-start | bytes 884744 | tf_op jit(solution)/shard_map/ppermute | solution.py:30
  141.1 8.0 %collective-permute-start.23 = (bf16[2,96,768]{2,1,0:T(8,128)(2,1)S(1)}, bf16[2,96,768]{2,1,0:T(8,128)(2,1)S(1)}, u32[]{:S(2)}, u32[]{:S(2)}) collective-permute-start(bf16[2,96,768]{2,1,0:T(8,128)(2,1)S(1)} %collective-permute-done.20.refs_4_), channel_id=1, source_target_pairs={{0,32},{32,0},{1,33},{33,1},{2,34},{34,2},{3,35},{35,3},{4,36},{36... | collective-permute-start | bytes 884744 | tf_op jit(solution)/shard_map/ppermute | solution.py:30
  142.2 8.3 %collective-permute-start.25 = (bf16[2,96,768]{2,1,0:T(8,128)(2,1)S(1)}, bf16[2,96,768]{2,1,0:T(8,128)(2,1)S(1)}, u32[]{:S(2)}, u32[]{:S(2)}) collective-permute-start(bf16[2,96,768]{2,1,0:T(8,128)(2,1)S(1)} %collective-permute-done.17.refs_1_), channel_id=1, source_target_pairs={{0,16},{16,0},{1,17},{17,1},{2,18},{18,2},{3,19},{19,3},{4,20},{20... | collective-permute-start | bytes 884744 | tf_op jit(solution)/shard_map/ppermute | solution.py:30
  143.1 7.4 %collective-permute-start.26 = (bf16[2,96,768]{2,1,0:T(8,128)(2,1)S(1)}, bf16[2,96,768]{2,1,0:T(8,128)(2,1)S(1)}, u32[]{:S(2)}, u32[]{:S(2)}) collective-permute-start(bf16[2,96,768]{2,1,0:T(8,128)(2,1)S(1)} %collective-permute-done.18.refs_2_), channel_id=1, source_target_pairs={{0,16},{16,0},{1,17},{17,1},{2,18},{18,2},{3,19},{19,3},{4,20},{20... | collective-permute-start | bytes 884744 | tf_op jit(solution)/shard_map/ppermute | solution.py:30
  147.4 5.4 %collective-permute-start.27 = (bf16[2,96,768]{2,1,0:T(8,128)(2,1)S(1)}, bf16[2,96,768]{2,1,0:T(8,128)(2,1)S(1)}, u32[]{:S(2)}, u32[]{:S(2)}) collective-permute-start(bf16[2,96,768]{2,1,0:T(8,128)(2,1)S(1)} %collective-permute-done.19.refs_3_), channel_id=1, source_target_pairs={{0,16},{16,0},{1,17},{17,1},{2,18},{18,2},{3,19},{19,3},{4,20},{20... | collective-permute-start | bytes 884744 | tf_op jit(solution)/shard_map/ppermute | solution.py:30
  147.9 4.9 %collective-permute-start.28 = (bf16[2,96,768]{2,1,0:T(8,128)(2,1)S(1)}, bf16[2,96,768]{2,1,0:T(8,128)(2,1)S(1)}, u32[]{:S(2)}, u32[]{:S(2)}) collective-permute-start(bf16[2,96,768]{2,1,0:T(8,128)(2,1)S(1)} %collective-permute-done.20.refs_4_), channel_id=1, source_target_pairs={{0,16},{16,0},{1,17},{17,1},{2,18},{18,2},{3,19},{19,3},{4,20},{20... | collective-permute-start | bytes 884744 | tf_op jit(solution)/shard_map/ppermute | solution.py:30
  149.0 3.8 %collective-permute-start.29 = (bf16[2,96,768]{2,1,0:T(8,128)(2,1)S(1)}, bf16[2,96,768]{2,1,0:T(8,128)(2,1)S(1)}, u32[]{:S(2)}, u32[]{:S(2)}) collective-permute-start(bf16[2,96,768]{2,1,0:T(8,128)(2,1)S(1)} %collective-permute-done.21.refs_5_), channel_id=1, source_target_pairs={{0,16},{16,0},{1,17},{17,1},{2,18},{18,2},{3,19},{19,3},{4,20},{20... | collective-permute-start | bytes 884744 | tf_op jit(solution)/shard_map/ppermute | solution.py:30
  150.5 2.3 %collective-permute-start.30 = (bf16[2,96,768]{2,1,0:T(8,128)(2,1)S(1)}, bf16[2,96,768]{2,1,0:T(8,128)(2,1)S(1)}, u32[]{:S(2)}, u32[]{:S(2)}) collective-permute-start(bf16[2,96,768]{2,1,0:T(8,128)(2,1)S(1)} %collective-permute-done.22.refs_6_), channel_id=1, source_target_pairs={{0,16},{16,0},{1,17},{17,1},{2,18},{18,2},{3,19},{19,3},{4,20},{20... | collective-permute-start | bytes 884744 | tf_op jit(solution)/shard_map/ppermute | solution.py:30
  150.5 2.3 %collective-permute-start.31 = (bf16[2,96,768]{2,1,0:T(8,128)(2,1)S(1)}, bf16[2,96,768]{2,1,0:T(8,128)(2,1)S(1)}, u32[]{:S(2)}, u32[]{:S(2)}) collective-permute-start(bf16[2,96,768]{2,1,0:T(8,128)(2,1)S(1)} %collective-permute-done.23.refs_7_), channel_id=1, source_target_pairs={{0,16},{16,0},{1,17},{17,1},{2,18},{18,2},{3,19},{19,3},{4,20},{20... | collective-permute-start | bytes 884744 | tf_op jit(solution)/shard_map/ppermute | solution.py:30

commit v2 on v1

--- a/solution.py
+++ b/solution.py
@@ -36,9 +36,11 @@
 core_swap = shift("core", CORE, 1)
 
 
-def gather_chips(mine):
+def gather_chips(mine, together):
     back, ahead, other, far = y_up(mine), y_down(mine), z_swap(mine), y_two(mine)
-    return (mine, back, ahead, other, far, y_up(other), y_down(other), z_swap(far))
+    if together:
+        other, far = lax.optimization_barrier((other, far))
+    return [mine, back, ahead, other, far, y_up(other), y_down(other), z_swap(far)]
 
 
 def piece_rows(place_ref, rows):
@@ -63,67 +65,66 @@
 SM = pl.BlockSpec(memory_space=pltpu.SMEM)
 
 
-def give_body(at_dp, grads, out, sems):
-    copies = []
-    for b in range(BPD):
-        copies.append(pltpu.make_async_copy(grads.at[b, :, 1 - at_dp[0] % CORE], out.at[:, b], sems.at[b]))
-    for c in copies:
-        c.start()
-    for c in copies:
-        c.wait()
-
-
-def give_call(at_dp, parts):
+def half_call(at_dp, parts, other):
     blocks, chips, _, rows, width = parts.shape
-    return pl.pallas_call(
-        give_body,
+
+    def half_body(at_dp, grads, out, sems):
+        core = at_dp[0] % CORE
+        copies = []
+        for b in range(BPD):
+            src = grads.at[b, :, 1 - core if other else core]
+            copies.append(pltpu.make_async_copy(src, out.at[:, b], sems.at[b]))
+        for c in copies:
+            c.start()
+        for c in copies:
+            c.wait()
+
+    return pl.pallas_call(
+        half_body,
         in_specs=[SM, ANY],
         out_specs=VM,
         out_shape=jax.ShapeDtypeStruct((chips, blocks, rows, width), BF),
         scratch_shapes=[pltpu.SemaphoreType.DMA((BPD,))],
         compiler_params=pltpu.CompilerParams(vmem_limit_bytes=4 << 20),
-        name="give",
+        name="give" if other else "keep",
     )(at_dp, parts)
 
 
-def pair_body(at_dp, grads, came, out, keep, sems):
-    copies = []
-    for b in range(BPD):
-        copies.append(pltpu.make_async_copy(grads.at[b, :, at_dp[0] % CORE], keep.at[:, b], sems.at[b]))
-    for c in copies:
-        c.start()
-    for c in copies:
-        c.wait()
+def pair_body(keep, came, out):
     for k in range(CHIPS):
         out[k] = (keep[k].astype(F32) + came[k].astype(F32)).astype(BF)
 
 
-def pair_call(at_dp, parts, came):
+def pair_call(keep, came):
     return pl.pallas_call(
         pair_body,
-        in_specs=[SM, ANY, VM],
+        in_specs=[VM, VM],
         out_specs=VM,
         out_shape=jax.ShapeDtypeStruct(came.shape, BF),
-        scratch_shapes=[pltpu.VMEM(came.shape, BF), pltpu.SemaphoreType.DMA((BPD,))],
-        compiler_params=pltpu.CompilerParams(vmem_limit_bytes=6 << 20),
+        compiler_params=pltpu.CompilerParams(vmem_limit_bytes=5 << 20),
         name="pair",
-    )(at_dp, parts, came)
+    )(keep, came)
 
 
 def precond_body(at_dp, adam_sq, left, *refs):
     rows = left.shape[1]
     g_refs, r_refs = refs[:CHIPS], refs[CHIPS : CHIPS + Y]
-    prec, sums, g, r = refs[CHIPS + Y :]
+    prec, sums, g, r, sems = refs[CHIPS + Y :]
     offs = piece_rows(at_dp, rows)
-    place(g_refs, offs, g, rows)
+    copies = []
     for p, n in enumerate((0, 1, 2, 4)):
         at = pl.ds(pl.multiple_of(offs[n] // (ZL * rows) * (ZL * rows), 16), ZL * rows)
-        for s in range(HALF):
-            r[s, at] = r_refs[p][s]
+        copies.append(pltpu.make_async_copy(r_refs[p], r.at[:, at], sems.at[p]))
+    for c in copies:
+        c.start()
+    place(g_refs, offs, g, rows)
     lane = lax.broadcasted_iota(jnp.int32, (1, 128), 1)
     packed = jnp.zeros((1, 128), F32)
     for s in range(HALF):
         half = jnp.dot(left[s], g[s], preferred_element_type=F32).astype(BF)
+        if s == 0:
+            for c in copies:
+                c.wait()
         out = jnp.dot(half, r[s], preferred_element_type=F32)
         prec[s] = out
         packed = jnp.where(lane == s, jnp.sum(out * out), packed)
@@ -134,36 +135,46 @@
 
 def precond_call(at_dp, adam_sq, left, g, r):
     slots, rows, width = left.shape
+    r = [pltpu.with_memory_space_constraint(p, pltpu.HBM) for p in r]
     return pl.pallas_call(
         precond_body,
-        in_specs=[SM, SM] + [VM] * (1 + CHIPS + Y),
+        in_specs=[SM, SM] + [VM] * (1 + CHIPS) + [ANY] * Y,
         out_specs=[VM] * 3,
         out_shape=[
             jax.ShapeDtypeStruct((slots, rows, width), F32),
             jax.ShapeDtypeStruct((CHIPS, 1, 128), F32),
             jax.ShapeDtypeStruct((slots, width, width), BF),
         ],
-        scratch_shapes=[pltpu.VMEM((slots, width, width), BF)],
-        compiler_params=pltpu.CompilerParams(vmem_limit_bytes=14 << 20),
+        scratch_shapes=[
+            pltpu.VMEM((slots, width, width), BF),
+            pltpu.SemaphoreType.DMA((Y,)),
+        ],
+        compiler_params=pltpu.CompilerParams(vmem_limit_bytes=6 << 20),
         name="precond",
     )(at_dp, adam_sq, left, *g, *r)
 
 
-def stats_body(at_dp, g, lout, rout):
-    rows, width = lout.shape[1], lout.shape[2]
+def stats_body(at_dp, g, lkeep, lgive, rkeep, rgive, prod):
+    part, width = lkeep.shape[1], lkeep.shape[2]
+    rows = CORE * part
     first = piece_rows(at_dp, rows)[0]
     row_id = lax.broadcasted_iota(jnp.int32, (rows, width), 0) + first
     col_id = lax.broadcasted_iota(jnp.int32, (rows, width), 1)
     pick = (row_id == col_id).astype(BF)
     nt = (((1,), (1,)), ((), ()))
+    mine = pl.ds(pl.multiple_of(at_dp[0] % CORE * part, 16), part)
+    theirs = pl.ds(pl.multiple_of((1 - at_dp[0] % CORE) * part, 16), part)
     for s in range(HALF):
         full = g[s]
         own = g[s, pl.ds(pl.multiple_of(first, 16), rows)]
         both = lax.dot_general(
             jnp.concatenate([own, pick], axis=0), full, nt, preferred_element_type=F32
         )
-        lout[s] = both[:rows]
-        rout[s] = jnp.dot(both[rows:].astype(BF), full, preferred_element_type=F32)
+        prod[0, s] = both[:rows]
+        prod[1, s] = jnp.dot(both[rows:].astype(BF), full, preferred_element_type=F32)
+        for n, (keep, give) in enumerate(((lkeep, lgive), (rkeep, rgive))):
+            keep[s] = prod[n, s, mine]
+            give[s] = prod[n, s, theirs]
 
 
 def stats_call(at_dp, g, rows):
@@ -171,9 +182,10 @@
     return pl.pallas_call(
         stats_body,
         in_specs=[SM, VM],
-        out_specs=[VM, VM],
-        out_shape=[jax.ShapeDtypeStruct((slots, rows, width), F32)] * 2,
-        compiler_params=pltpu.CompilerParams(vmem_limit_bytes=8 << 20),
+        out_specs=[VM] * 4,
+        out_shape=[jax.ShapeDtypeStruct((slots, rows, width), F32)] * 4,
+        scratch_shapes=[pltpu.VMEM((2, slots, CORE * rows, width), F32)],
+        compiler_params=pltpu.CompilerParams(vmem_limit_bytes=6 << 20),
         name="stats",
     )(at_dp, g)
 
@@ -200,23 +212,15 @@
     )(sums, weights, prec)
 
 
-def sort_body(table, parts, out):
+def sort_body(table, parts, out, totals):
     for b in range(BPD):
         total = parts[0, b].astype(F32)
         for k in range(1, CHIPS):
             total = total + parts[k, b].astype(F32)
-        total = total.astype(BF)
-        for n in range(out.shape[0]):
-
-            @pl.when(table[n] == b)
-            def _(n=n, total=total):
-                out[n] = total
-
+        totals[b] = total.astype(BF)
+    totals[BPD] = jnp.zeros(out.shape[1:], BF)
     for n in range(out.shape[0]):
-
-        @pl.when(table[n] < 0)
-        def _(n=n):
-            out[n] = jnp.zeros(out.shape[1:], BF)
+        out[n] = totals[table[n]]
 
 
 def sort_call(table, parts):
@@ -226,6 +230,7 @@
         in_specs=[SM, VM],
         out_specs=VM,
         out_shape=jax.ShapeDtypeStruct((table.shape[0], rows, width), BF),
+        scratch_shapes=[pltpu.VMEM((BPD + 1, rows, width), BF)],
         compiler_params=pltpu.CompilerParams(vmem_limit_bytes=5 << 20),
         name="sort",
     )(table, parts)
@@ -251,12 +256,20 @@
 
 
 def assemble_body(at_dp, *refs):
-    mine, theirs, out = refs[:CHIPS], refs[CHIPS : 2 * CHIPS], refs[2 * CHIPS]
-    rows = mine[0].shape[1]
+    pieces, out, sems = refs[: 2 * CHIPS], refs[2 * CHIPS], refs[2 * CHIPS + 1]
+    rows = pieces[0].shape[1]
     offs = piece_rows(at_dp, rows)
-    at = HALF * (at_dp[0] % CORE)
-    place(mine, offs, out, rows, at)
-    place(theirs, offs, out, rows, HALF - at)
+    mine = HALF * (at_dp[0] % CORE)
+    copies = []
+    for n, piece in enumerate(pieces):
+        first = mine if n < CHIPS else HALF - mine
+        at = pl.ds(pl.multiple_of(offs[n % CHIPS], 16), rows)
+        dest = out.at[pl.ds(first, HALF), at]
+        copies.append(pltpu.make_async_copy(piece, dest, sems.at[n]))
+    for c in copies:
+        c.start()
+    for c in copies:
+        c.wait()
 
 
 def assemble_call(at_dp, mine, theirs):
@@ -264,9 +277,10 @@
     return pl.pallas_call(
         assemble_body,
         in_specs=[SM] + [VM] * (2 * CHIPS),
-        out_specs=VM,
+        out_specs=ANY,
         out_shape=jax.ShapeDtypeStruct((CORE * slots, CHIPS * rows, width), BF),
-        compiler_params=pltpu.CompilerParams(vmem_limit_bytes=12 << 20),
+        scratch_shapes=[pltpu.SemaphoreType.DMA((2 * CHIPS,))],
+        compiler_params=pltpu.CompilerParams(vmem_limit_bytes=7 << 20),
         name="assemble",
     )(at_dp, *mine, *theirs)
 
@@ -293,20 +307,19 @@
         keep, give = halves(value)
         return join_rows(keep, core_swap(give))
 
-    def to_core_rows(value):
-        keep = lax.dynamic_slice_in_dim(value, rows * core, rows, 1)
-        give = lax.dynamic_slice_in_dim(value, rows * (1 - core), rows, 1)
-        came = core_swap(give)
+    def join_slots(keep, came):
         return jnp.where(
             core == 0,
             jnp.concatenate([keep, came], axis=0),
             jnp.concatenate([came, keep], axis=0),
         )
 
-    parts = grads[0].reshape(blocks, CHIPS, CORE, rows, width)
+    parts = pltpu.with_memory_space_constraint(
+        grads[0].reshape(blocks, CHIPS, CORE, rows, width), pltpu.HBM
+    )
     at_dp = lax.axis_index(("y", "zl", "core")).astype(jnp.int32)[None]
     r_near = z_swap(root_right)
-    chip = pair_call(at_dp, parts, core_swap(give_call(at_dp, parts)))
+    chip = pair_call(half_call(at_dp, parts, False), core_swap(half_call(at_dp, parts, True)))
     chip, r_near = lax.optimization_barrier((chip, r_near))
     r_keep, r_give = halves(
         jnp.where(
@@ -323,15 +336,9 @@
     owners = X * ZH
     me = x * ZH + zh
     mine_of = lax.dynamic_slice_in_dim(owner, me * BPD, BPD, 0)
-    to = jnp.sum(
-        jnp.where(
-            mine_of[None, :] == jnp.arange(owners, dtype=jnp.int32)[:, None],
-            jnp.arange(1, BPD + 1, dtype=jnp.int32)[None, :],
-            0,
-        ),
-        axis=1,
-    )
-    to = to - 1
+    hit = mine_of[None, :] == jnp.arange(owners, dtype=jnp.int32)[:, None]
+    order = jnp.arange(BPD, dtype=jnp.int32)
+    to = BPD + jnp.maximum(jnp.sum(jnp.where(hit, order[None, :] - BPD, 0), axis=1), -BPD)
     target = me * CAP + jnp.arange(CAP, dtype=jnp.int32)
     source = jnp.arange(owners * BPD, dtype=jnp.int32) // BPD + 1
     held = jnp.sum(jnp.where(slot[None, :] == target[:, None], source[None, :], 0), axis=1) - 1
@@ -347,9 +354,9 @@
     mine = pick_call(held, came)
     mine, r_all = lax.optimization_barrier((mine, r_all))
 
-    g_own = to_chip_rows(mine)
-    g_all = gather_chips(g_own)
-
+    g_all = gather_chips(to_chip_rows(mine), True)
+
+    mine, _ = lax.optimization_barrier((mine, g_all[1]))
     grad32 = mine.astype(F32)
     new_second = 0.9 * adam_second + 0.1 * grad32 * grad32
     adam_dir = grad32 / (jnp.sqrt(new_second) + 1e-08)
@@ -358,14 +365,18 @@
 
     precond, sums, g_full = precond_call(at_dp, adam_sq, left2, g_all, r_all)
     sums = lax.all_to_all(sums, ("y", "zl"), 0, 0, tiled=True)
-    lprod, rprod = stats_call(at_dp, g_full, CORE * rows)
-    sums, lprod, rprod = lax.optimization_barrier((sums, lprod, rprod))
+    prods = stats_call(at_dp, g_full, rows)
+    lkeep, lgive, rkeep, rgive = prods
+    sums, lcame, rcame = lax.optimization_barrier((sums, core_swap(lgive), core_swap(rgive)))
+    precond = pltpu.with_memory_space_constraint(precond, pltpu.HBM)
     fresh = fresh_call(sums, weights2, precond)
-    new_left = 0.5 * stat_left + 0.5 * to_core_rows(lprod)
-    new_right = 0.5 * stat_right + 0.5 * to_core_rows(rprod)
-
-    n_all = gather_chips(fresh)
-    n_other = tuple(core_swap(p) for p in n_all)
+
+    n_all = gather_chips(fresh, False)
+    n_all[:5] = lax.optimization_barrier(n_all[:5])
+    new_left = 0.5 * stat_left + 0.5 * join_slots(lkeep, lcame)
+    new_right = 0.5 * stat_right + 0.5 * join_slots(rkeep, rcame)
+    n_all[7], new_left, new_right = lax.optimization_barrier((n_all[7], new_left, new_right))
+    n_other = [core_swap(p) for p in n_all]
     new_weights = assemble_call(at_dp, n_all, n_other)
     return (new_weights, new_left, new_right, new_second)
 

time: 156 us -> 151 us (0.968)
  blocking collectives: 0 us -> 10.3 us
  starting transfers between devices: 55.2 us -> 48.2 us
  local copies, waits for them, and re-layouts: 6.99 us -> 1.76 us
  waiting for transfers between devices: 72.7 us -> 69.9 us
  other arithmetic: 6.83 us -> 4.25 us
  Pallas kernels: 12.7 us -> 14.9 us
    all_to_all x0 -> x1, blocking collectives: none -> 10.3 us  [on_device(): sums = lax.all_to_all(sums, ('y', 'zl'), 0, 0, tiled=True)]
    unnamed x32 -> x18, local copies, waits for them, and re-layouts: 5.46 us -> 0.05 us
    all_to_all x1 -> x0, starting transfers between devices: 4.67 us -> none  [on_device(): sums = lax.all_to_all(sums, ('y', 'zl'), 0, 0, tiled=True)]
    ppermute x34, waiting for transfers between devices: 36.6 us -> 33.6 us  [shift(): return lambda value: lax.ppermute(value, axis, pairs)]
    all_to_all x1 -> x0, waiting for transfers between devices: 2.54 us -> none  [on_device(): sums = lax.all_to_all(sums, ('y', 'zl'), 0, 0, tiled=True)]
    all_to_all x1, waiting for transfers between devices: 8.5 us -> 10.9 us  [on_device(): parts = lax.all_to_all(chip, ('y', 'zl'), 0, 0, tiled=True)]
    ppermute x34, starting transfers between devices: 36.9 us -> 34.5 us  [shift(): return lambda value: lax.ppermute(value, axis, pairs)]
    pallas_call x4 -> x5, Pallas kernels: 7.23 us -> 8.9 us  [the longest x1 3.36 us: precond_call(): pl.pallas_call(precond_body, in_specs=[SM, SM] + [VM] * (1 + CHIPS) + [AN...]
  transfers between devices with their start and end apart: 37 -> 36, of which waited for: 15 -> 20; matrix products, arithmetic and copies ran while one was open for 5% -> 4% of each run, Pallas kernels for 2% -> 2%
where the time goes in v2:
time: 151 us; the launch traced here: 150 us
  waiting for transfers between devices  69.9 us (46%)
  starting transfers between devices  48.2 us (32%)
  Pallas kernels  14.9 us (10%)
  blocking collectives  10.3 us (7%)
  other arithmetic  4.25 us (3%)
  local copies, waits for them, and re-layouts  1.76 us (1%)
    ppermute x34, starting transfers between devices, shift(): return lambda value: lax.ppermute(value, axis, pairs)  34.5 us
    ppermute x34, waiting for transfers between devices, shift(): return lambda value: lax.ppermute(value, axis, pairs)  33.6 us
    all_to_all x1, waiting for transfers between devices, on_device(): came = lax.all_to_all(sends, ('x', 'zh'), 0, 0, tiled=True)  25.3 us
    all_to_all x1, waiting for transfers between devices, on_device(): parts = lax.all_to_all(chip, ('y', 'zl'), 0, 0, tiled=True)  10.9 us
    all_to_all x1, blocking collectives, on_device(): sums = lax.all_to_all(sums, ('y', 'zl'), 0, 0, tiled=True)  10.3 us
    all_to_all x1, starting transfers between devices, on_device(): came = lax.all_to_all(sends, ('x', 'zh'), 0, 0, tiled=True)  9.85 us
    all_to_all x1, starting transfers between devices, on_device(): parts = lax.all_to_all(chip, ('y', 'zl'), 0, 0, tiled=True)  3.81 us
    pallas_call x1, Pallas kernels, precond_call(): pl.pallas_call(precond_body, in_specs=[SM, SM] + [VM] * (1 + CHIPS) + [AN...  3.36 us
  transfers between devices with their start and end apart: 36, of which 20 were waited for; matrix products, arithmetic and copies ran while one was open for 4% of the time, Pallas kernels for 2%

profile of v2, /device:TPU:1, one launch (start us, length us, event | category | flops | bytes accessed | tf_op | source)
XLA Modules:
  0.0 150.3 jit_solution(4592752084650608433)
XLA Ops:
  0.7 1.3 give.1
  2.0 3.3 %collective-permute-start.2 = (bf16[8,2,48,768]{3,2,1,0:T(8,128)(2,1)S(1)}, bf16[8,2,48,768]{3,2,1,0:T(8,128)(2,1)S(1)}, u32[]{:S(2)}, u32[]{:S(2)}) collective-permute-start(bf16[8,2,48,768]{3,2,1,0:T(8,128)(2,1)S(1)} %give.1), channel_id=1, source_target_pairs={{0,16},{16,0},{1,17},{17,1},{2,18},{18,2},{3,19},{19,3},{4,20},{20... | collective-permute-start | bytes 3538952 | tf_op jit(solution)/shard_map/ppermute | solution.py:30
  5.3 0.7 constant_dynamic-slice_fusion.6
  6.0 0.3 collective-permute-start
  6.3 1.3 keep.1
  7.6 0.2 collective-permute-done.2.came
  7.8 1.3 pair.1
  9.1 4.8 %collective-permute-done.3 = bf16[4,48,768]{2,1,0:T(8,128)(2,1)S(1)} collective-permute-done((bf16[4,48,768]{2,1,0:T(8,128)(2,1)S(1)}, bf16[4,48,768]{2,1,0:T(8,128)(2,1)S(1)}, u32[]{:S(2)}, u32[]{:S(2)}) %collective-permute-start.3) | collective-permute-done | bytes 294944 | tf_op jit(solution)/shard_map/ppermute | solution.py:30
  13.9 3.8 %all-to-all-start = ((bf16[8,2,48,768]{3,2,1,0:T(8,128)(2,1)}), bf16[8,2,48,768]{3,2,1,0:T(8,128)(2,1)S(1)}, u32[]{:S(2)}, u32[]{:S(2)}) async-start(bf16[8,2,48,768]{3,2,1,0:T(8,128)(2,1)} %pair.1), calls=%async_computation | async-start | bytes 2359296 | tf_op jit(solution)/shard_map/all_to_all | solution.py:333
  17.7 0.8 constant_dynamic-slice_fusion.4
  18.5 1.2 collective-permute-start.1
  19.7 0.2 convert_reduce_fusion
  19.9 0.2 select_reduce_fusion
  20.5 0.7 collective-permute-done.1
  21.2 1.1 maximum_select_fusion.weights
  22.5 10.9 %all-to-all-done.parts = bf16[8,2,48,768]{3,2,1,0:T(8,128)(2,1)S(1)} async-done(((bf16[8,2,48,768]{3,2,1,0:T(8,128)(2,1)}), bf16[8,2,48,768]{3,2,1,0:T(8,128)(2,1)S(1)}, u32[]{:S(2)}, u32[]{:S(2)}) %all-to-all-start) | async-done | bytes 1179680 | tf_op jit(solution)/shard_map/all_to_all | solution.py:333
  33.4 1.8 %sort.1 = bf16[16,48,768]{2,1,0:T(8,128)(2,1)} custom-call(s32[16]{0:T(128)S(1)} %maximum_add_fusion.table, bf16[8,2,48,768]{3,2,1,0:T(8,128)(2,1)S(1)} %all-to-all-done.parts), custom_call_target="tpu_custom_call" | custom-call | tf_op jit(solution)/shard_map/sort/pallas_call | solution.py:228
  35.2 9.8 %all-to-all-start.1 = ((bf16[16,48,768]{2,1,0:T(8,128)(2,1)}), bf16[16,48,768]{2,1,0:T(8,128)(2,1)S(1)}, u32[]{:S(2)}, u32[]{:S(2)}) async-start(bf16[16,48,768]{2,1,0:T(8,128)(2,1)} %sort.1), calls=%async_computation.1 | async-start | bytes 2359296 | tf_op jit(solution)/shard_map/all_to_all | solution.py:352
  45.1 1.0 collective-permute-start.7
  46.0 0.9 collective-permute-start.6
  46.9 0.6 collective-permute-start.5
  47.5 25.3 %all-to-all-done.1.blocks = bf16[16,48,768]{2,1,0:T(8,128)(2,1)S(1)} async-done(((bf16[16,48,768]{2,1,0:T(8,128)(2,1)}), bf16[16,48,768]{2,1,0:T(8,128)(2,1)S(1)}, u32[]{:S(2)}, u32[]{:S(2)}) %all-to-all-start.1) | async-done | bytes 1179680 | tf_op jit(solution)/shard_map/all_to_all | solution.py:352
  72.8 0.6 pick.1
  73.5 1.2 collective-permute-done.5.refs_9_
  74.7 2.3 %collective-permute-start.8 = (bf16[2,48,768]{2,1,0:T(8,128)(2,1)S(1)}, bf16[2,48,768]{2,1,0:T(8,128)(2,1)S(1)}, u32[]{:S(2)}, u32[]{:S(2)}) collective-permute-start(bf16[2,48,768]{2,1,0:T(8,128)(2,1)S(1)} %get-tuple-element.81), channel_id=1, source_target_pairs={{0,16},{16,0},{1,17},{17,1},{2,18},{18,2},{3,19},{19,3},{4,20},{20... | collective-permute-start | bytes 442376 | tf_op jit(solution)/shard_map/ppermute | solution.py:30
  77.0 1.0 collective-permute-done.8
  78.1 3.2 %collective-permute-start.13 = (bf16[2,96,768]{2,1,0:T(8,128)(2,1)S(1)}, bf16[2,96,768]{2,1,0:T(8,128)(2,1)S(1)}, u32[]{:S(2)}, u32[]{:S(2)}) collective-permute-start(bf16[2,96,768]{2,1,0:T(8,128)(2,1)S(1)} %maximum_select_fusion.6.refs_0_), channel_id=1, source_target_pairs={{0,128},{64,192},{128,0},{192,64},{1,129},{65,193},{129,1},{193,65... | collective-permute-start | bytes 884744 | tf_op jit(solution)/shard_map/ppermute | solution.py:30
  81.3 2.1 %collective-permute-start.9 = (bf16[2,96,768]{2,1,0:T(8,128)(2,1)S(1)}, bf16[2,96,768]{2,1,0:T(8,128)(2,1)S(1)}, u32[]{:S(2)}, u32[]{:S(2)}) collective-permute-start(bf16[2,96,768]{2,1,0:T(8,128)(2,1)S(1)} %maximum_select_fusion.6.refs_0_), channel_id=1, source_target_pairs={{0,64},{64,128},{128,192},{192,0},{1,65},{65,129},{129,193},{193,1... | collective-permute-start | bytes 884744 | tf_op jit(solution)/shard_map/ppermute | solution.py:30
  83.4 0.6 collective-permute-start.11
  84.0 4.3 %collective-permute-done.13.refs_4_ = bf16[2,96,768]{2,1,0:T(8,128)(2,1)S(1)} collective-permute-done((bf16[2,96,768]{2,1,0:T(8,128)(2,1)S(1)}, bf16[2,96,768]{2,1,0:T(8,128)(2,1)S(1)}, u32[]{:S(2)}, u32[]{:S(2)}) %collective-permute-start.13) | collective-permute-done | bytes 294944 | tf_op jit(solution)/shard_map/ppermute | solution.py:30
  88.3 0.9 collective-permute-done.12.refs_3_
  89.2 1.3 collective-permute-start.15
  90.7 1.9 %collective-permute-start.16 = (bf16[2,96,768]{2,1,0:T(8,128)(2,1)S(1)}, bf16[2,96,768]{2,1,0:T(8,128)(2,1)S(1)}, u32[]{:S(2)}, u32[]{:S(2)}) collective-permute-start(bf16[2,96,768]{2,1,0:T(8,128)(2,1)S(1)} %collective-permute-done.13.refs_4_), channel_id=1, source_target_pairs={{0,32},{32,0},{1,33},{33,1},{2,34},{34,2},{3,35},{35,3},{4,36},{36... | collective-permute-start | bytes 884744 | tf_op jit(solution)/shard_map/ppermute | solution.py:30
  92.6 2.5 %collective-permute-done.9.refs_1_ = bf16[2,96,768]{2,1,0:T(8,128)(2,1)S(1)} collective-permute-done((bf16[2,96,768]{2,1,0:T(8,128)(2,1)S(1)}, bf16[2,96,768]{2,1,0:T(8,128)(2,1)S(1)}, u32[]{:S(2)}, u32[]{:S(2)}) %collective-permute-start.9) | collective-permute-done | bytes 294944 | tf_op jit(solution)/shard_map/ppermute | solution.py:30
  95.1 1.1 fusion.6
  96.3 0.6 collective-permute-start.10
  96.9 0.8 collective-permute-done.10
  97.8 2.4 %collective-permute-done.14.refs_5_ = bf16[2,96,768]{2,1,0:T(8,128)(2,1)S(1)} collective-permute-done((bf16[2,96,768]{2,1,0:T(8,128)(2,1)S(1)}, bf16[2,96,768]{2,1,0:T(8,128)(2,1)S(1)}, u32[]{:S(2)}, u32[]{:S(2)}) %collective-permute-start.14) | collective-permute-done | bytes 294944 | tf_op jit(solution)/shard_map/ppermute | solution.py:30
  100.3 3.4 %precond.1 = (f32[2,96,768]{2,1,0:T(8,128)S(1)}, f32[8,1,128]{2,1,0:T(1,128)S(1)}, bf16[2,768,768]{2,1,0:T(8,128)(2,1)S(1)}) custom-call(s32[1]{0:T(128)} %bitcast.at_dp, f32[2]{0:T(128)S(1)} %dynamic-slice_add_fusion.adam_sq, bf16[2,96,768]{2,1,0:T(8,128)(2,1)S(1)} %maximum_select_fusion.5.left, bf16[2,96,768]{2,1,0:T(8,128)(2,1)S(1)} %maximum_select_fusion.6.refs_0_, ...), custom_call_target="tpu_custom_call" | custom-call | tf_op jit(solution)/shard_map/precond/pallas_call | solution.py:139
  103.7 1.7 %stats.1 = (f32[2,48,768]{2,1,0:T(8,128)S(1)}, f32[2,48,768]{2,1,0:T(8,128)S(1)}, f32[2,48,768]{2,1,0:T(8,128)S(1)}, f32[2,48,768]{2,1,0:T(8,128)S(1)}) custom-call(s32[1]{0:T(128)} %bitcast.at_dp, bf16[2,768,768]{2,1,0:T(8,128)(2,1)S(1)} %get-tuple-element.56.g), custom_call_target="tpu_custom_call" | custom-call | tf_op jit(solution)/shard_map/stats/pallas_call | solution.py:182
  105.4 1.7 %collective-permute-start.17 = (f32[2,48,768]{2,1,0:T(8,128)S(1)}, f32[2,48,768]{2,1,0:T(8,128)S(1)}, u32[]{:S(2)}, u32[]{:S(2)}) collective-permute-start(f32[2,48,768]{2,1,0:T(8,128)S(1)} %get-tuple-element.57), channel_id=1, source_target_pairs={{0,16},{16,0},{1,17},{17,1},{2,18},{18,2},{3,19},{19,3},{4,20},{20... | collective-permute-start | bytes 884744 | tf_op jit(solution)/shard_map/ppermute | solution.py:30
  107.2 10.3 %all_to_all.15.sums = f32[8,1,128]{2,1,0:T(1,128)S(1)} all-to-all(f32[8,1,128]{2,1,0:T(1,128)S(1)} %get-tuple-element.55), channel_id=1, replica_groups=mesh['y'=4,'zl'=2,'core'=2,'x'=4,'zh'=4] {'y','zl'}, dimensions={0} | all-to-all | bytes 8192 | tf_op jit(solution)/shard_map/all_to_all | solution.py:367
  117.5 1.3 fresh.1.refs_0_
  118.8 1.0 collective-permute-start.22
  119.8 0.3 collective-permute-start.21
  120.1 1.8 %collective-permute-start.20 = (bf16[2,96,768]{2,1,0:T(8,128)(2,1)S(1)}, bf16[2,96,768]{2,1,0:T(8,128)(2,1)S(1)}, u32[]{:S(2)}, u32[]{:S(2)}) collective-permute-start(bf16[2,96,768]{2,1,0:T(8,128)(2,1)S(1)} %fresh.1.refs_0_), channel_id=1, source_target_pairs={{0,192},{64,0},{128,64},{192,128},{1,193},{65,1},{129,65},{193,129... | collective-permute-start | bytes 884744 | tf_op jit(solution)/shard_map/ppermute | solution.py:30
  121.9 5.2 %collective-permute-done.22.refs_4_ = bf16[2,96,768]{2,1,0:T(8,128)(2,1)S(1)} collective-permute-done((bf16[2,96,768]{2,1,0:T(8,128)(2,1)S(1)}, bf16[2,96,768]{2,1,0:T(8,128)(2,1)S(1)}, u32[]{:S(2)}, u32[]{:S(2)}) %collective-permute-start.22) | collective-permute-done | bytes 294944 | tf_op jit(solution)/shard_map/ppermute | solution.py:30
  127.1 0.3 collective-permute-start.25
  127.4 0.9 collective-permute-start.24
  128.3 4.5 %collective-permute-done.20.refs_2_ = bf16[2,96,768]{2,1,0:T(8,128)(2,1)S(1)} collective-permute-done((bf16[2,96,768]{2,1,0:T(8,128)(2,1)S(1)}, bf16[2,96,768]{2,1,0:T(8,128)(2,1)S(1)}, u32[]{:S(2)}, u32[]{:S(2)}) %collective-permute-start.20) | collective-permute-done | bytes 294944 | tf_op jit(solution)/shard_map/ppermute | solution.py:30
  132.8 2.0 %collective-permute-done.19.refs_1_ = bf16[2,96,768]{2,1,0:T(8,128)(2,1)S(1)} collective-permute-done((bf16[2,96,768]{2,1,0:T(8,128)(2,1)S(1)}, bf16[2,96,768]{2,1,0:T(8,128)(2,1)S(1)}, u32[]{:S(2)}, u32[]{:S(2)}) %collective-permute-start.19) | collective-permute-done | bytes 294944 | tf_op jit(solution)/shard_map/ppermute | solution.py:30
  134.8 1.1 collective-permute-start.23
  135.9 1.2 collective-permute-start.26
  137.2 1.8 %collective-permute-start.28 = (bf16[2,96,768]{2,1,0:T(8,128)(2,1)S(1)}, bf16[2,96,768]{2,1,0:T(8,128)(2,1)S(1)}, u32[]{:S(2)}, u32[]{:S(2)}) collective-permute-start(bf16[2,96,768]{2,1,0:T(8,128)(2,1)S(1)} %collective-permute-done.20.refs_2_), channel_id=1, source_target_pairs={{0,16},{16,0},{1,17},{17,1},{2,18},{18,2},{3,19},{19,3},{4,20},{20... | collective-permute-start | bytes 884744 | tf_op jit(solution)/shard_map/ppermute | solution.py:30
  138.9 1.1 fusion.3
  140.1 0.9 collective-permute-start.29
  141.0 1.2 collective-permute-done.23.refs_5_
  142.2 3.2 %collective-permute-start.30 = (bf16[2,96,768]{2,1,0:T(8,128)(2,1)S(1)}, bf16[2,96,768]{2,1,0:T(8,128)(2,1)S(1)}, u32[]{:S(2)}, u32[]{:S(2)}) collective-permute-start(bf16[2,96,768]{2,1,0:T(8,128)(2,1)S(1)} %collective-permute-done.22.refs_4_), channel_id=1, source_target_pairs={{0,16},{16,0},{1,17},{17,1},{2,18},{18,2},{3,19},{19,3},{4,20},{20... | collective-permute-start | bytes 884744 | tf_op jit(solution)/shard_map/ppermute | solution.py:30
  145.4 0.5 collective-permute-start.31
  146.0 0.6 collective-permute-done.30.refs_12_
  146.6 0.4 collective-permute-done.32.refs_14_
  147.0 0.4 collective-permute-done.31.refs_13_
  147.4 0.4 collective-permute-done.33.refs_15_
  147.9 2.3 %assemble.1 = bf16[4,768,768]{2,1,0:T(8,128)(2,1)} custom-call(s32[1]{0:T(128)} %bitcast.at_dp, bf16[2,96,768]{2,1,0:T(8,128)(2,1)S(1)} %fresh.1.refs_0_, bf16[2,96,768]{2,1,0:T(8,128)(2,1)S(1)} %collective-permute-done.19.refs_1_, bf16[2,96,768]{2,1,0:T(8,128)(2,1)S(1)} %collective-permute-done.20.refs_2_, ...), custom_call_target="tpu_custom_call" | custom-call | tf_op jit(solution)/shard_map/assemble/pallas_call | solution.py:277
  (60 shorter events, 1.4 us)
Async XLA Ops:
  0.6 4.7 %copy-start.7 = (bf16[4,48,768]{2,1,0:T(8,128)(2,1)S(1)}, bf16[4,48,768]{2,1,0:T(8,128)(2,1)}, u32[]{:S(2)}) copy-start(bf16[4,48,768]{2,1,0:T(8,128)(2,1)} %param.15) | copy-start | bytes 884740
  0.7 4.7 %copy-start.6 = (bf16[4,48,768]{2,1,0:T(8,128)(2,1)S(1)}, bf16[4,48,768]{2,1,0:T(8,128)(2,1)}, u32[]{:S(2)}) copy-start(bf16[4,48,768]{2,1,0:T(8,128)(2,1)} %param.14) | copy-start | bytes 884740
  2.0 5.8 %collective-permute-start.2 = (bf16[8,2,48,768]{3,2,1,0:T(8,128)(2,1)S(1)}, bf16[8,2,48,768]{3,2,1,0:T(8,128)(2,1)S(1)}, u32[]{:S(2)}, u32[]{:S(2)}) collective-permute-start(bf16[8,2,48,768]{3,2,1,0:T(8,128)(2,1)S(1)} %give.1), channel_id=1, source_target_pairs={{0,16},{16,0},{1,17},{17,1},{2,18},{18,2},{3,19},{19,3},{4,20},{20... | collective-permute-start | bytes 3538952 | tf_op jit(solution)/shard_map/ppermute | solution.py:30
  5.3 8.6 %collective-permute-start.3 = (bf16[4,48,768]{2,1,0:T(8,128)(2,1)S(1)}, bf16[4,48,768]{2,1,0:T(8,128)(2,1)S(1)}, u32[]{:S(2)}, u32[]{:S(2)}) collective-permute-start(bf16[4,48,768]{2,1,0:T(8,128)(2,1)S(1)} %copy-done.7), channel_id=1, source_target_pairs={{0,32},{32,0},{1,33},{33,1},{2,34},{34,2},{3,35},{35,3},{4,36},{36... | collective-permute-start | bytes 884744 | tf_op jit(solution)/shard_map/ppermute | solution.py:30
  6.0 14.5 %collective-permute-start = (bf16[2,48,768]{2,1,0:T(8,128)(2,1)}, bf16[2,48,768]{2,1,0:T(8,128)(2,1)S(1)}, u32[]{:S(2)}, u32[]{:S(2)}) collective-permute-start(bf16[2,48,768]{2,1,0:T(8,128)(2,1)} %get-tuple-element.83), channel_id=1, source_target_pairs={{0,16},{16,0},{1,17},{17,1},{2,18},{18,2},{3,19},{19,3},{4,20},{20... | collective-permute-start | bytes 442376 | tf_op jit(solution)/shard_map/ppermute | solution.py:30
  9.1 8.6 %copy-start.3 = (f32[4,48,768]{2,1,0:T(8,128)S(1)}, f32[4,48,768]{2,1,0:T(8,128)}, u32[]{:S(2)}) copy-start(f32[4,48,768]{2,1,0:T(8,128)} %param.10) | copy-start | bytes 1769476
  13.9 19.5 %all-to-all-start = ((bf16[8,2,48,768]{3,2,1,0:T(8,128)(2,1)}), bf16[8,2,48,768]{3,2,1,0:T(8,128)(2,1)S(1)}, u32[]{:S(2)}, u32[]{:S(2)}) async-start(bf16[8,2,48,768]{3,2,1,0:T(8,128)(2,1)} %pair.1), calls=%async_computation | async-start | bytes 2359296 | tf_op jit(solution)/shard_map/all_to_all | solution.py:333
  17.7 1.9 %copy-start.8 = (s32[32]{0:T(128)S(1)}, s32[32]{0:T(128)}, u32[]{:S(2)}) copy-start(s32[32]{0:T(128)} %param.9) | copy-start | bytes 388
  18.5 2.7 %collective-permute-start.1 = (f32[2,48,768]{2,1,0:T(8,128)}, f32[2,48,768]{2,1,0:T(8,128)}, u32[]{:S(2)}, u32[]{:S(2)}) collective-permute-start(f32[2,48,768]{2,1,0:T(8,128)} %get-tuple-element.79), channel_id=1, source_target_pairs={{0,16},{16,0},{1,17},{17,1},{2,18},{18,2},{3,19},{19,3},{4,20},{20... | collective-permute-start | bytes 884744 | tf_op jit(solution)/shard_map/ppermute | solution.py:30
  20.4 2.0 %collective-permute-start.4 = (bf16[2,2,48,768]{3,2,0,1:T(8,128)(2,1)S(1)}, bf16[2,2,48,768]{3,2,0,1:T(8,128)(2,1)S(1)}, u32[]{:S(2)}, u32[]{:S(2)}) collective-permute-start(bf16[2,2,48,768]{3,2,0,1:T(8,128)(2,1)S(1)} %get-tuple-element.77), channel_id=1, source_target_pairs={{0,16},{16,0},{1,17},{17,1},{2,18},{18,2},{3,19},{19,3},{4,20},{20... | collective-permute-start | bytes 884744 | tf_op jit(solution)/shard_map/ppermute | solution.py:30
  22.5 24.5 %copy-start.1 = (bf16[2,2,2,48,768]{4,3,2,1,0:T(8,128)(2,1)}, bf16[2,2,2,48,768]{4,3,2,1,0:T(8,128)(2,1)S(1)}, u32[]{:S(2)}) copy-start(bf16[2,2,2,48,768]{4,3,2,1,0:T(8,128)(2,1)S(1)} %copy.13) | copy-start | bytes 1769476
  35.2 37.6 %all-to-all-start.1 = ((bf16[16,48,768]{2,1,0:T(8,128)(2,1)}), bf16[16,48,768]{2,1,0:T(8,128)(2,1)S(1)}, u32[]{:S(2)}, u32[]{:S(2)}) async-start(bf16[16,48,768]{2,1,0:T(8,128)(2,1)} %sort.1), calls=%async_computation.1 | async-start | bytes 2359296 | tf_op jit(solution)/shard_map/all_to_all | solution.py:352
  45.1 50.0 %copy-start.2 = (f32[4,48,768]{2,1,0:T(8,128)S(1)}, f32[4,48,768]{2,1,0:T(8,128)}, u32[]{:S(2)}) copy-start(f32[4,48,768]{2,1,0:T(8,128)} %param.13) | copy-start | bytes 1769476
  45.1 28.4 %collective-permute-start.7 = (bf16[2,192,768]{2,1,0:T(8,128)(2,1)S(1)}, bf16[2,192,768]{2,1,0:T(8,128)(2,1)}, u32[]{:S(2)}, u32[]{:S(2)}) collective-permute-start(bf16[2,192,768]{2,1,0:T(8,128)(2,1)S(1)} %bitcast.10), channel_id=1, source_target_pairs={{0,128},{64,192},{128,0},{192,64},{1,129},{65,193},{129,1},{193,65... | collective-permute-start | bytes 1769480 | tf_op jit(solution)/shard_map/ppermute | solution.py:30
  46.0 27.4 %collective-permute-start.6 = (bf16[2,192,768]{2,1,0:T(8,128)(2,1)S(1)}, bf16[2,192,768]{2,1,0:T(8,128)(2,1)}, u32[]{:S(2)}, u32[]{:S(2)}) collective-permute-start(bf16[2,192,768]{2,1,0:T(8,128)(2,1)S(1)} %bitcast.11), channel_id=1, source_target_pairs={{0,192},{64,0},{128,64},{192,128},{1,193},{65,1},{129,65},{193,129... | collective-permute-start | bytes 1769480 | tf_op jit(solution)/shard_map/ppermute | solution.py:30
  46.9 27.7 %collective-permute-start.5 = (bf16[2,192,768]{2,1,0:T(8,128)(2,1)S(1)}, bf16[2,192,768]{2,1,0:T(8,128)(2,1)}, u32[]{:S(2)}, u32[]{:S(2)}) collective-permute-start(bf16[2,192,768]{2,1,0:T(8,128)(2,1)S(1)} %bitcast.12), channel_id=1, source_target_pairs={{0,64},{64,128},{128,192},{192,0},{1,65},{65,129},{129,193},{193,1... | collective-permute-start | bytes 1769480 | tf_op jit(solution)/shard_map/ppermute | solution.py:30
  74.7 3.3 %collective-permute-start.8 = (bf16[2,48,768]{2,1,0:T(8,128)(2,1)S(1)}, bf16[2,48,768]{2,1,0:T(8,128)(2,1)S(1)}, u32[]{:S(2)}, u32[]{:S(2)}) collective-permute-start(bf16[2,48,768]{2,1,0:T(8,128)(2,1)S(1)} %get-tuple-element.81), channel_id=1, source_target_pairs={{0,16},{16,0},{1,17},{17,1},{2,18},{18,2},{3,19},{19,3},{4,20},{20... | collective-permute-start | bytes 442376 | tf_op jit(solution)/shard_map/ppermute | solution.py:30
  78.1 10.3 %collective-permute-start.13 = (bf16[2,96,768]{2,1,0:T(8,128)(2,1)S(1)}, bf16[2,96,768]{2,1,0:T(8,128)(2,1)S(1)}, u32[]{:S(2)}, u32[]{:S(2)}) collective-permute-start(bf16[2,96,768]{2,1,0:T(8,128)(2,1)S(1)} %maximum_select_fusion.6.refs_0_), channel_id=1, source_target_pairs={{0,128},{64,192},{128,0},{192,64},{1,129},{65,193},{129,1},{193,65... | collective-permute-start | bytes 884744 | tf_op jit(solution)/shard_map/ppermute | solution.py:30
  81.3 7.9 %collective-permute-start.12 = (bf16[2,96,768]{2,1,0:T(8,128)(2,1)S(1)}, bf16[2,96,768]{2,1,0:T(8,128)(2,1)S(1)}, u32[]{:S(2)}, u32[]{:S(2)}) collective-permute-start(bf16[2,96,768]{2,1,0:T(8,128)(2,1)S(1)} %maximum_select_fusion.6.refs_0_), channel_id=1, source_target_pairs={{0,32},{32,0},{1,33},{33,1},{2,34},{34,2},{3,35},{35,3},{4,36},{36... | collective-permute-start | bytes 884744 | tf_op jit(solution)/shard_map/ppermute | solution.py:30
  81.3 13.8 %collective-permute-start.9 = (bf16[2,96,768]{2,1,0:T(8,128)(2,1)S(1)}, bf16[2,96,768]{2,1,0:T(8,128)(2,1)S(1)}, u32[]{:S(2)}, u32[]{:S(2)}) collective-permute-start(bf16[2,96,768]{2,1,0:T(8,128)(2,1)S(1)} %maximum_select_fusion.6.refs_0_), channel_id=1, source_target_pairs={{0,64},{64,128},{128,192},{192,0},{1,65},{65,129},{129,193},{193,1... | collective-permute-start | bytes 884744 | tf_op jit(solution)/shard_map/ppermute | solution.py:30
  83.4 14.4 %collective-permute-start.11 = (bf16[2,96,768]{2,1,0:T(8,128)(2,1)S(1)}, bf16[2,96,768]{2,1,0:T(8,128)(2,1)S(1)}, u32[]{:S(2)}, u32[]{:S(2)}) collective-permute-start(bf16[2,96,768]{2,1,0:T(8,128)(2,1)S(1)} %maximum_select_fusion.6.refs_0_), channel_id=1, source_target_pairs={{0,192},{64,0},{128,64},{192,128},{1,193},{65,1},{129,65},{193,129... | collective-permute-start | bytes 884744 | tf_op jit(solution)/shard_map/ppermute | solution.py:30
  89.2 8.6 %collective-permute-start.15 = (bf16[2,96,768]{2,1,0:T(8,128)(2,1)S(1)}, bf16[2,96,768]{2,1,0:T(8,128)(2,1)S(1)}, u32[]{:S(2)}, u32[]{:S(2)}) collective-permute-start(bf16[2,96,768]{2,1,0:T(8,128)(2,1)S(1)} %collective-permute-done.12.refs_3_), channel_id=1, source_target_pairs={{0,192},{64,0},{128,64},{192,128},{1,193},{65,1},{129,65},{193,129... | collective-permute-start | bytes 884744 | tf_op jit(solution)/shard_map/ppermute | solution.py:30
  90.5 9.7 %collective-permute-start.14 = (bf16[2,96,768]{2,1,0:T(8,128)(2,1)S(1)}, bf16[2,96,768]{2,1,0:T(8,128)(2,1)S(1)}, u32[]{:S(2)}, u32[]{:S(2)}) collective-permute-start(bf16[2,96,768]{2,1,0:T(8,128)(2,1)S(1)} %collective-permute-done.12.refs_3_), channel_id=1, source_target_pairs={{0,64},{64,128},{128,192},{192,0},{1,65},{65,129},{129,193},{193,1... | collective-permute-start | bytes 884744 | tf_op jit(solution)/shard_map/ppermute | solution.py:30
  90.7 7.1 %collective-permute-start.16 = (bf16[2,96,768]{2,1,0:T(8,128)(2,1)S(1)}, bf16[2,96,768]{2,1,0:T(8,128)(2,1)S(1)}, u32[]{:S(2)}, u32[]{:S(2)}) collective-permute-start(bf16[2,96,768]{2,1,0:T(8,128)(2,1)S(1)} %collective-permute-done.13.refs_4_), channel_id=1, source_target_pairs={{0,32},{32,0},{1,33},{33,1},{2,34},{34,2},{3,35},{35,3},{4,36},{36... | collective-permute-start | bytes 884744 | tf_op jit(solution)/shard_map/ppermute | solution.py:30
  96.3 1.4 collective-permute-start.10
  103.6 1.7 %copy-start = (f32[2,96,768]{2,1,0:T(8,128)}, f32[2,96,768]{2,1,0:T(8,128)S(1)}, u32[]{:S(2)}) copy-start(f32[2,96,768]{2,1,0:T(8,128)S(1)} %get-tuple-element.61.prec) | copy-start | bytes 1769476
  105.3 33.6 %copy-start.4 = (f32[4,48,768]{2,1,0:T(8,128)S(1)}, f32[4,48,768]{2,1,0:T(8,128)}, u32[]{:S(2)}) copy-start(f32[4,48,768]{2,1,0:T(8,128)} %param.11) | copy-start | bytes 1769476
  105.4 33.6 %copy-start.5 = (f32[4,48,768]{2,1,0:T(8,128)S(1)}, f32[4,48,768]{2,1,0:T(8,128)}, u32[]{:S(2)}) copy-start(f32[4,48,768]{2,1,0:T(8,128)} %param.12) | copy-start | bytes 1769476
  105.4 12.1 %collective-permute-start.17 = (f32[2,48,768]{2,1,0:T(8,128)S(1)}, f32[2,48,768]{2,1,0:T(8,128)S(1)}, u32[]{:S(2)}, u32[]{:S(2)}) collective-permute-start(f32[2,48,768]{2,1,0:T(8,128)S(1)} %get-tuple-element.57), channel_id=1, source_target_pairs={{0,16},{16,0},{1,17},{17,1},{2,18},{18,2},{3,19},{19,3},{4,20},{20... | collective-permute-start | bytes 884744 | tf_op jit(solution)/shard_map/ppermute | solution.py:30
  107.1 10.4 %collective-permute-start.18 = (f32[2,48,768]{2,1,0:T(8,128)S(1)}, f32[2,48,768]{2,1,0:T(8,128)S(1)}, u32[]{:S(2)}, u32[]{:S(2)}) collective-permute-start(f32[2,48,768]{2,1,0:T(8,128)S(1)} %get-tuple-element.58), channel_id=1, source_target_pairs={{0,16},{16,0},{1,17},{17,1},{2,18},{18,2},{3,19},{19,3},{4,20},{20... | collective-permute-start | bytes 884744 | tf_op jit(solution)/shard_map/ppermute | solution.py:30
  118.8 8.2 %collective-permute-start.22 = (bf16[2,96,768]{2,1,0:T(8,128)(2,1)S(1)}, bf16[2,96,768]{2,1,0:T(8,128)(2,1)S(1)}, u32[]{:S(2)}, u32[]{:S(2)}) collective-permute-start(bf16[2,96,768]{2,1,0:T(8,128)(2,1)S(1)} %fresh.1.refs_0_), channel_id=1, source_target_pairs={{0,128},{64,192},{128,0},{192,64},{1,129},{65,193},{129,1},{193,65... | collective-permute-start | bytes 884744 | tf_op jit(solution)/shard_map/ppermute | solution.py:30
  119.8 7.6 %collective-permute-start.21 = (bf16[2,96,768]{2,1,0:T(8,128)(2,1)S(1)}, bf16[2,96,768]{2,1,0:T(8,128)(2,1)S(1)}, u32[]{:S(2)}, u32[]{:S(2)}) collective-permute-start(bf16[2,96,768]{2,1,0:T(8,128)(2,1)S(1)} %fresh.1.refs_0_), channel_id=1, source_target_pairs={{0,32},{32,0},{1,33},{33,1},{2,34},{34,2},{3,35},{35,3},{4,36},{36... | collective-permute-start | bytes 884744 | tf_op jit(solution)/shard_map/ppermute | solution.py:30
  120.1 12.7 %collective-permute-start.20 = (bf16[2,96,768]{2,1,0:T(8,128)(2,1)S(1)}, bf16[2,96,768]{2,1,0:T(8,128)(2,1)S(1)}, u32[]{:S(2)}, u32[]{:S(2)}) collective-permute-start(bf16[2,96,768]{2,1,0:T(8,128)(2,1)S(1)} %fresh.1.refs_0_), channel_id=1, source_target_pairs={{0,192},{64,0},{128,64},{192,128},{1,193},{65,1},{129,65},{193,129... | collective-permute-start | bytes 884744 | tf_op jit(solution)/shard_map/ppermute | solution.py:30
  121.9 12.9 %collective-permute-start.19 = (bf16[2,96,768]{2,1,0:T(8,128)(2,1)S(1)}, bf16[2,96,768]{2,1,0:T(8,128)(2,1)S(1)}, u32[]{:S(2)}, u32[]{:S(2)}) collective-permute-start(bf16[2,96,768]{2,1,0:T(8,128)(2,1)S(1)} %fresh.1.refs_0_), channel_id=1, source_target_pairs={{0,64},{64,128},{128,192},{192,0},{1,65},{65,129},{129,193},{193,1... | collective-permute-start | bytes 884744 | tf_op jit(solution)/shard_map/ppermute | solution.py:30
  127.1 10.1 %collective-permute-start.25 = (bf16[2,96,768]{2,1,0:T(8,128)(2,1)S(1)}, bf16[2,96,768]{2,1,0:T(8,128)(2,1)S(1)}, u32[]{:S(2)}, u32[]{:S(2)}) collective-permute-start(bf16[2,96,768]{2,1,0:T(8,128)(2,1)S(1)} %collective-permute-done.22.refs_4_), channel_id=1, source_target_pairs={{0,32},{32,0},{1,33},{33,1},{2,34},{34,2},{3,35},{35,3},{4,36},{36... | collective-permute-start | bytes 884744 | tf_op jit(solution)/shard_map/ppermute | solution.py:30
  127.4 12.7 %collective-permute-start.24 = (bf16[2,96,768]{2,1,0:T(8,128)(2,1)S(1)}, bf16[2,96,768]{2,1,0:T(8,128)(2,1)S(1)}, u32[]{:S(2)}, u32[]{:S(2)}) collective-permute-start(bf16[2,96,768]{2,1,0:T(8,128)(2,1)S(1)} %collective-permute-done.21.refs_3_), channel_id=1, source_target_pairs={{0,192},{64,0},{128,64},{192,128},{1,193},{65,1},{129,65},{193,129... | collective-permute-start | bytes 884744 | tf_op jit(solution)/shard_map/ppermute | solution.py:30
  134.8 7.4 %collective-permute-start.23 = (bf16[2,96,768]{2,1,0:T(8,128)(2,1)S(1)}, bf16[2,96,768]{2,1,0:T(8,128)(2,1)S(1)}, u32[]{:S(2)}, u32[]{:S(2)}) collective-permute-start(bf16[2,96,768]{2,1,0:T(8,128)(2,1)S(1)} %collective-permute-done.21.refs_3_), channel_id=1, source_target_pairs={{0,64},{64,128},{128,192},{192,0},{1,65},{65,129},{129,193},{193,1... | collective-permute-start | bytes 884744 | tf_op jit(solution)/shard_map/ppermute | solution.py:30
  135.9 9.5 %collective-permute-start.26 = (bf16[2,96,768]{2,1,0:T(8,128)(2,1)S(1)}, bf16[2,96,768]{2,1,0:T(8,128)(2,1)S(1)}, u32[]{:S(2)}, u32[]{:S(2)}) collective-permute-start(bf16[2,96,768]{2,1,0:T(8,128)(2,1)S(1)} %fresh.1.refs_0_), channel_id=1, source_target_pairs={{0,16},{16,0},{1,17},{17,1},{2,18},{18,2},{3,19},{19,3},{4,20},{20... | collective-permute-start | bytes 884744 | tf_op jit(solution)/shard_map/ppermute | solution.py:30
  137.1 8.3 %collective-permute-start.27 = (bf16[2,96,768]{2,1,0:T(8,128)(2,1)S(1)}, bf16[2,96,768]{2,1,0:T(8,128)(2,1)S(1)}, u32[]{:S(2)}, u32[]{:S(2)}) collective-permute-start(bf16[2,96,768]{2,1,0:T(8,128)(2,1)S(1)} %collective-permute-done.19.refs_1_), channel_id=1, source_target_pairs={{0,16},{16,0},{1,17},{17,1},{2,18},{18,2},{3,19},{19,3},{4,20},{20... | collective-permute-start | bytes 884744 | tf_op jit(solution)/shard_map/ppermute | solution.py:30
  137.2 8.8 %collective-permute-start.28 = (bf16[2,96,768]{2,1,0:T(8,128)(2,1)S(1)}, bf16[2,96,768]{2,1,0:T(8,128)(2,1)S(1)}, u32[]{:S(2)}, u32[]{:S(2)}) collective-permute-start(bf16[2,96,768]{2,1,0:T(8,128)(2,1)S(1)} %collective-permute-done.20.refs_2_), channel_id=1, source_target_pairs={{0,16},{16,0},{1,17},{17,1},{2,18},{18,2},{3,19},{19,3},{4,20},{20... | collective-permute-start | bytes 884744 | tf_op jit(solution)/shard_map/ppermute | solution.py:30
  140.1 5.9 %collective-permute-start.29 = (bf16[2,96,768]{2,1,0:T(8,128)(2,1)S(1)}, bf16[2,96,768]{2,1,0:T(8,128)(2,1)S(1)}, u32[]{:S(2)}, u32[]{:S(2)}) collective-permute-start(bf16[2,96,768]{2,1,0:T(8,128)(2,1)S(1)} %collective-permute-done.21.refs_3_), channel_id=1, source_target_pairs={{0,16},{16,0},{1,17},{17,1},{2,18},{18,2},{3,19},{19,3},{4,20},{20... | collective-permute-start | bytes 884744 | tf_op jit(solution)/shard_map/ppermute | solution.py:30
  142.2 4.4 %collective-permute-start.30 = (bf16[2,96,768]{2,1,0:T(8,128)(2,1)S(1)}, bf16[2,96,768]{2,1,0:T(8,128)(2,1)S(1)}, u32[]{:S(2)}, u32[]{:S(2)}) collective-permute-start(bf16[2,96,768]{2,1,0:T(8,128)(2,1)S(1)} %collective-permute-done.22.refs_4_), channel_id=1, source_target_pairs={{0,16},{16,0},{1,17},{17,1},{2,18},{18,2},{3,19},{19,3},{4,20},{20... | collective-permute-start | bytes 884744 | tf_op jit(solution)/shard_map/ppermute | solution.py:30
  145.4 1.6 %collective-permute-start.32 = (bf16[2,96,768]{2,1,0:T(8,128)(2,1)S(1)}, bf16[2,96,768]{2,1,0:T(8,128)(2,1)S(1)}, u32[]{:S(2)}, u32[]{:S(2)}) collective-permute-start(bf16[2,96,768]{2,1,0:T(8,128)(2,1)S(1)} %collective-permute-done.24.refs_6_), channel_id=1, source_target_pairs={{0,16},{16,0},{1,17},{17,1},{2,18},{18,2},{3,19},{19,3},{4,20},{20... | collective-permute-start | bytes 884744 | tf_op jit(solution)/shard_map/ppermute | solution.py:30
  145.4 2.0 %collective-permute-start.31 = (bf16[2,96,768]{2,1,0:T(8,128)(2,1)S(1)}, bf16[2,96,768]{2,1,0:T(8,128)(2,1)S(1)}, u32[]{:S(2)}, u32[]{:S(2)}) collective-permute-start(bf16[2,96,768]{2,1,0:T(8,128)(2,1)S(1)} %collective-permute-done.23.refs_5_), channel_id=1, source_target_pairs={{0,16},{16,0},{1,17},{17,1},{2,18},{18,2},{3,19},{19,3},{4,20},{20... | collective-permute-start | bytes 884744 | tf_op jit(solution)/shard_map/ppermute | solution.py:30
  145.9 2.0 %collective-permute-start.33 = (bf16[2,96,768]{2,1,0:T(8,128)(2,1)S(1)}, bf16[2,96,768]{2,1,0:T(8,128)(2,1)S(1)}, u32[]{:S(2)}, u32[]{:S(2)}) collective-permute-start(bf16[2,96,768]{2,1,0:T(8,128)(2,1)S(1)} %collective-permute-done.25.refs_7_), channel_id=1, source_target_pairs={{0,16},{16,0},{1,17},{17,1},{2,18},{18,2},{3,19},{19,3},{4,20},{20... | collective-permute-start | bytes 884744 | tf_op jit(solution)/shard_map/ppermute | solution.py:30

commit v3 on v2

--- a/solution.py
+++ b/solution.py
@@ -36,10 +36,9 @@
 core_swap = shift("core", CORE, 1)
 
 
-def gather_chips(mine, together):
+def gather_chips(mine):
     back, ahead, other, far = y_up(mine), y_down(mine), z_swap(mine), y_two(mine)
-    if together:
-        other, far = lax.optimization_barrier((other, far))
+    other, far = lax.optimization_barrier((other, far))
     return [mine, back, ahead, other, far, y_up(other), y_down(other), z_swap(far)]
 
 
@@ -354,7 +353,7 @@
     mine = pick_call(held, came)
     mine, r_all = lax.optimization_barrier((mine, r_all))
 
-    g_all = gather_chips(to_chip_rows(mine), True)
+    g_all = gather_chips(to_chip_rows(mine))
 
     mine, _ = lax.optimization_barrier((mine, g_all[1]))
     grad32 = mine.astype(F32)
@@ -371,7 +370,7 @@
     precond = pltpu.with_memory_space_constraint(precond, pltpu.HBM)
     fresh = fresh_call(sums, weights2, precond)
 
-    n_all = gather_chips(fresh, False)
+    n_all = gather_chips(fresh)
     n_all[:5] = lax.optimization_barrier(n_all[:5])
     new_left = 0.5 * stat_left + 0.5 * join_slots(lkeep, lcame)
     new_right = 0.5 * stat_right + 0.5 * join_slots(rkeep, rcame)

time: 151 us -> 148 us (0.980)
  waiting for transfers between devices: 69.9 us -> 68.1 us
    ppermute x34, waiting for transfers between devices: 33.6 us -> 31.9 us  [shift(): return lambda value: lax.ppermute(value, axis, pairs)]
  transfers between devices with their start and end apart: 36 -> 36, of which waited for: 20 -> 19; matrix products, arithmetic and copies ran while one was open for 4% -> 4% of each run, Pallas kernels for 2% -> 2%
where the time goes in v3:
time: 148 us; the launch traced here: 147 us
  waiting for transfers between devices  68.1 us (46%)
  starting transfers between devices  47 us (32%)
  Pallas kernels  14.9 us (10%)
  blocking collectives  10.3 us (7%)
  other arithmetic  4.25 us (3%)
  local copies, waits for them, and re-layouts  1.76 us (1%)
    ppermute x34, starting transfers between devices, shift(): return lambda value: lax.ppermute(value, axis, pairs)  33.3 us
    ppermute x34, waiting for transfers between devices, shift(): return lambda value: lax.ppermute(value, axis, pairs)  31.9 us
    all_to_all x1, waiting for transfers between devices, on_device(): came = lax.all_to_all(sends, ('x', 'zh'), 0, 0, tiled=True)  25.3 us
    all_to_all x1, waiting for transfers between devices, on_device(): parts = lax.all_to_all(chip, ('y', 'zl'), 0, 0, tiled=True)  10.9 us
    all_to_all x1, blocking collectives, on_device(): sums = lax.all_to_all(sums, ('y', 'zl'), 0, 0, tiled=True)  10.3 us
    all_to_all x1, starting transfers between devices, on_device(): came = lax.all_to_all(sends, ('x', 'zh'), 0, 0, tiled=True)  9.85 us
    all_to_all x1, starting transfers between devices, on_device(): parts = lax.all_to_all(chip, ('y', 'zl'), 0, 0, tiled=True)  3.81 us
    pallas_call x1, Pallas kernels, precond_call(): pl.pallas_call(precond_body, in_specs=[SM, SM] + [VM] * (1 + CHIPS) + [AN...  3.36 us
  transfers between devices with their start and end apart: 36, of which 19 were waited for; matrix products, arithmetic and copies ran while one was open for 4% of the time, Pallas kernels for 2%

profile of v3, /device:TPU:1, one launch (start us, length us, event | category | flops | bytes accessed | tf_op | source)
XLA Modules:
  0.0 147.4 jit_solution(9672459621630677086)
XLA Ops:
  0.7 1.3 give.1
  2.0 3.3 %collective-permute-start.2 = (bf16[8,2,48,768]{3,2,1,0:T(8,128)(2,1)S(1)}, bf16[8,2,48,768]{3,2,1,0:T(8,128)(2,1)S(1)}, u32[]{:S(2)}, u32[]{:S(2)}) collective-permute-start(bf16[8,2,48,768]{3,2,1,0:T(8,128)(2,1)S(1)} %give.1), channel_id=1, source_target_pairs={{0,16},{16,0},{1,17},{17,1},{2,18},{18,2},{3,19},{19,3},{4,20},{20... | collective-permute-start | bytes 3538952 | tf_op jit(solution)/shard_map/ppermute | solution.py:30
  5.3 0.7 constant_dynamic-slice_fusion.6
  6.0 0.3 collective-permute-start
  6.3 1.3 keep.1
  7.6 0.2 collective-permute-done.2.came
  7.8 1.3 pair.1
  9.1 4.8 %collective-permute-done.3 = bf16[4,48,768]{2,1,0:T(8,128)(2,1)S(1)} collective-permute-done((bf16[4,48,768]{2,1,0:T(8,128)(2,1)S(1)}, bf16[4,48,768]{2,1,0:T(8,128)(2,1)S(1)}, u32[]{:S(2)}, u32[]{:S(2)}) %collective-permute-start.3) | collective-permute-done | bytes 294944 | tf_op jit(solution)/shard_map/ppermute | solution.py:30
  13.9 3.8 %all-to-all-start = ((bf16[8,2,48,768]{3,2,1,0:T(8,128)(2,1)}), bf16[8,2,48,768]{3,2,1,0:T(8,128)(2,1)S(1)}, u32[]{:S(2)}, u32[]{:S(2)}) async-start(bf16[8,2,48,768]{3,2,1,0:T(8,128)(2,1)} %pair.1), calls=%async_computation | async-start | bytes 2359296 | tf_op jit(solution)/shard_map/all_to_all | solution.py:332
  17.7 0.8 constant_dynamic-slice_fusion.4
  18.5 1.2 collective-permute-start.1
  19.7 0.2 convert_reduce_fusion
  19.9 0.2 select_reduce_fusion
  20.5 0.7 collective-permute-done.1
  21.2 1.1 maximum_select_fusion.weights
  22.5 10.9 %all-to-all-done.parts = bf16[8,2,48,768]{3,2,1,0:T(8,128)(2,1)S(1)} async-done(((bf16[8,2,48,768]{3,2,1,0:T(8,128)(2,1)}), bf16[8,2,48,768]{3,2,1,0:T(8,128)(2,1)S(1)}, u32[]{:S(2)}, u32[]{:S(2)}) %all-to-all-start) | async-done | bytes 1179680 | tf_op jit(solution)/shard_map/all_to_all | solution.py:332
  33.4 1.8 %sort.1 = bf16[16,48,768]{2,1,0:T(8,128)(2,1)} custom-call(s32[16]{0:T(128)S(1)} %maximum_add_fusion.table, bf16[8,2,48,768]{3,2,1,0:T(8,128)(2,1)S(1)} %all-to-all-done.parts), custom_call_target="tpu_custom_call" | custom-call | tf_op jit(solution)/shard_map/sort/pallas_call | solution.py:227
  35.2 9.9 %all-to-all-start.1 = ((bf16[16,48,768]{2,1,0:T(8,128)(2,1)}), bf16[16,48,768]{2,1,0:T(8,128)(2,1)S(1)}, u32[]{:S(2)}, u32[]{:S(2)}) async-start(bf16[16,48,768]{2,1,0:T(8,128)(2,1)} %sort.1), calls=%async_computation.1 | async-start | bytes 2359296 | tf_op jit(solution)/shard_map/all_to_all | solution.py:351
  45.1 1.0 collective-permute-start.7
  46.0 0.9 collective-permute-start.6
  46.9 0.6 collective-permute-start.5
  47.5 25.3 %all-to-all-done.1.blocks = bf16[16,48,768]{2,1,0:T(8,128)(2,1)S(1)} async-done(((bf16[16,48,768]{2,1,0:T(8,128)(2,1)}), bf16[16,48,768]{2,1,0:T(8,128)(2,1)S(1)}, u32[]{:S(2)}, u32[]{:S(2)}) %all-to-all-start.1) | async-done | bytes 1179680 | tf_op jit(solution)/shard_map/all_to_all | solution.py:351
  72.8 0.6 pick.1
  73.5 1.2 collective-permute-done.5.refs_9_
  74.7 2.3 %collective-permute-start.8 = (bf16[2,48,768]{2,1,0:T(8,128)(2,1)S(1)}, bf16[2,48,768]{2,1,0:T(8,128)(2,1)S(1)}, u32[]{:S(2)}, u32[]{:S(2)}) collective-permute-start(bf16[2,48,768]{2,1,0:T(8,128)(2,1)S(1)} %get-tuple-element.85), channel_id=1, source_target_pairs={{0,16},{16,0},{1,17},{17,1},{2,18},{18,2},{3,19},{19,3},{4,20},{20... | collective-permute-start | bytes 442376 | tf_op jit(solution)/shard_map/ppermute | solution.py:30
  77.0 1.0 collective-permute-done.8
  78.1 3.2 %collective-permute-start.13 = (bf16[2,96,768]{2,1,0:T(8,128)(2,1)S(1)}, bf16[2,96,768]{2,1,0:T(8,128)(2,1)S(1)}, u32[]{:S(2)}, u32[]{:S(2)}) collective-permute-start(bf16[2,96,768]{2,1,0:T(8,128)(2,1)S(1)} %maximum_select_fusion.6.refs_0_), channel_id=1, source_target_pairs={{0,128},{64,192},{128,0},{192,64},{1,129},{65,193},{129,1},{193,65... | collective-permute-start | bytes 884744 | tf_op jit(solution)/shard_map/ppermute | solution.py:30
  81.3 2.1 %collective-permute-start.9 = (bf16[2,96,768]{2,1,0:T(8,128)(2,1)S(1)}, bf16[2,96,768]{2,1,0:T(8,128)(2,1)S(1)}, u32[]{:S(2)}, u32[]{:S(2)}) collective-permute-start(bf16[2,96,768]{2,1,0:T(8,128)(2,1)S(1)} %maximum_select_fusion.6.refs_0_), channel_id=1, source_target_pairs={{0,64},{64,128},{128,192},{192,0},{1,65},{65,129},{129,193},{193,1... | collective-permute-start | bytes 884744 | tf_op jit(solution)/shard_map/ppermute | solution.py:30
  83.4 0.6 collective-permute-start.11
  84.0 4.3 %collective-permute-done.13.refs_4_ = bf16[2,96,768]{2,1,0:T(8,128)(2,1)S(1)} collective-permute-done((bf16[2,96,768]{2,1,0:T(8,128)(2,1)S(1)}, bf16[2,96,768]{2,1,0:T(8,128)(2,1)S(1)}, u32[]{:S(2)}, u32[]{:S(2)}) %collective-permute-start.13) | collective-permute-done | bytes 294944 | tf_op jit(solution)/shard_map/ppermute | solution.py:30
  88.3 0.9 collective-permute-done.12.refs_3_
  89.2 1.3 collective-permute-start.15
  90.5 0.2 collective-permute-start.14
  90.7 1.9 %collective-permute-start.16 = (bf16[2,96,768]{2,1,0:T(8,128)(2,1)S(1)}, bf16[2,96,768]{2,1,0:T(8,128)(2,1)S(1)}, u32[]{:S(2)}, u32[]{:S(2)}) collective-permute-start(bf16[2,96,768]{2,1,0:T(8,128)(2,1)S(1)} %collective-permute-done.13.refs_4_), channel_id=1, source_target_pairs={{0,32},{32,0},{1,33},{33,1},{2,34},{34,2},{3,35},{35,3},{4,36},{36... | collective-permute-start | bytes 884744 | tf_op jit(solution)/shard_map/ppermute | solution.py:30
  92.6 2.5 %collective-permute-done.9.refs_1_ = bf16[2,96,768]{2,1,0:T(8,128)(2,1)S(1)} collective-permute-done((bf16[2,96,768]{2,1,0:T(8,128)(2,1)S(1)}, bf16[2,96,768]{2,1,0:T(8,128)(2,1)S(1)}, u32[]{:S(2)}, u32[]{:S(2)}) %collective-permute-start.9) | collective-permute-done | bytes 294944 | tf_op jit(solution)/shard_map/ppermute | solution.py:30
  95.1 1.1 fusion.6
  96.3 0.6 collective-permute-start.10
  96.9 0.8 collective-permute-done.10
  97.8 2.4 %collective-permute-done.14.refs_5_ = bf16[2,96,768]{2,1,0:T(8,128)(2,1)S(1)} collective-permute-done((bf16[2,96,768]{2,1,0:T(8,128)(2,1)S(1)}, bf16[2,96,768]{2,1,0:T(8,128)(2,1)S(1)}, u32[]{:S(2)}, u32[]{:S(2)}) %collective-permute-start.14) | collective-permute-done | bytes 294944 | tf_op jit(solution)/shard_map/ppermute | solution.py:30
  100.3 3.4 %precond.1 = (f32[2,96,768]{2,1,0:T(8,128)S(1)}, f32[8,1,128]{2,1,0:T(1,128)S(1)}, bf16[2,768,768]{2,1,0:T(8,128)(2,1)S(1)}) custom-call(s32[1]{0:T(128)} %bitcast.at_dp, f32[2]{0:T(128)S(1)} %dynamic-slice_add_fusion.adam_sq, bf16[2,96,768]{2,1,0:T(8,128)(2,1)S(1)} %maximum_select_fusion.5.left, bf16[2,96,768]{2,1,0:T(8,128)(2,1)S(1)} %maximum_select_fusion.6.refs_0_, ...), custom_call_target="tpu_custom_call" | custom-call | tf_op jit(solution)/shard_map/precond/pallas_call | solution.py:138
  103.7 1.7 %stats.1 = (f32[2,48,768]{2,1,0:T(8,128)S(1)}, f32[2,48,768]{2,1,0:T(8,128)S(1)}, f32[2,48,768]{2,1,0:T(8,128)S(1)}, f32[2,48,768]{2,1,0:T(8,128)S(1)}) custom-call(s32[1]{0:T(128)} %bitcast.at_dp, bf16[2,768,768]{2,1,0:T(8,128)(2,1)S(1)} %get-tuple-element.58.g), custom_call_target="tpu_custom_call" | custom-call | tf_op jit(solution)/shard_map/stats/pallas_call | solution.py:181
  105.4 1.7 %collective-permute-start.17 = (f32[2,48,768]{2,1,0:T(8,128)S(1)}, f32[2,48,768]{2,1,0:T(8,128)S(1)}, u32[]{:S(2)}, u32[]{:S(2)}) collective-permute-start(f32[2,48,768]{2,1,0:T(8,128)S(1)} %get-tuple-element.59), channel_id=1, source_target_pairs={{0,16},{16,0},{1,17},{17,1},{2,18},{18,2},{3,19},{19,3},{4,20},{20... | collective-permute-start | bytes 884744 | tf_op jit(solution)/shard_map/ppermute | solution.py:30
  107.2 10.3 %all_to_all.15.sums = f32[8,1,128]{2,1,0:T(1,128)S(1)} all-to-all(f32[8,1,128]{2,1,0:T(1,128)S(1)} %get-tuple-element.57), channel_id=1, replica_groups=mesh['y'=4,'zl'=2,'core'=2,'x'=4,'zh'=4] {'y','zl'}, dimensions={0} | all-to-all | bytes 8192 | tf_op jit(solution)/shard_map/all_to_all | solution.py:366
  117.5 1.3 fresh.1.refs_0_
  118.8 1.0 collective-permute-start.22
  119.8 0.3 collective-permute-start.21
  120.1 1.8 %collective-permute-start.20 = (bf16[2,96,768]{2,1,0:T(8,128)(2,1)S(1)}, bf16[2,96,768]{2,1,0:T(8,128)(2,1)S(1)}, u32[]{:S(2)}, u32[]{:S(2)}) collective-permute-start(bf16[2,96,768]{2,1,0:T(8,128)(2,1)S(1)} %fresh.1.refs_0_), channel_id=1, source_target_pairs={{0,192},{64,0},{128,64},{192,128},{1,193},{65,1},{129,65},{193,129... | collective-permute-start | bytes 884744 | tf_op jit(solution)/shard_map/ppermute | solution.py:30
  121.9 5.2 %collective-permute-done.22.refs_4_ = bf16[2,96,768]{2,1,0:T(8,128)(2,1)S(1)} collective-permute-done((bf16[2,96,768]{2,1,0:T(8,128)(2,1)S(1)}, bf16[2,96,768]{2,1,0:T(8,128)(2,1)S(1)}, u32[]{:S(2)}, u32[]{:S(2)}) %collective-permute-start.22) | collective-permute-done | bytes 294944 | tf_op jit(solution)/shard_map/ppermute | solution.py:30
  127.1 0.3 collective-permute-start.25
  127.4 0.9 collective-permute-start.24
  128.3 0.6 collective-permute-start.23
  128.8 4.0 %collective-permute-done.20.refs_2_ = bf16[2,96,768]{2,1,0:T(8,128)(2,1)S(1)} collective-permute-done((bf16[2,96,768]{2,1,0:T(8,128)(2,1)S(1)}, bf16[2,96,768]{2,1,0:T(8,128)(2,1)S(1)}, u32[]{:S(2)}, u32[]{:S(2)}) %collective-permute-start.20) | collective-permute-done | bytes 294944 | tf_op jit(solution)/shard_map/ppermute | solution.py:30
  132.8 2.0 %collective-permute-done.19.refs_1_ = bf16[2,96,768]{2,1,0:T(8,128)(2,1)S(1)} collective-permute-done((bf16[2,96,768]{2,1,0:T(8,128)(2,1)S(1)}, bf16[2,96,768]{2,1,0:T(8,128)(2,1)S(1)}, u32[]{:S(2)}, u32[]{:S(2)}) %collective-permute-start.19) | collective-permute-done | bytes 294944 | tf_op jit(solution)/shard_map/ppermute | solution.py:30
  134.8 2.4 %collective-permute-start.26 = (bf16[2,96,768]{2,1,0:T(8,128)(2,1)S(1)}, bf16[2,96,768]{2,1,0:T(8,128)(2,1)S(1)}, u32[]{:S(2)}, u32[]{:S(2)}) collective-permute-start(bf16[2,96,768]{2,1,0:T(8,128)(2,1)S(1)} %fresh.1.refs_0_), channel_id=1, source_target_pairs={{0,16},{16,0},{1,17},{17,1},{2,18},{18,2},{3,19},{19,3},{4,20},{20... | collective-permute-start | bytes 884744 | tf_op jit(solution)/shard_map/ppermute | solution.py:30
  137.2 1.8 %collective-permute-start.28 = (bf16[2,96,768]{2,1,0:T(8,128)(2,1)S(1)}, bf16[2,96,768]{2,1,0:T(8,128)(2,1)S(1)}, u32[]{:S(2)}, u32[]{:S(2)}) collective-permute-start(bf16[2,96,768]{2,1,0:T(8,128)(2,1)S(1)} %collective-permute-done.20.refs_2_), channel_id=1, source_target_pairs={{0,16},{16,0},{1,17},{17,1},{2,18},{18,2},{3,19},{19,3},{4,20},{20... | collective-permute-start | bytes 884744 | tf_op jit(solution)/shard_map/ppermute | solution.py:30
  138.9 1.1 fusion.3
  140.1 0.9 collective-permute-start.29
  141.0 1.5 collective-permute-start.30
  142.5 0.5 collective-permute-start.31
  143.1 0.6 collective-permute-done.30.refs_12_
  143.7 0.4 collective-permute-done.32.refs_14_
  144.1 0.4 collective-permute-done.31.refs_13_
  144.5 0.4 collective-permute-done.33.refs_15_
  144.9 2.3 %assemble.1 = bf16[4,768,768]{2,1,0:T(8,128)(2,1)} custom-call(s32[1]{0:T(128)} %bitcast.at_dp, bf16[2,96,768]{2,1,0:T(8,128)(2,1)S(1)} %fresh.1.refs_0_, bf16[2,96,768]{2,1,0:T(8,128)(2,1)S(1)} %collective-permute-done.19.refs_1_, bf16[2,96,768]{2,1,0:T(8,128)(2,1)S(1)} %collective-permute-done.20.refs_2_, ...), custom_call_target="tpu_custom_call" | custom-call | tf_op jit(solution)/shard_map/assemble/pallas_call | solution.py:276
  (60 shorter events, 1.1 us)
Async XLA Ops:
  0.6 4.7 %copy-start.7 = (bf16[4,48,768]{2,1,0:T(8,128)(2,1)S(1)}, bf16[4,48,768]{2,1,0:T(8,128)(2,1)}, u32[]{:S(2)}) copy-start(bf16[4,48,768]{2,1,0:T(8,128)(2,1)} %param.15) | copy-start | bytes 884740
  0.7 4.7 %copy-start.6 = (bf16[4,48,768]{2,1,0:T(8,128)(2,1)S(1)}, bf16[4,48,768]{2,1,0:T(8,128)(2,1)}, u32[]{:S(2)}) copy-start(bf16[4,48,768]{2,1,0:T(8,128)(2,1)} %param.14) | copy-start | bytes 884740
  2.0 5.8 %collective-permute-start.2 = (bf16[8,2,48,768]{3,2,1,0:T(8,128)(2,1)S(1)}, bf16[8,2,48,768]{3,2,1,0:T(8,128)(2,1)S(1)}, u32[]{:S(2)}, u32[]{:S(2)}) collective-permute-start(bf16[8,2,48,768]{3,2,1,0:T(8,128)(2,1)S(1)} %give.1), channel_id=1, source_target_pairs={{0,16},{16,0},{1,17},{17,1},{2,18},{18,2},{3,19},{19,3},{4,20},{20... | collective-permute-start | bytes 3538952 | tf_op jit(solution)/shard_map/ppermute | solution.py:30
  5.3 8.6 %collective-permute-start.3 = (bf16[4,48,768]{2,1,0:T(8,128)(2,1)S(1)}, bf16[4,48,768]{2,1,0:T(8,128)(2,1)S(1)}, u32[]{:S(2)}, u32[]{:S(2)}) collective-permute-start(bf16[4,48,768]{2,1,0:T(8,128)(2,1)S(1)} %copy-done.7), channel_id=1, source_target_pairs={{0,32},{32,0},{1,33},{33,1},{2,34},{34,2},{3,35},{35,3},{4,36},{36... | collective-permute-start | bytes 884744 | tf_op jit(solution)/shard_map/ppermute | solution.py:30
  6.0 14.5 %collective-permute-start = (bf16[2,48,768]{2,1,0:T(8,128)(2,1)}, bf16[2,48,768]{2,1,0:T(8,128)(2,1)S(1)}, u32[]{:S(2)}, u32[]{:S(2)}) collective-permute-start(bf16[2,48,768]{2,1,0:T(8,128)(2,1)} %get-tuple-element.87), channel_id=1, source_target_pairs={{0,16},{16,0},{1,17},{17,1},{2,18},{18,2},{3,19},{19,3},{4,20},{20... | collective-permute-start | bytes 442376 | tf_op jit(solution)/shard_map/ppermute | solution.py:30
  9.1 8.6 %copy-start.3 = (f32[4,48,768]{2,1,0:T(8,128)S(1)}, f32[4,48,768]{2,1,0:T(8,128)}, u32[]{:S(2)}) copy-start(f32[4,48,768]{2,1,0:T(8,128)} %param.10) | copy-start | bytes 1769476
  13.9 19.5 %all-to-all-start = ((bf16[8,2,48,768]{3,2,1,0:T(8,128)(2,1)}), bf16[8,2,48,768]{3,2,1,0:T(8,128)(2,1)S(1)}, u32[]{:S(2)}, u32[]{:S(2)}) async-start(bf16[8,2,48,768]{3,2,1,0:T(8,128)(2,1)} %pair.1), calls=%async_computation | async-start | bytes 2359296 | tf_op jit(solution)/shard_map/all_to_all | solution.py:332
  17.7 1.9 %copy-start.8 = (s32[32]{0:T(128)S(1)}, s32[32]{0:T(128)}, u32[]{:S(2)}) copy-start(s32[32]{0:T(128)} %param.9) | copy-start | bytes 388
  18.5 2.7 %collective-permute-start.1 = (f32[2,48,768]{2,1,0:T(8,128)}, f32[2,48,768]{2,1,0:T(8,128)}, u32[]{:S(2)}, u32[]{:S(2)}) collective-permute-start(f32[2,48,768]{2,1,0:T(8,128)} %get-tuple-element.83), channel_id=1, source_target_pairs={{0,16},{16,0},{1,17},{17,1},{2,18},{18,2},{3,19},{19,3},{4,20},{20... | collective-permute-start | bytes 884744 | tf_op jit(solution)/shard_map/ppermute | solution.py:30
  20.4 2.0 %collective-permute-start.4 = (bf16[2,2,48,768]{3,2,0,1:T(8,128)(2,1)S(1)}, bf16[2,2,48,768]{3,2,0,1:T(8,128)(2,1)S(1)}, u32[]{:S(2)}, u32[]{:S(2)}) collective-permute-start(bf16[2,2,48,768]{3,2,0,1:T(8,128)(2,1)S(1)} %get-tuple-element.81), channel_id=1, source_target_pairs={{0,16},{16,0},{1,17},{17,1},{2,18},{18,2},{3,19},{19,3},{4,20},{20... | collective-permute-start | bytes 884744 | tf_op jit(solution)/shard_map/ppermute | solution.py:30
  22.5 24.5 %copy-start.1 = (bf16[2,2,2,48,768]{4,3,2,1,0:T(8,128)(2,1)}, bf16[2,2,2,48,768]{4,3,2,1,0:T(8,128)(2,1)S(1)}, u32[]{:S(2)}) copy-start(bf16[2,2,2,48,768]{4,3,2,1,0:T(8,128)(2,1)S(1)} %copy.13) | copy-start | bytes 1769476
  35.2 37.6 %all-to-all-start.1 = ((bf16[16,48,768]{2,1,0:T(8,128)(2,1)}), bf16[16,48,768]{2,1,0:T(8,128)(2,1)S(1)}, u32[]{:S(2)}, u32[]{:S(2)}) async-start(bf16[16,48,768]{2,1,0:T(8,128)(2,1)} %sort.1), calls=%async_computation.1 | async-start | bytes 2359296 | tf_op jit(solution)/shard_map/all_to_all | solution.py:351
  45.1 50.0 %copy-start.2 = (f32[4,48,768]{2,1,0:T(8,128)S(1)}, f32[4,48,768]{2,1,0:T(8,128)}, u32[]{:S(2)}) copy-start(f32[4,48,768]{2,1,0:T(8,128)} %param.13) | copy-start | bytes 1769476
  45.1 28.4 %collective-permute-start.7 = (bf16[2,192,768]{2,1,0:T(8,128)(2,1)S(1)}, bf16[2,192,768]{2,1,0:T(8,128)(2,1)}, u32[]{:S(2)}, u32[]{:S(2)}) collective-permute-start(bf16[2,192,768]{2,1,0:T(8,128)(2,1)S(1)} %bitcast.10), channel_id=1, source_target_pairs={{0,128},{64,192},{128,0},{192,64},{1,129},{65,193},{129,1},{193,65... | collective-permute-start | bytes 1769480 | tf_op jit(solution)/shard_map/ppermute | solution.py:30
  46.0 27.4 %collective-permute-start.6 = (bf16[2,192,768]{2,1,0:T(8,128)(2,1)S(1)}, bf16[2,192,768]{2,1,0:T(8,128)(2,1)}, u32[]{:S(2)}, u32[]{:S(2)}) collective-permute-start(bf16[2,192,768]{2,1,0:T(8,128)(2,1)S(1)} %bitcast.11), channel_id=1, source_target_pairs={{0,192},{64,0},{128,64},{192,128},{1,193},{65,1},{129,65},{193,129... | collective-permute-start | bytes 1769480 | tf_op jit(solution)/shard_map/ppermute | solution.py:30
  46.9 27.7 %collective-permute-start.5 = (bf16[2,192,768]{2,1,0:T(8,128)(2,1)S(1)}, bf16[2,192,768]{2,1,0:T(8,128)(2,1)}, u32[]{:S(2)}, u32[]{:S(2)}) collective-permute-start(bf16[2,192,768]{2,1,0:T(8,128)(2,1)S(1)} %bitcast.12), channel_id=1, source_target_pairs={{0,64},{64,128},{128,192},{192,0},{1,65},{65,129},{129,193},{193,1... | collective-permute-start | bytes 1769480 | tf_op jit(solution)/shard_map/ppermute | solution.py:30
  74.7 3.3 %collective-permute-start.8 = (bf16[2,48,768]{2,1,0:T(8,128)(2,1)S(1)}, bf16[2,48,768]{2,1,0:T(8,128)(2,1)S(1)}, u32[]{:S(2)}, u32[]{:S(2)}) collective-permute-start(bf16[2,48,768]{2,1,0:T(8,128)(2,1)S(1)} %get-tuple-element.85), channel_id=1, source_target_pairs={{0,16},{16,0},{1,17},{17,1},{2,18},{18,2},{3,19},{19,3},{4,20},{20... | collective-permute-start | bytes 442376 | tf_op jit(solution)/shard_map/ppermute | solution.py:30
  78.1 10.3 %collective-permute-start.13 = (bf16[2,96,768]{2,1,0:T(8,128)(2,1)S(1)}, bf16[2,96,768]{2,1,0:T(8,128)(2,1)S(1)}, u32[]{:S(2)}, u32[]{:S(2)}) collective-permute-start(bf16[2,96,768]{2,1,0:T(8,128)(2,1)S(1)} %maximum_select_fusion.6.refs_0_), channel_id=1, source_target_pairs={{0,128},{64,192},{128,0},{192,64},{1,129},{65,193},{129,1},{193,65... | collective-permute-start | bytes 884744 | tf_op jit(solution)/shard_map/ppermute | solution.py:30
  81.3 7.9 %collective-permute-start.12 = (bf16[2,96,768]{2,1,0:T(8,128)(2,1)S(1)}, bf16[2,96,768]{2,1,0:T(8,128)(2,1)S(1)}, u32[]{:S(2)}, u32[]{:S(2)}) collective-permute-start(bf16[2,96,768]{2,1,0:T(8,128)(2,1)S(1)} %maximum_select_fusion.6.refs_0_), channel_id=1, source_target_pairs={{0,32},{32,0},{1,33},{33,1},{2,34},{34,2},{3,35},{35,3},{4,36},{36... | collective-permute-start | bytes 884744 | tf_op jit(solution)/shard_map/ppermute | solution.py:30
  81.3 13.8 %collective-permute-start.9 = (bf16[2,96,768]{2,1,0:T(8,128)(2,1)S(1)}, bf16[2,96,768]{2,1,0:T(8,128)(2,1)S(1)}, u32[]{:S(2)}, u32[]{:S(2)}) collective-permute-start(bf16[2,96,768]{2,1,0:T(8,128)(2,1)S(1)} %maximum_select_fusion.6.refs_0_), channel_id=1, source_target_pairs={{0,64},{64,128},{128,192},{192,0},{1,65},{65,129},{129,193},{193,1... | collective-permute-start | bytes 884744 | tf_op jit(solution)/shard_map/ppermute | solution.py:30
  83.4 14.4 %collective-permute-start.11 = (bf16[2,96,768]{2,1,0:T(8,128)(2,1)S(1)}, bf16[2,96,768]{2,1,0:T(8,128)(2,1)S(1)}, u32[]{:S(2)}, u32[]{:S(2)}) collective-permute-start(bf16[2,96,768]{2,1,0:T(8,128)(2,1)S(1)} %maximum_select_fusion.6.refs_0_), channel_id=1, source_target_pairs={{0,192},{64,0},{128,64},{192,128},{1,193},{65,1},{129,65},{193,129... | collective-permute-start | bytes 884744 | tf_op jit(solution)/shard_map/ppermute | solution.py:30
  89.2 8.6 %collective-permute-start.15 = (bf16[2,96,768]{2,1,0:T(8,128)(2,1)S(1)}, bf16[2,96,768]{2,1,0:T(8,128)(2,1)S(1)}, u32[]{:S(2)}, u32[]{:S(2)}) collective-permute-start(bf16[2,96,768]{2,1,0:T(8,128)(2,1)S(1)} %collective-permute-done.12.refs_3_), channel_id=1, source_target_pairs={{0,192},{64,0},{128,64},{192,128},{1,193},{65,1},{129,65},{193,129... | collective-permute-start | bytes 884744 | tf_op jit(solution)/shard_map/ppermute | solution.py:30
  90.5 9.7 %collective-permute-start.14 = (bf16[2,96,768]{2,1,0:T(8,128)(2,1)S(1)}, bf16[2,96,768]{2,1,0:T(8,128)(2,1)S(1)}, u32[]{:S(2)}, u32[]{:S(2)}) collective-permute-start(bf16[2,96,768]{2,1,0:T(8,128)(2,1)S(1)} %collective-permute-done.12.refs_3_), channel_id=1, source_target_pairs={{0,64},{64,128},{128,192},{192,0},{1,65},{65,129},{129,193},{193,1... | collective-permute-start | bytes 884744 | tf_op jit(solution)/shard_map/ppermute | solution.py:30
  90.7 7.1 %collective-permute-start.16 = (bf16[2,96,768]{2,1,0:T(8,128)(2,1)S(1)}, bf16[2,96,768]{2,1,0:T(8,128)(2,1)S(1)}, u32[]{:S(2)}, u32[]{:S(2)}) collective-permute-start(bf16[2,96,768]{2,1,0:T(8,128)(2,1)S(1)} %collective-permute-done.13.refs_4_), channel_id=1, source_target_pairs={{0,32},{32,0},{1,33},{33,1},{2,34},{34,2},{3,35},{35,3},{4,36},{36... | collective-permute-start | bytes 884744 | tf_op jit(solution)/shard_map/ppermute | solution.py:30
  96.3 1.4 collective-permute-start.10
  103.6 1.7 %copy-start = (f32[2,96,768]{2,1,0:T(8,128)}, f32[2,96,768]{2,1,0:T(8,128)S(1)}, u32[]{:S(2)}) copy-start(f32[2,96,768]{2,1,0:T(8,128)S(1)} %get-tuple-element.63.prec) | copy-start | bytes 1769476
  105.3 33.6 %copy-start.4 = (f32[4,48,768]{2,1,0:T(8,128)S(1)}, f32[4,48,768]{2,1,0:T(8,128)}, u32[]{:S(2)}) copy-start(f32[4,48,768]{2,1,0:T(8,128)} %param.11) | copy-start | bytes 1769476
  105.4 33.6 %copy-start.5 = (f32[4,48,768]{2,1,0:T(8,128)S(1)}, f32[4,48,768]{2,1,0:T(8,128)}, u32[]{:S(2)}) copy-start(f32[4,48,768]{2,1,0:T(8,128)} %param.12) | copy-start | bytes 1769476
  105.4 12.1 %collective-permute-start.17 = (f32[2,48,768]{2,1,0:T(8,128)S(1)}, f32[2,48,768]{2,1,0:T(8,128)S(1)}, u32[]{:S(2)}, u32[]{:S(2)}) collective-permute-start(f32[2,48,768]{2,1,0:T(8,128)S(1)} %get-tuple-element.59), channel_id=1, source_target_pairs={{0,16},{16,0},{1,17},{17,1},{2,18},{18,2},{3,19},{19,3},{4,20},{20... | collective-permute-start | bytes 884744 | tf_op jit(solution)/shard_map/ppermute | solution.py:30
  107.1 10.4 %collective-permute-start.18 = (f32[2,48,768]{2,1,0:T(8,128)S(1)}, f32[2,48,768]{2,1,0:T(8,128)S(1)}, u32[]{:S(2)}, u32[]{:S(2)}) collective-permute-start(f32[2,48,768]{2,1,0:T(8,128)S(1)} %get-tuple-element.60), channel_id=1, source_target_pairs={{0,16},{16,0},{1,17},{17,1},{2,18},{18,2},{3,19},{19,3},{4,20},{20... | collective-permute-start | bytes 884744 | tf_op jit(solution)/shard_map/ppermute | solution.py:30
  118.8 8.2 %collective-permute-start.22 = (bf16[2,96,768]{2,1,0:T(8,128)(2,1)S(1)}, bf16[2,96,768]{2,1,0:T(8,128)(2,1)S(1)}, u32[]{:S(2)}, u32[]{:S(2)}) collective-permute-start(bf16[2,96,768]{2,1,0:T(8,128)(2,1)S(1)} %fresh.1.refs_0_), channel_id=1, source_target_pairs={{0,128},{64,192},{128,0},{192,64},{1,129},{65,193},{129,1},{193,65... | collective-permute-start | bytes 884744 | tf_op jit(solution)/shard_map/ppermute | solution.py:30
  119.8 7.3 %collective-permute-start.21 = (bf16[2,96,768]{2,1,0:T(8,128)(2,1)S(1)}, bf16[2,96,768]{2,1,0:T(8,128)(2,1)S(1)}, u32[]{:S(2)}, u32[]{:S(2)}) collective-permute-start(bf16[2,96,768]{2,1,0:T(8,128)(2,1)S(1)} %fresh.1.refs_0_), channel_id=1, source_target_pairs={{0,32},{32,0},{1,33},{33,1},{2,34},{34,2},{3,35},{35,3},{4,36},{36... | collective-permute-start | bytes 884744 | tf_op jit(solution)/shard_map/ppermute | solution.py:30
  120.1 12.7 %collective-permute-start.20 = (bf16[2,96,768]{2,1,0:T(8,128)(2,1)S(1)}, bf16[2,96,768]{2,1,0:T(8,128)(2,1)S(1)}, u32[]{:S(2)}, u32[]{:S(2)}) collective-permute-start(bf16[2,96,768]{2,1,0:T(8,128)(2,1)S(1)} %fresh.1.refs_0_), channel_id=1, source_target_pairs={{0,192},{64,0},{128,64},{192,128},{1,193},{65,1},{129,65},{193,129... | collective-permute-start | bytes 884744 | tf_op jit(solution)/shard_map/ppermute | solution.py:30
  121.9 12.9 %collective-permute-start.19 = (bf16[2,96,768]{2,1,0:T(8,128)(2,1)S(1)}, bf16[2,96,768]{2,1,0:T(8,128)(2,1)S(1)}, u32[]{:S(2)}, u32[]{:S(2)}) collective-permute-start(bf16[2,96,768]{2,1,0:T(8,128)(2,1)S(1)} %fresh.1.refs_0_), channel_id=1, source_target_pairs={{0,64},{64,128},{128,192},{192,0},{1,65},{65,129},{129,193},{193,1... | collective-permute-start | bytes 884744 | tf_op jit(solution)/shard_map/ppermute | solution.py:30
  127.1 10.1 %collective-permute-start.25 = (bf16[2,96,768]{2,1,0:T(8,128)(2,1)S(1)}, bf16[2,96,768]{2,1,0:T(8,128)(2,1)S(1)}, u32[]{:S(2)}, u32[]{:S(2)}) collective-permute-start(bf16[2,96,768]{2,1,0:T(8,128)(2,1)S(1)} %collective-permute-done.22.refs_4_), channel_id=1, source_target_pairs={{0,32},{32,0},{1,33},{33,1},{2,34},{34,2},{3,35},{35,3},{4,36},{36... | collective-permute-start | bytes 884744 | tf_op jit(solution)/shard_map/ppermute | solution.py:30
  127.4 12.7 %collective-permute-start.24 = (bf16[2,96,768]{2,1,0:T(8,128)(2,1)S(1)}, bf16[2,96,768]{2,1,0:T(8,128)(2,1)S(1)}, u32[]{:S(2)}, u32[]{:S(2)}) collective-permute-start(bf16[2,96,768]{2,1,0:T(8,128)(2,1)S(1)} %collective-permute-done.21.refs_3_), channel_id=1, source_target_pairs={{0,192},{64,0},{128,64},{192,128},{1,193},{65,1},{129,65},{193,129... | collective-permute-start | bytes 884744 | tf_op jit(solution)/shard_map/ppermute | solution.py:30
  128.3 12.8 %collective-permute-start.23 = (bf16[2,96,768]{2,1,0:T(8,128)(2,1)S(1)}, bf16[2,96,768]{2,1,0:T(8,128)(2,1)S(1)}, u32[]{:S(2)}, u32[]{:S(2)}) collective-permute-start(bf16[2,96,768]{2,1,0:T(8,128)(2,1)S(1)} %collective-permute-done.21.refs_3_), channel_id=1, source_target_pairs={{0,64},{64,128},{128,192},{192,0},{1,65},{65,129},{129,193},{193,1... | collective-permute-start | bytes 884744 | tf_op jit(solution)/shard_map/ppermute | solution.py:30
  134.8 7.7 %collective-permute-start.26 = (bf16[2,96,768]{2,1,0:T(8,128)(2,1)S(1)}, bf16[2,96,768]{2,1,0:T(8,128)(2,1)S(1)}, u32[]{:S(2)}, u32[]{:S(2)}) collective-permute-start(bf16[2,96,768]{2,1,0:T(8,128)(2,1)S(1)} %fresh.1.refs_0_), channel_id=1, source_target_pairs={{0,16},{16,0},{1,17},{17,1},{2,18},{18,2},{3,19},{19,3},{4,20},{20... | collective-permute-start | bytes 884744 | tf_op jit(solution)/shard_map/ppermute | solution.py:30
  137.1 5.3 %collective-permute-start.27 = (bf16[2,96,768]{2,1,0:T(8,128)(2,1)S(1)}, bf16[2,96,768]{2,1,0:T(8,128)(2,1)S(1)}, u32[]{:S(2)}, u32[]{:S(2)}) collective-permute-start(bf16[2,96,768]{2,1,0:T(8,128)(2,1)S(1)} %collective-permute-done.19.refs_1_), channel_id=1, source_target_pairs={{0,16},{16,0},{1,17},{17,1},{2,18},{18,2},{3,19},{19,3},{4,20},{20... | collective-permute-start | bytes 884744 | tf_op jit(solution)/shard_map/ppermute | solution.py:30
  137.2 5.8 %collective-permute-start.28 = (bf16[2,96,768]{2,1,0:T(8,128)(2,1)S(1)}, bf16[2,96,768]{2,1,0:T(8,128)(2,1)S(1)}, u32[]{:S(2)}, u32[]{:S(2)}) collective-permute-start(bf16[2,96,768]{2,1,0:T(8,128)(2,1)S(1)} %collective-permute-done.20.refs_2_), channel_id=1, source_target_pairs={{0,16},{16,0},{1,17},{17,1},{2,18},{18,2},{3,19},{19,3},{4,20},{20... | collective-permute-start | bytes 884744 | tf_op jit(solution)/shard_map/ppermute | solution.py:30
  140.1 3.0 %collective-permute-start.29 = (bf16[2,96,768]{2,1,0:T(8,128)(2,1)S(1)}, bf16[2,96,768]{2,1,0:T(8,128)(2,1)S(1)}, u32[]{:S(2)}, u32[]{:S(2)}) collective-permute-start(bf16[2,96,768]{2,1,0:T(8,128)(2,1)S(1)} %collective-permute-done.21.refs_3_), channel_id=1, source_target_pairs={{0,16},{16,0},{1,17},{17,1},{2,18},{18,2},{3,19},{19,3},{4,20},{20... | collective-permute-start | bytes 884744 | tf_op jit(solution)/shard_map/ppermute | solution.py:30
  141.0 2.7 %collective-permute-start.30 = (bf16[2,96,768]{2,1,0:T(8,128)(2,1)S(1)}, bf16[2,96,768]{2,1,0:T(8,128)(2,1)S(1)}, u32[]{:S(2)}, u32[]{:S(2)}) collective-permute-start(bf16[2,96,768]{2,1,0:T(8,128)(2,1)S(1)} %collective-permute-done.22.refs_4_), channel_id=1, source_target_pairs={{0,16},{16,0},{1,17},{17,1},{2,18},{18,2},{3,19},{19,3},{4,20},{20... | collective-permute-start | bytes 884744 | tf_op jit(solution)/shard_map/ppermute | solution.py:30
  142.5 1.6 %collective-permute-start.32 = (bf16[2,96,768]{2,1,0:T(8,128)(2,1)S(1)}, bf16[2,96,768]{2,1,0:T(8,128)(2,1)S(1)}, u32[]{:S(2)}, u32[]{:S(2)}) collective-permute-start(bf16[2,96,768]{2,1,0:T(8,128)(2,1)S(1)} %collective-permute-done.24.refs_6_), channel_id=1, source_target_pairs={{0,16},{16,0},{1,17},{17,1},{2,18},{18,2},{3,19},{19,3},{4,20},{20... | collective-permute-start | bytes 884744 | tf_op jit(solution)/shard_map/ppermute | solution.py:30
  142.5 2.0 %collective-permute-start.31 = (bf16[2,96,768]{2,1,0:T(8,128)(2,1)S(1)}, bf16[2,96,768]{2,1,0:T(8,128)(2,1)S(1)}, u32[]{:S(2)}, u32[]{:S(2)}) collective-permute-start(bf16[2,96,768]{2,1,0:T(8,128)(2,1)S(1)} %collective-permute-done.23.refs_5_), channel_id=1, source_target_pairs={{0,16},{16,0},{1,17},{17,1},{2,18},{18,2},{3,19},{19,3},{4,20},{20... | collective-permute-start | bytes 884744 | tf_op jit(solution)/shard_map/ppermute | solution.py:30
  143.0 2.0 %collective-permute-start.33 = (bf16[2,96,768]{2,1,0:T(8,128)(2,1)S(1)}, bf16[2,96,768]{2,1,0:T(8,128)(2,1)S(1)}, u32[]{:S(2)}, u32[]{:S(2)}) collective-permute-start(bf16[2,96,768]{2,1,0:T(8,128)(2,1)S(1)} %collective-permute-done.25.refs_7_), channel_id=1, source_target_pairs={{0,16},{16,0},{1,17},{17,1},{2,18},{18,2},{3,19},{19,3},{4,20},{20... | collective-permute-start | bytes 884744 | tf_op jit(solution)/shard_map/ppermute | solution.py:30

commit v4 on v3

--- a/solution.py
+++ b/solution.py
@@ -317,9 +317,10 @@
         grads[0].reshape(blocks, CHIPS, CORE, rows, width), pltpu.HBM
     )
     at_dp = lax.axis_index(("y", "zl", "core")).astype(jnp.int32)[None]
-    r_near = z_swap(root_right)
+    r_near, r_late = z_swap(root_right[:HALF]), z_swap(root_right[HALF:])
     chip = pair_call(half_call(at_dp, parts, False), core_swap(half_call(at_dp, parts, True)))
     chip, r_near = lax.optimization_barrier((chip, r_near))
+    r_near = jnp.concatenate([r_near, r_late], axis=0)
     r_keep, r_give = halves(
         jnp.where(
             zl == 0, jnp.stack([root_right, r_near], axis=1), jnp.stack([r_near, root_right], axis=1)

time: 148 us -> 147 us (level)
  blocking collectives: 10.3 us -> 7.51 us
  starting transfers between devices: 47 us -> 44.9 us
  other arithmetic: 4.25 us -> 6.27 us
    all_to_all x1, blocking collectives: 10.3 us -> 7.51 us  [on_device(): sums = lax.all_to_all(sums, ('y', 'zl'), 0, 0, tiled=True)]
    ppermute x34 -> x35, starting transfers between devices: 33.3 us -> 31.1 us  [shift(): return lambda value: lax.ppermute(value, axis, pairs)]
    all_to_all x1, waiting for transfers between devices: 25.3 us -> 27.4 us  [on_device(): came = lax.all_to_all(sends, ('x', 'zh'), 0, 0, tiled=True)]
    ppermute x34 -> x35, waiting for transfers between devices: 31.9 us -> 30.3 us  [shift(): return lambda value: lax.ppermute(value, axis, pairs)]
  transfers between devices with their start and end apart: 36 -> 37, of which waited for: 19 -> 14; matrix products, arithmetic and copies ran while one was open for 4% -> 6% of each run, Pallas kernels for 2% -> 2%
where the time goes in v4:
time: 147 us
  waiting for transfers between devices  69.5 us (47%)
  starting transfers between devices  44.9 us (31%)
  Pallas kernels  14.9 us (10%)
  blocking collectives  7.51 us (5%)
  other arithmetic  6.27 us (4%)
  local copies, waits for them, and re-layouts  2.67 us (2%)
    ppermute x35, starting transfers between devices, shift(): return lambda value: lax.ppermute(value, axis, pairs)  31.1 us
    ppermute x35, waiting for transfers between devices, shift(): return lambda value: lax.ppermute(value, axis, pairs)  30.3 us
    all_to_all x1, waiting for transfers between devices, on_device(): came = lax.all_to_all(sends, ('x', 'zh'), 0, 0, tiled=True)  27.4 us
    all_to_all x1, waiting for transfers between devices, on_device(): parts = lax.all_to_all(chip, ('y', 'zl'), 0, 0, tiled=True)  11.8 us
    all_to_all x1, starting transfers between devices, on_device(): came = lax.all_to_all(sends, ('x', 'zh'), 0, 0, tiled=True)  9.85 us
    all_to_all x1, blocking collectives, on_device(): sums = lax.all_to_all(sums, ('y', 'zl'), 0, 0, tiled=True)  7.51 us
    all_to_all x1, starting transfers between devices, on_device(): parts = lax.all_to_all(chip, ('y', 'zl'), 0, 0, tiled=True)  3.94 us
    pallas_call x1, Pallas kernels, precond_call(): pl.pallas_call(precond_body, in_specs=[SM, SM] + [VM] * (1 + CHIPS) + [AN...  3.36 us
  transfers between devices with their start and end apart: 37, of which 14 were waited for; matrix products, arithmetic and copies ran while one was open for 6% of the time, Pallas kernels for 2%

profile of v4, /device:TPU:1, one launch (start us, length us, event | category | flops | bytes accessed | tf_op | source)
XLA Modules:
  0.0 146.9 jit_solution(5341448199133926431)
XLA Ops:
  0.7 1.3 give.1
  2.0 3.3 %collective-permute-start.2 = (bf16[8,2,48,768]{3,2,1,0:T(8,128)(2,1)S(1)}, bf16[8,2,48,768]{3,2,1,0:T(8,128)(2,1)S(1)}, u32[]{:S(2)}, u32[]{:S(2)}) collective-permute-start(bf16[8,2,48,768]{3,2,1,0:T(8,128)(2,1)S(1)} %give.1), channel_id=1, source_target_pairs={{0,16},{16,0},{1,17},{17,1},{2,18},{18,2},{3,19},{19,3},{4,20},{20... | collective-permute-start | bytes 3538952 | tf_op jit(solution)/shard_map/ppermute | solution.py:30
  5.3 0.7 fusion.11
  6.1 0.7 constant_dynamic-slice_fusion.6
  6.8 0.2 collective-permute-start
  7.0 1.6 %collective-permute-start.4 = (bf16[2,48,768]{2,1,0:T(8,128)(2,1)}, bf16[2,48,768]{2,1,0:T(8,128)(2,1)}, u32[]{:S(2)}, u32[]{:S(2)}) collective-permute-start(bf16[2,48,768]{2,1,0:T(8,128)(2,1)} %get-tuple-element.86), channel_id=1, source_target_pairs={{0,32},{32,0},{1,33},{33,1},{2,34},{34,2},{3,35},{35,3},{4,36},{36... | collective-permute-start | bytes 442376 | tf_op jit(solution)/shard_map/ppermute | solution.py:30
  8.6 0.9 constant_dynamic-slice_fusion.4
  9.4 0.5 collective-permute-start.1
  9.9 1.3 keep.1
  11.3 1.3 pair.1
  12.6 3.9 %all-to-all-start = ((bf16[8,2,48,768]{3,2,1,0:T(8,128)(2,1)}), bf16[8,2,48,768]{3,2,1,0:T(8,128)(2,1)S(1)}, u32[]{:S(2)}, u32[]{:S(2)}) async-start(bf16[8,2,48,768]{3,2,1,0:T(8,128)(2,1)} %pair.1), calls=%async_computation | async-start | bytes 2359296 | tf_op jit(solution)/shard_map/all_to_all | solution.py:333
  16.5 0.2 convert_reduce_fusion
  16.8 0.2 select_reduce_fusion
  17.0 1.0 maximum_bitcast_fusion
  18.2 0.7 collective-permute-start.5
  19.0 1.1 maximum_select_fusion.5.left
  20.0 1.1 maximum_select_fusion.weights
  21.3 11.8 %all-to-all-done.parts = bf16[8,2,48,768]{3,2,1,0:T(8,128)(2,1)S(1)} async-done(((bf16[8,2,48,768]{3,2,1,0:T(8,128)(2,1)}), bf16[8,2,48,768]{3,2,1,0:T(8,128)(2,1)S(1)}, u32[]{:S(2)}, u32[]{:S(2)}) %all-to-all-start) | async-done | bytes 1179680 | tf_op jit(solution)/shard_map/all_to_all | solution.py:333
  33.1 1.8 %sort.1 = bf16[16,48,768]{2,1,0:T(8,128)(2,1)} custom-call(s32[16]{0:T(128)S(1)} %maximum_add_fusion.table, bf16[8,2,48,768]{3,2,1,0:T(8,128)(2,1)S(1)} %all-to-all-done.parts), custom_call_target="tpu_custom_call" | custom-call | tf_op jit(solution)/shard_map/sort/pallas_call | solution.py:227
  34.9 9.9 %all-to-all-start.1 = ((bf16[16,48,768]{2,1,0:T(8,128)(2,1)}), bf16[16,48,768]{2,1,0:T(8,128)(2,1)S(1)}, u32[]{:S(2)}, u32[]{:S(2)}) async-start(bf16[16,48,768]{2,1,0:T(8,128)(2,1)} %sort.1), calls=%async_computation.1 | async-start | bytes 2359296 | tf_op jit(solution)/shard_map/all_to_all | solution.py:352
  44.8 0.7 collective-permute-start.8
  45.5 1.5 collective-permute-start.7
  46.9 27.4 %all-to-all-done.1.blocks = bf16[16,48,768]{2,1,0:T(8,128)(2,1)S(1)} async-done(((bf16[16,48,768]{2,1,0:T(8,128)(2,1)}), bf16[16,48,768]{2,1,0:T(8,128)(2,1)S(1)}, u32[]{:S(2)}, u32[]{:S(2)}) %all-to-all-start.1) | async-done | bytes 1179680 | tf_op jit(solution)/shard_map/all_to_all | solution.py:352
  74.3 0.6 pick.1
  75.0 4.6 %collective-permute-start.9 = (bf16[2,48,768]{2,1,0:T(8,128)(2,1)S(1)}, bf16[2,48,768]{2,1,0:T(8,128)(2,1)S(1)}, u32[]{:S(2)}, u32[]{:S(2)}) collective-permute-start(bf16[2,48,768]{2,1,0:T(8,128)(2,1)S(1)} %get-tuple-element.85), channel_id=1, source_target_pairs={{0,16},{16,0},{1,17},{17,1},{2,18},{18,2},{3,19},{19,3},{4,20},{20... | collective-permute-start | bytes 442376 | tf_op jit(solution)/shard_map/ppermute | solution.py:30
  79.6 1.0 collective-permute-done.9
  80.6 0.1 collective-permute-start.14
  80.7 0.1 collective-permute-start.13
  80.8 2.1 %collective-permute-start.10 = (bf16[2,96,768]{2,1,0:T(8,128)(2,1)S(1)}, bf16[2,96,768]{2,1,0:T(8,128)(2,1)S(1)}, u32[]{:S(2)}, u32[]{:S(2)}) collective-permute-start(bf16[2,96,768]{2,1,0:T(8,128)(2,1)S(1)} %maximum_select_fusion.6.refs_0_), channel_id=1, source_target_pairs={{0,64},{64,128},{128,192},{192,0},{1,65},{65,129},{129,193},{193,1... | collective-permute-start | bytes 884744 | tf_op jit(solution)/shard_map/ppermute | solution.py:30
  82.9 0.7 collective-permute-start.12
  83.6 6.9 %collective-permute-done.14.refs_4_ = bf16[2,96,768]{2,1,0:T(8,128)(2,1)S(1)} collective-permute-done((bf16[2,96,768]{2,1,0:T(8,128)(2,1)S(1)}, bf16[2,96,768]{2,1,0:T(8,128)(2,1)S(1)}, u32[]{:S(2)}, u32[]{:S(2)}) %collective-permute-start.14) | collective-permute-done | bytes 294944 | tf_op jit(solution)/shard_map/ppermute | solution.py:30
  90.5 1.5 collective-permute-start.15
  92.0 0.2 collective-permute-start.17
  92.1 5.1 %collective-permute-done.10.refs_1_ = bf16[2,96,768]{2,1,0:T(8,128)(2,1)S(1)} collective-permute-done((bf16[2,96,768]{2,1,0:T(8,128)(2,1)S(1)}, bf16[2,96,768]{2,1,0:T(8,128)(2,1)S(1)}, u32[]{:S(2)}, u32[]{:S(2)}) %collective-permute-start.10) | collective-permute-done | bytes 294944 | tf_op jit(solution)/shard_map/ppermute | solution.py:30
  97.3 1.1 fusion.6
  98.5 0.8 collective-permute-start.11
  99.3 0.8 collective-permute-done.11
  100.2 3.4 %collective-permute-done.15.refs_5_ = bf16[2,96,768]{2,1,0:T(8,128)(2,1)S(1)} collective-permute-done((bf16[2,96,768]{2,1,0:T(8,128)(2,1)S(1)}, bf16[2,96,768]{2,1,0:T(8,128)(2,1)S(1)}, u32[]{:S(2)}, u32[]{:S(2)}) %collective-permute-start.15) | collective-permute-done | bytes 294944 | tf_op jit(solution)/shard_map/ppermute | solution.py:30
  103.6 3.4 %precond.1 = (f32[2,96,768]{2,1,0:T(8,128)S(1)}, f32[8,1,128]{2,1,0:T(1,128)S(1)}, bf16[2,768,768]{2,1,0:T(8,128)(2,1)S(1)}) custom-call(s32[1]{0:T(128)} %bitcast.at_dp, f32[2]{0:T(128)S(1)} %dynamic-slice_add_fusion.adam_sq, bf16[2,96,768]{2,1,0:T(8,128)(2,1)S(1)} %maximum_select_fusion.5.left, bf16[2,96,768]{2,1,0:T(8,128)(2,1)S(1)} %maximum_select_fusion.6.refs_0_, ...), custom_call_target="tpu_custom_call" | custom-call | tf_op jit(solution)/shard_map/precond/pallas_call | solution.py:138
  107.0 1.7 %stats.1 = (f32[2,48,768]{2,1,0:T(8,128)S(1)}, f32[2,48,768]{2,1,0:T(8,128)S(1)}, f32[2,48,768]{2,1,0:T(8,128)S(1)}, f32[2,48,768]{2,1,0:T(8,128)S(1)}) custom-call(s32[1]{0:T(128)} %bitcast.at_dp, bf16[2,768,768]{2,1,0:T(8,128)(2,1)S(1)} %get-tuple-element.58.g), custom_call_target="tpu_custom_call" | custom-call | tf_op jit(solution)/shard_map/stats/pallas_call | solution.py:181
  108.7 0.7 collective-permute-start.18
  109.4 0.1 collective-permute-start.19
  109.5 7.5 %all_to_all.15.sums = f32[8,1,128]{2,1,0:T(1,128)S(1)} all-to-all(f32[8,1,128]{2,1,0:T(1,128)S(1)} %get-tuple-element.57), channel_id=1, replica_groups=mesh['y'=4,'zl'=2,'core'=2,'x'=4,'zh'=4] {'y','zl'}, dimensions={0} | all-to-all | bytes 8192 | tf_op jit(solution)/shard_map/all_to_all | solution.py:367
  117.0 1.3 fresh.1.refs_0_
  118.3 1.0 collective-permute-start.23
  119.3 0.3 collective-permute-start.22
  119.6 1.8 %collective-permute-start.21 = (bf16[2,96,768]{2,1,0:T(8,128)(2,1)S(1)}, bf16[2,96,768]{2,1,0:T(8,128)(2,1)S(1)}, u32[]{:S(2)}, u32[]{:S(2)}) collective-permute-start(bf16[2,96,768]{2,1,0:T(8,128)(2,1)S(1)} %fresh.1.refs_0_), channel_id=1, source_target_pairs={{0,192},{64,0},{128,64},{192,128},{1,193},{65,1},{129,65},{193,129... | collective-permute-start | bytes 884744 | tf_op jit(solution)/shard_map/ppermute | solution.py:30
  121.4 5.2 %collective-permute-done.23.refs_4_ = bf16[2,96,768]{2,1,0:T(8,128)(2,1)S(1)} collective-permute-done((bf16[2,96,768]{2,1,0:T(8,128)(2,1)S(1)}, bf16[2,96,768]{2,1,0:T(8,128)(2,1)S(1)}, u32[]{:S(2)}, u32[]{:S(2)}) %collective-permute-start.23) | collective-permute-done | bytes 294944 | tf_op jit(solution)/shard_map/ppermute | solution.py:30
  126.6 0.3 collective-permute-start.26
  126.9 0.9 collective-permute-start.25
  127.8 0.6 collective-permute-start.24
  128.3 4.0 %collective-permute-done.21.refs_2_ = bf16[2,96,768]{2,1,0:T(8,128)(2,1)S(1)} collective-permute-done((bf16[2,96,768]{2,1,0:T(8,128)(2,1)S(1)}, bf16[2,96,768]{2,1,0:T(8,128)(2,1)S(1)}, u32[]{:S(2)}, u32[]{:S(2)}) %collective-permute-start.21) | collective-permute-done | bytes 294944 | tf_op jit(solution)/shard_map/ppermute | solution.py:30
  132.3 2.0 %collective-permute-done.20.refs_1_ = bf16[2,96,768]{2,1,0:T(8,128)(2,1)S(1)} collective-permute-done((bf16[2,96,768]{2,1,0:T(8,128)(2,1)S(1)}, bf16[2,96,768]{2,1,0:T(8,128)(2,1)S(1)}, u32[]{:S(2)}, u32[]{:S(2)}) %collective-permute-start.20) | collective-permute-done | bytes 294944 | tf_op jit(solution)/shard_map/ppermute | solution.py:30
  134.3 2.4 %collective-permute-start.27 = (bf16[2,96,768]{2,1,0:T(8,128)(2,1)S(1)}, bf16[2,96,768]{2,1,0:T(8,128)(2,1)S(1)}, u32[]{:S(2)}, u32[]{:S(2)}) collective-permute-start(bf16[2,96,768]{2,1,0:T(8,128)(2,1)S(1)} %fresh.1.refs_0_), channel_id=1, source_target_pairs={{0,16},{16,0},{1,17},{17,1},{2,18},{18,2},{3,19},{19,3},{4,20},{20... | collective-permute-start | bytes 884744 | tf_op jit(solution)/shard_map/ppermute | solution.py:30
  136.7 1.8 %collective-permute-start.29 = (bf16[2,96,768]{2,1,0:T(8,128)(2,1)S(1)}, bf16[2,96,768]{2,1,0:T(8,128)(2,1)S(1)}, u32[]{:S(2)}, u32[]{:S(2)}) collective-permute-start(bf16[2,96,768]{2,1,0:T(8,128)(2,1)S(1)} %collective-permute-done.21.refs_2_), channel_id=1, source_target_pairs={{0,16},{16,0},{1,17},{17,1},{2,18},{18,2},{3,19},{19,3},{4,20},{20... | collective-permute-start | bytes 884744 | tf_op jit(solution)/shard_map/ppermute | solution.py:30
  138.4 1.1 fusion.3
  139.6 0.9 collective-permute-start.30
  140.5 1.5 collective-permute-start.31
  142.0 0.5 collective-permute-start.32
  142.6 0.6 collective-permute-done.31.refs_12_
  143.2 0.4 collective-permute-done.33.refs_14_
  143.6 0.4 collective-permute-done.32.refs_13_
  144.0 0.4 collective-permute-done.34.refs_15_
  144.4 2.3 %assemble.1 = bf16[4,768,768]{2,1,0:T(8,128)(2,1)} custom-call(s32[1]{0:T(128)} %bitcast.at_dp, bf16[2,96,768]{2,1,0:T(8,128)(2,1)S(1)} %fresh.1.refs_0_, bf16[2,96,768]{2,1,0:T(8,128)(2,1)S(1)} %collective-permute-done.20.refs_1_, bf16[2,96,768]{2,1,0:T(8,128)(2,1)S(1)} %collective-permute-done.21.refs_2_, ...), custom_call_target="tpu_custom_call" | custom-call | tf_op jit(solution)/shard_map/assemble/pallas_call | solution.py:276
  (70 shorter events, 1.0 us)
Async XLA Ops:
  0.6 4.7 %copy-start.2 = (bf16[4,48,768]{2,1,0:T(8,128)(2,1)S(1)}, bf16[4,48,768]{2,1,0:T(8,128)(2,1)}, u32[]{:S(2)}) copy-start(bf16[4,48,768]{2,1,0:T(8,128)(2,1)} %param.15) | copy-start | bytes 884740
  0.7 5.4 %copy-start.10 = (bf16[4,48,768]{2,1,0:T(8,128)(2,1)S(1)}, bf16[4,48,768]{2,1,0:T(8,128)(2,1)}, u32[]{:S(2)}) copy-start(bf16[4,48,768]{2,1,0:T(8,128)(2,1)} %param.14) | copy-start | bytes 884740
  2.0 6.6 %copy-start.6 = (f32[4,48,768]{2,1,0:T(8,128)S(1)}, f32[4,48,768]{2,1,0:T(8,128)}, u32[]{:S(2)}) copy-start(f32[4,48,768]{2,1,0:T(8,128)} %param.10) | copy-start | bytes 1769476
  2.0 9.3 %collective-permute-start.2 = (bf16[8,2,48,768]{3,2,1,0:T(8,128)(2,1)S(1)}, bf16[8,2,48,768]{3,2,1,0:T(8,128)(2,1)S(1)}, u32[]{:S(2)}, u32[]{:S(2)}) collective-permute-start(bf16[8,2,48,768]{3,2,1,0:T(8,128)(2,1)S(1)} %give.1), channel_id=1, source_target_pairs={{0,16},{16,0},{1,17},{17,1},{2,18},{18,2},{3,19},{19,3},{4,20},{20... | collective-permute-start | bytes 3538952 | tf_op jit(solution)/shard_map/ppermute | solution.py:30
  6.1 6.5 %collective-permute-start.3 = (bf16[2,48,768]{2,1,0:T(8,128)(2,1)}, bf16[2,48,768]{2,1,0:T(8,128)(2,1)}, u32[]{:S(2)}, u32[]{:S(2)}) collective-permute-start(bf16[2,48,768]{2,1,0:T(8,128)(2,1)} %get-tuple-element.87), channel_id=1, source_target_pairs={{0,32},{32,0},{1,33},{33,1},{2,34},{34,2},{3,35},{35,3},{4,36},{36... | collective-permute-start | bytes 442376 | tf_op jit(solution)/shard_map/ppermute | solution.py:30
  6.8 12.1 %collective-permute-start = (bf16[2,48,768]{2,1,0:T(8,128)(2,1)}, bf16[2,48,768]{2,1,0:T(8,128)(2,1)}, u32[]{:S(2)}, u32[]{:S(2)}) collective-permute-start(bf16[2,48,768]{2,1,0:T(8,128)(2,1)} %get-tuple-element.89), channel_id=1, source_target_pairs={{0,16},{16,0},{1,17},{17,1},{2,18},{18,2},{3,19},{19,3},{4,20},{20... | collective-permute-start | bytes 442376 | tf_op jit(solution)/shard_map/ppermute | solution.py:30
  7.0 10.0 %collective-permute-start.4 = (bf16[2,48,768]{2,1,0:T(8,128)(2,1)}, bf16[2,48,768]{2,1,0:T(8,128)(2,1)}, u32[]{:S(2)}, u32[]{:S(2)}) collective-permute-start(bf16[2,48,768]{2,1,0:T(8,128)(2,1)} %get-tuple-element.86), channel_id=1, source_target_pairs={{0,32},{32,0},{1,33},{33,1},{2,34},{34,2},{3,35},{35,3},{4,36},{36... | collective-permute-start | bytes 442376 | tf_op jit(solution)/shard_map/ppermute | solution.py:30
  9.4 10.6 %collective-permute-start.1 = (f32[2,48,768]{2,1,0:T(8,128)}, f32[2,48,768]{2,1,0:T(8,128)}, u32[]{:S(2)}, u32[]{:S(2)}) collective-permute-start(f32[2,48,768]{2,1,0:T(8,128)} %get-tuple-element.83), channel_id=1, source_target_pairs={{0,16},{16,0},{1,17},{17,1},{2,18},{18,2},{3,19},{19,3},{4,20},{20... | collective-permute-start | bytes 884744 | tf_op jit(solution)/shard_map/ppermute | solution.py:30
  9.9 1.3 copy-start.11
  12.6 5.5 %copy-start.3 = (bf16[4,48,768]{2,1,0:T(8,128)(2,1)S(1)}, bf16[4,48,768]{2,1,0:T(8,128)(2,1)}, u32[]{:S(2)}) copy-start(bf16[4,48,768]{2,1,0:T(8,128)(2,1)} %param.15) | copy-start | bytes 884740
  12.6 20.5 %all-to-all-start = ((bf16[8,2,48,768]{3,2,1,0:T(8,128)(2,1)}), bf16[8,2,48,768]{3,2,1,0:T(8,128)(2,1)S(1)}, u32[]{:S(2)}, u32[]{:S(2)}) async-start(bf16[8,2,48,768]{3,2,1,0:T(8,128)(2,1)} %pair.1), calls=%async_computation | async-start | bytes 2359296 | tf_op jit(solution)/shard_map/all_to_all | solution.py:333
  18.1 0.9 copy-start.7
  18.2 1.9 %copy-start.4 = (f32[2,48,768]{2,1,0:T(8,128)S(1)}, f32[2,48,768]{2,1,0:T(8,128)}, u32[]{:S(2)}) copy-start(f32[2,48,768]{2,1,0:T(8,128)} %get-tuple-element.82) | copy-start | bytes 884740
  18.2 2.9 %collective-permute-start.5 = (bf16[2,2,48,768]{3,2,0,1:T(8,128)(2,1)S(1)}, bf16[2,2,48,768]{3,2,0,1:T(8,128)(2,1)S(1)}, u32[]{:S(2)}, u32[]{:S(2)}) collective-permute-start(bf16[2,2,48,768]{3,2,0,1:T(8,128)(2,1)S(1)} %get-tuple-element.81), channel_id=1, source_target_pairs={{0,16},{16,0},{1,17},{17,1},{2,18},{18,2},{3,19},{19,3},{4,20},{20... | collective-permute-start | bytes 884744 | tf_op jit(solution)/shard_map/ppermute | solution.py:30
  21.3 25.6 %copy-start.1 = (bf16[2,2,2,48,768]{4,3,2,1,0:T(8,128)(2,1)}, bf16[2,2,2,48,768]{4,3,2,1,0:T(8,128)(2,1)S(1)}, u32[]{:S(2)}) copy-start(bf16[2,2,2,48,768]{4,3,2,1,0:T(8,128)(2,1)S(1)} %copy.13) | copy-start | bytes 1769476
  34.9 39.4 %all-to-all-start.1 = ((bf16[16,48,768]{2,1,0:T(8,128)(2,1)}), bf16[16,48,768]{2,1,0:T(8,128)(2,1)S(1)}, u32[]{:S(2)}, u32[]{:S(2)}) async-start(bf16[16,48,768]{2,1,0:T(8,128)(2,1)} %sort.1), calls=%async_computation.1 | async-start | bytes 2359296 | tf_op jit(solution)/shard_map/all_to_all | solution.py:352
  44.8 52.5 %copy-start.5 = (f32[4,48,768]{2,1,0:T(8,128)S(1)}, f32[4,48,768]{2,1,0:T(8,128)}, u32[]{:S(2)}) copy-start(f32[4,48,768]{2,1,0:T(8,128)} %param.13) | copy-start | bytes 1769476
  44.8 30.1 %collective-permute-start.8 = (bf16[2,192,768]{2,1,0:T(8,128)(2,1)S(1)}, bf16[2,192,768]{2,1,0:T(8,128)(2,1)}, u32[]{:S(2)}, u32[]{:S(2)}) collective-permute-start(bf16[2,192,768]{2,1,0:T(8,128)(2,1)S(1)} %bitcast.11), channel_id=1, source_target_pairs={{0,128},{64,192},{128,0},{192,64},{1,129},{65,193},{129,1},{193,65... | collective-permute-start | bytes 1769480 | tf_op jit(solution)/shard_map/ppermute | solution.py:30
  45.5 29.5 %collective-permute-start.7 = (bf16[2,192,768]{2,1,0:T(8,128)(2,1)S(1)}, bf16[2,192,768]{2,1,0:T(8,128)(2,1)}, u32[]{:S(2)}, u32[]{:S(2)}) collective-permute-start(bf16[2,192,768]{2,1,0:T(8,128)(2,1)S(1)} %bitcast.12), channel_id=1, source_target_pairs={{0,192},{64,0},{128,64},{192,128},{1,193},{65,1},{129,65},{193,129... | collective-permute-start | bytes 1769480 | tf_op jit(solution)/shard_map/ppermute | solution.py:30
  46.9 28.0 %collective-permute-start.6 = (bf16[2,192,768]{2,1,0:T(8,128)(2,1)S(1)}, bf16[2,192,768]{2,1,0:T(8,128)(2,1)}, u32[]{:S(2)}, u32[]{:S(2)}) collective-permute-start(bf16[2,192,768]{2,1,0:T(8,128)(2,1)S(1)} %bitcast.13), channel_id=1, source_target_pairs={{0,64},{64,128},{128,192},{192,0},{1,65},{65,129},{129,193},{193,1... | collective-permute-start | bytes 1769480 | tf_op jit(solution)/shard_map/ppermute | solution.py:30
  75.0 5.6 %collective-permute-start.9 = (bf16[2,48,768]{2,1,0:T(8,128)(2,1)S(1)}, bf16[2,48,768]{2,1,0:T(8,128)(2,1)S(1)}, u32[]{:S(2)}, u32[]{:S(2)}) collective-permute-start(bf16[2,48,768]{2,1,0:T(8,128)(2,1)S(1)} %get-tuple-element.85), channel_id=1, source_target_pairs={{0,16},{16,0},{1,17},{17,1},{2,18},{18,2},{3,19},{19,3},{4,20},{20... | collective-permute-start | bytes 442376 | tf_op jit(solution)/shard_map/ppermute | solution.py:30
  80.6 9.9 %collective-permute-start.14 = (bf16[2,96,768]{2,1,0:T(8,128)(2,1)S(1)}, bf16[2,96,768]{2,1,0:T(8,128)(2,1)S(1)}, u32[]{:S(2)}, u32[]{:S(2)}) collective-permute-start(bf16[2,96,768]{2,1,0:T(8,128)(2,1)S(1)} %maximum_select_fusion.6.refs_0_), channel_id=1, source_target_pairs={{0,128},{64,192},{128,0},{192,64},{1,129},{65,193},{129,1},{193,65... | collective-permute-start | bytes 884744 | tf_op jit(solution)/shard_map/ppermute | solution.py:30
  80.7 9.8 %collective-permute-start.13 = (bf16[2,96,768]{2,1,0:T(8,128)(2,1)S(1)}, bf16[2,96,768]{2,1,0:T(8,128)(2,1)S(1)}, u32[]{:S(2)}, u32[]{:S(2)}) collective-permute-start(bf16[2,96,768]{2,1,0:T(8,128)(2,1)S(1)} %maximum_select_fusion.6.refs_0_), channel_id=1, source_target_pairs={{0,32},{32,0},{1,33},{33,1},{2,34},{34,2},{3,35},{35,3},{4,36},{36... | collective-permute-start | bytes 884744 | tf_op jit(solution)/shard_map/ppermute | solution.py:30
  80.8 16.4 %collective-permute-start.10 = (bf16[2,96,768]{2,1,0:T(8,128)(2,1)S(1)}, bf16[2,96,768]{2,1,0:T(8,128)(2,1)S(1)}, u32[]{:S(2)}, u32[]{:S(2)}) collective-permute-start(bf16[2,96,768]{2,1,0:T(8,128)(2,1)S(1)} %maximum_select_fusion.6.refs_0_), channel_id=1, source_target_pairs={{0,64},{64,128},{128,192},{192,0},{1,65},{65,129},{129,193},{193,1... | collective-permute-start | bytes 884744 | tf_op jit(solution)/shard_map/ppermute | solution.py:30
  82.9 17.3 %collective-permute-start.12 = (bf16[2,96,768]{2,1,0:T(8,128)(2,1)S(1)}, bf16[2,96,768]{2,1,0:T(8,128)(2,1)S(1)}, u32[]{:S(2)}, u32[]{:S(2)}) collective-permute-start(bf16[2,96,768]{2,1,0:T(8,128)(2,1)S(1)} %maximum_select_fusion.6.refs_0_), channel_id=1, source_target_pairs={{0,192},{64,0},{128,64},{192,128},{1,193},{65,1},{129,65},{193,129... | collective-permute-start | bytes 884744 | tf_op jit(solution)/shard_map/ppermute | solution.py:30
  90.5 9.7 %collective-permute-start.16 = (bf16[2,96,768]{2,1,0:T(8,128)(2,1)S(1)}, bf16[2,96,768]{2,1,0:T(8,128)(2,1)S(1)}, u32[]{:S(2)}, u32[]{:S(2)}) collective-permute-start(bf16[2,96,768]{2,1,0:T(8,128)(2,1)S(1)} %collective-permute-done.13.refs_3_), channel_id=1, source_target_pairs={{0,192},{64,0},{128,64},{192,128},{1,193},{65,1},{129,65},{193,129... | collective-permute-start | bytes 884744 | tf_op jit(solution)/shard_map/ppermute | solution.py:30
  90.5 13.1 %collective-permute-start.15 = (bf16[2,96,768]{2,1,0:T(8,128)(2,1)S(1)}, bf16[2,96,768]{2,1,0:T(8,128)(2,1)S(1)}, u32[]{:S(2)}, u32[]{:S(2)}) collective-permute-start(bf16[2,96,768]{2,1,0:T(8,128)(2,1)S(1)} %collective-permute-done.13.refs_3_), channel_id=1, source_target_pairs={{0,64},{64,128},{128,192},{192,0},{1,65},{65,129},{129,193},{193,1... | collective-permute-start | bytes 884744 | tf_op jit(solution)/shard_map/ppermute | solution.py:30
  92.0 8.2 %collective-permute-start.17 = (bf16[2,96,768]{2,1,0:T(8,128)(2,1)S(1)}, bf16[2,96,768]{2,1,0:T(8,128)(2,1)S(1)}, u32[]{:S(2)}, u32[]{:S(2)}) collective-permute-start(bf16[2,96,768]{2,1,0:T(8,128)(2,1)S(1)} %collective-permute-done.14.refs_4_), channel_id=1, source_target_pairs={{0,32},{32,0},{1,33},{33,1},{2,34},{34,2},{3,35},{35,3},{4,36},{36... | collective-permute-start | bytes 884744 | tf_op jit(solution)/shard_map/ppermute | solution.py:30
  98.5 1.6 %collective-permute-start.11 = (f32[2]{0:T(128)S(1)}, f32[2]{0:T(128)S(1)}, u32[]{:S(2)}, u32[]{:S(2)}) collective-permute-start(f32[2]{0:T(128)S(1)} %dynamic_slice.43), channel_id=1, source_target_pairs={{0,16},{16,0},{1,17},{17,1},{2,18},{18,2},{3,19},{19,3},{4,20},{20... | collective-permute-start | bytes 32 | tf_op jit(solution)/shard_map/ppermute | solution.py:30
  107.0 1.7 %copy-start = (f32[2,96,768]{2,1,0:T(8,128)}, f32[2,96,768]{2,1,0:T(8,128)S(1)}, u32[]{:S(2)}) copy-start(f32[2,96,768]{2,1,0:T(8,128)S(1)} %get-tuple-element.63.prec) | copy-start | bytes 1769476
  108.7 29.8 %copy-start.8 = (f32[4,48,768]{2,1,0:T(8,128)S(1)}, f32[4,48,768]{2,1,0:T(8,128)}, u32[]{:S(2)}) copy-start(f32[4,48,768]{2,1,0:T(8,128)} %param.11) | copy-start | bytes 1769476
  108.7 29.7 %copy-start.9 = (f32[4,48,768]{2,1,0:T(8,128)S(1)}, f32[4,48,768]{2,1,0:T(8,128)}, u32[]{:S(2)}) copy-start(f32[4,48,768]{2,1,0:T(8,128)} %param.12) | copy-start | bytes 1769476
  108.7 8.3 %collective-permute-start.18 = (f32[2,48,768]{2,1,0:T(8,128)S(1)}, f32[2,48,768]{2,1,0:T(8,128)S(1)}, u32[]{:S(2)}, u32[]{:S(2)}) collective-permute-start(f32[2,48,768]{2,1,0:T(8,128)S(1)} %get-tuple-element.59), channel_id=1, source_target_pairs={{0,16},{16,0},{1,17},{17,1},{2,18},{18,2},{3,19},{19,3},{4,20},{20... | collective-permute-start | bytes 884744 | tf_op jit(solution)/shard_map/ppermute | solution.py:30
  109.4 7.6 %collective-permute-start.19 = (f32[2,48,768]{2,1,0:T(8,128)S(1)}, f32[2,48,768]{2,1,0:T(8,128)S(1)}, u32[]{:S(2)}, u32[]{:S(2)}) collective-permute-start(f32[2,48,768]{2,1,0:T(8,128)S(1)} %get-tuple-element.60), channel_id=1, source_target_pairs={{0,16},{16,0},{1,17},{17,1},{2,18},{18,2},{3,19},{19,3},{4,20},{20... | collective-permute-start | bytes 884744 | tf_op jit(solution)/shard_map/ppermute | solution.py:30
  118.3 8.2 %collective-permute-start.23 = (bf16[2,96,768]{2,1,0:T(8,128)(2,1)S(1)}, bf16[2,96,768]{2,1,0:T(8,128)(2,1)S(1)}, u32[]{:S(2)}, u32[]{:S(2)}) collective-permute-start(bf16[2,96,768]{2,1,0:T(8,128)(2,1)S(1)} %fresh.1.refs_0_), channel_id=1, source_target_pairs={{0,128},{64,192},{128,0},{192,64},{1,129},{65,193},{129,1},{193,65... | collective-permute-start | bytes 884744 | tf_op jit(solution)/shard_map/ppermute | solution.py:30
  119.3 7.3 %collective-permute-start.22 = (bf16[2,96,768]{2,1,0:T(8,128)(2,1)S(1)}, bf16[2,96,768]{2,1,0:T(8,128)(2,1)S(1)}, u32[]{:S(2)}, u32[]{:S(2)}) collective-permute-start(bf16[2,96,768]{2,1,0:T(8,128)(2,1)S(1)} %fresh.1.refs_0_), channel_id=1, source_target_pairs={{0,32},{32,0},{1,33},{33,1},{2,34},{34,2},{3,35},{35,3},{4,36},{36... | collective-permute-start | bytes 884744 | tf_op jit(solution)/shard_map/ppermute | solution.py:30
  119.6 12.7 %collective-permute-start.21 = (bf16[2,96,768]{2,1,0:T(8,128)(2,1)S(1)}, bf16[2,96,768]{2,1,0:T(8,128)(2,1)S(1)}, u32[]{:S(2)}, u32[]{:S(2)}) collective-permute-start(bf16[2,96,768]{2,1,0:T(8,128)(2,1)S(1)} %fresh.1.refs_0_), channel_id=1, source_target_pairs={{0,192},{64,0},{128,64},{192,128},{1,193},{65,1},{129,65},{193,129... | collective-permute-start | bytes 884744 | tf_op jit(solution)/shard_map/ppermute | solution.py:30
  121.4 12.9 %collective-permute-start.20 = (bf16[2,96,768]{2,1,0:T(8,128)(2,1)S(1)}, bf16[2,96,768]{2,1,0:T(8,128)(2,1)S(1)}, u32[]{:S(2)}, u32[]{:S(2)}) collective-permute-start(bf16[2,96,768]{2,1,0:T(8,128)(2,1)S(1)} %fresh.1.refs_0_), channel_id=1, source_target_pairs={{0,64},{64,128},{128,192},{192,0},{1,65},{65,129},{129,193},{193,1... | collective-permute-start | bytes 884744 | tf_op jit(solution)/shard_map/ppermute | solution.py:30
  126.6 10.1 %collective-permute-start.26 = (bf16[2,96,768]{2,1,0:T(8,128)(2,1)S(1)}, bf16[2,96,768]{2,1,0:T(8,128)(2,1)S(1)}, u32[]{:S(2)}, u32[]{:S(2)}) collective-permute-start(bf16[2,96,768]{2,1,0:T(8,128)(2,1)S(1)} %collective-permute-done.23.refs_4_), channel_id=1, source_target_pairs={{0,32},{32,0},{1,33},{33,1},{2,34},{34,2},{3,35},{35,3},{4,36},{36... | collective-permute-start | bytes 884744 | tf_op jit(solution)/shard_map/ppermute | solution.py:30
  126.9 12.7 %collective-permute-start.25 = (bf16[2,96,768]{2,1,0:T(8,128)(2,1)S(1)}, bf16[2,96,768]{2,1,0:T(8,128)(2,1)S(1)}, u32[]{:S(2)}, u32[]{:S(2)}) collective-permute-start(bf16[2,96,768]{2,1,0:T(8,128)(2,1)S(1)} %collective-permute-done.22.refs_3_), channel_id=1, source_target_pairs={{0,192},{64,0},{128,64},{192,128},{1,193},{65,1},{129,65},{193,129... | collective-permute-start | bytes 884744 | tf_op jit(solution)/shard_map/ppermute | solution.py:30
  127.8 12.8 %collective-permute-start.24 = (bf16[2,96,768]{2,1,0:T(8,128)(2,1)S(1)}, bf16[2,96,768]{2,1,0:T(8,128)(2,1)S(1)}, u32[]{:S(2)}, u32[]{:S(2)}) collective-permute-start(bf16[2,96,768]{2,1,0:T(8,128)(2,1)S(1)} %collective-permute-done.22.refs_3_), channel_id=1, source_target_pairs={{0,64},{64,128},{128,192},{192,0},{1,65},{65,129},{129,193},{193,1... | collective-permute-start | bytes 884744 | tf_op jit(solution)/shard_map/ppermute | solution.py:30
  134.3 7.7 %collective-permute-start.27 = (bf16[2,96,768]{2,1,0:T(8,128)(2,1)S(1)}, bf16[2,96,768]{2,1,0:T(8,128)(2,1)S(1)}, u32[]{:S(2)}, u32[]{:S(2)}) collective-permute-start(bf16[2,96,768]{2,1,0:T(8,128)(2,1)S(1)} %fresh.1.refs_0_), channel_id=1, source_target_pairs={{0,16},{16,0},{1,17},{17,1},{2,18},{18,2},{3,19},{19,3},{4,20},{20... | collective-permute-start | bytes 884744 | tf_op jit(solution)/shard_map/ppermute | solution.py:30
  136.6 5.3 %collective-permute-start.28 = (bf16[2,96,768]{2,1,0:T(8,128)(2,1)S(1)}, bf16[2,96,768]{2,1,0:T(8,128)(2,1)S(1)}, u32[]{:S(2)}, u32[]{:S(2)}) collective-permute-start(bf16[2,96,768]{2,1,0:T(8,128)(2,1)S(1)} %collective-permute-done.20.refs_1_), channel_id=1, source_target_pairs={{0,16},{16,0},{1,17},{17,1},{2,18},{18,2},{3,19},{19,3},{4,20},{20... | collective-permute-start | bytes 884744 | tf_op jit(solution)/shard_map/ppermute | solution.py:30
  136.7 5.8 %collective-permute-start.29 = (bf16[2,96,768]{2,1,0:T(8,128)(2,1)S(1)}, bf16[2,96,768]{2,1,0:T(8,128)(2,1)S(1)}, u32[]{:S(2)}, u32[]{:S(2)}) collective-permute-start(bf16[2,96,768]{2,1,0:T(8,128)(2,1)S(1)} %collective-permute-done.21.refs_2_), channel_id=1, source_target_pairs={{0,16},{16,0},{1,17},{17,1},{2,18},{18,2},{3,19},{19,3},{4,20},{20... | collective-permute-start | bytes 884744 | tf_op jit(solution)/shard_map/ppermute | solution.py:30
  139.6 3.0 %collective-permute-start.30 = (bf16[2,96,768]{2,1,0:T(8,128)(2,1)S(1)}, bf16[2,96,768]{2,1,0:T(8,128)(2,1)S(1)}, u32[]{:S(2)}, u32[]{:S(2)}) collective-permute-start(bf16[2,96,768]{2,1,0:T(8,128)(2,1)S(1)} %collective-permute-done.22.refs_3_), channel_id=1, source_target_pairs={{0,16},{16,0},{1,17},{17,1},{2,18},{18,2},{3,19},{19,3},{4,20},{20... | collective-permute-start | bytes 884744 | tf_op jit(solution)/shard_map/ppermute | solution.py:30
  140.5 2.7 %collective-permute-start.31 = (bf16[2,96,768]{2,1,0:T(8,128)(2,1)S(1)}, bf16[2,96,768]{2,1,0:T(8,128)(2,1)S(1)}, u32[]{:S(2)}, u32[]{:S(2)}) collective-permute-start(bf16[2,96,768]{2,1,0:T(8,128)(2,1)S(1)} %collective-permute-done.23.refs_4_), channel_id=1, source_target_pairs={{0,16},{16,0},{1,17},{17,1},{2,18},{18,2},{3,19},{19,3},{4,20},{20... | collective-permute-start | bytes 884744 | tf_op jit(solution)/shard_map/ppermute | solution.py:30
  142.0 1.6 %collective-permute-start.33 = (bf16[2,96,768]{2,1,0:T(8,128)(2,1)S(1)}, bf16[2,96,768]{2,1,0:T(8,128)(2,1)S(1)}, u32[]{:S(2)}, u32[]{:S(2)}) collective-permute-start(bf16[2,96,768]{2,1,0:T(8,128)(2,1)S(1)} %collective-permute-done.25.refs_6_), channel_id=1, source_target_pairs={{0,16},{16,0},{1,17},{17,1},{2,18},{18,2},{3,19},{19,3},{4,20},{20... | collective-permute-start | bytes 884744 | tf_op jit(solution)/shard_map/ppermute | solution.py:30
  142.0 2.0 %collective-permute-start.32 = (bf16[2,96,768]{2,1,0:T(8,128)(2,1)S(1)}, bf16[2,96,768]{2,1,0:T(8,128)(2,1)S(1)}, u32[]{:S(2)}, u32[]{:S(2)}) collective-permute-start(bf16[2,96,768]{2,1,0:T(8,128)(2,1)S(1)} %collective-permute-done.24.refs_5_), channel_id=1, source_target_pairs={{0,16},{16,0},{1,17},{17,1},{2,18},{18,2},{3,19},{19,3},{4,20},{20... | collective-permute-start | bytes 884744 | tf_op jit(solution)/shard_map/ppermute | solution.py:30
  142.5 2.0 %collective-permute-start.34 = (bf16[2,96,768]{2,1,0:T(8,128)(2,1)S(1)}, bf16[2,96,768]{2,1,0:T(8,128)(2,1)S(1)}, u32[]{:S(2)}, u32[]{:S(2)}) collective-permute-start(bf16[2,96,768]{2,1,0:T(8,128)(2,1)S(1)} %collective-permute-done.26.refs_7_), channel_id=1, source_target_pairs={{0,16},{16,0},{1,17},{17,1},{2,18},{18,2},{3,19},{19,3},{4,20},{20... | collective-permute-start | bytes 884744 | tf_op jit(solution)/shard_map/ppermute | solution.py:30
